TPU v7x, 32 devices: a whole 2x2x4 slice. The times are simulated.
32 devices in a mesh: shard: 4 (over z), ctx: 2 (over y), tp: 4 (over x, core).
Axes of the slice: x: 2, y: 2, z: 4, core: 2. Of those that a mesh axis runs over, the one named last changes fastest.
Arguments:
- video_in: bfloat16 [16, 8, 196, 768], P('shard', 'tp', 'ctx'), may hold values from -6 to 6
- cotangent: bfloat16 [16, 8, 196, 768], P('shard', 'tp', 'ctx'), may hold values from -6 to 6
- qkv_time: bfloat16 [768, 3, 768], P(('shard', 'ctx'), None, 'tp'), may hold values from -0.21875 to 0.21875
- proj_time: bfloat16 [768, 768], P('tp', ('shard', 'ctx')), may hold values from -0.4375 to 0.4375
- qkv_space: bfloat16 [768, 3, 768], P(('shard', 'ctx'), None, 'tp'), may hold values from -0.21875 to 0.21875
- proj_space: bfloat16 [768, 768], P('tp', ('shard', 'ctx')), may hold values from -1.5 to 1.5
- fc_in: bfloat16 [768, 3072], P(('shard', 'ctx'), 'tp'), may hold values from -0.21875 to 0.21875
- fc_out: bfloat16 [3072, 768], P('tp', ('shard', 'ctx')), may hold values from -0.15625 to 0.15625
- gain_time: float32 [768], P(('shard', 'ctx', 'tp')), may hold values from 0.25 to 1.75
- shift_time: float32 [768], P(('shard', 'ctx', 'tp')), may hold values from -3 to 3
- bias_time: float32 [768], P(('shard', 'ctx', 'tp')), may hold values from -3 to 3
- gain_space: float32 [768], P(('shard', 'ctx', 'tp')), may hold values from 0.25 to 1.75
- shift_space: float32 [768], P(('shard', 'ctx', 'tp')), may hold values from -3 to 3
- bias_space: float32 [768], P(('shard', 'ctx', 'tp')), may hold values from -3 to 3
- gain_mlp: float32 [768], P(('shard', 'ctx', 'tp')), may hold values from 0.25 to 1.75
- shift_mlp: float32 [768], P(('shard', 'ctx', 'tp')), may hold values from -3 to 3
- bias_in: float32 [3072], P(('shard', 'ctx', 'tp')), may hold values from -3 to 3
- bias_out: float32 [768], P(('shard', 'ctx', 'tp')), may hold values from -3 to 3
Outputs:
- result: bfloat16 [16, 8, 196, 768], P('shard', 'tp', 'ctx')
- grad_video: float32 [16, 8, 196, 768], P('shard', 'tp', 'ctx')
- grad_qkv_time: float32 [768, 3, 768], P(('shard', 'ctx'), None, 'tp')
- grad_proj_time: float32 [768, 768], P('tp', ('shard', 'ctx'))
- grad_qkv_space: float32 [768, 3, 768], P(('shard', 'ctx'), None, 'tp')
- grad_proj_space: float32 [768, 768], P('tp', ('shard', 'ctx'))
- grad_fc_in: float32 [768, 3072], P(('shard', 'ctx'), 'tp')
- grad_fc_out: float32 [3072, 768], P('tp', ('shard', 'ctx'))
- grad_gain_time: float32 [768], P(('shard', 'ctx', 'tp'))
- grad_shift_time: float32 [768], P(('shard', 'ctx', 'tp'))
- grad_bias_time: float32 [768], P(('shard', 'ctx', 'tp'))
- grad_gain_space: float32 [768], P(('shard', 'ctx', 'tp'))
- grad_shift_space: float32 [768], P(('shard', 'ctx', 'tp'))
- grad_bias_space: float32 [768], P(('shard', 'ctx', 'tp'))
- grad_gain_mlp: float32 [768], P(('shard', 'ctx', 'tp'))
- grad_shift_mlp: float32 [768], P(('shard', 'ctx', 'tp'))
- grad_bias_in: float32 [3072], P(('shard', 'ctx', 'tp'))
- grad_bias_out: float32 [768], P(('shard', 'ctx', 'tp'))
All inputs are finite; a program needn't handle non-finite values.
Results may differ from a plain program's by a relative error of at most 0.03.
Values may be sent and summed in bfloat16 or wider, within the bound.
No kernel may reach another device: no remote copies, remote signals or barrier semaphores. Data moves between devices by JAX's collectives and lax.ppermute only.
A program may use at most 256 MiB of HBM per device.

v0:
```python
import functools

import jax
import jax.numpy as jnp
from jax import lax
from jax.experimental import pallas as pl
from jax.experimental.pallas import tpu as pltpu
from jax.sharding import Mesh
from jax.sharding import PartitionSpec as P

F32 = jnp.float32
B16 = jnp.bfloat16
HEAD_DIM = 64
SCALING = HEAD_DIM ** (-0.5)
EPSILON = 1e-06
NEGATIVE = -1e30
PAD = 104
NT_DIMS = (((1,), (1,)), ((), ()))
TN_DIMS = (((0,), (0,)), ((), ()))
FLIP = [(0, 1), (1, 0)]
VMEM_LIMIT = 64 * 1024 * 1024 - 65536


def over_x(v):
    return lax.ppermute(v, "x", FLIP)


def over_y(v):
    return lax.ppermute(v, "ctx", FLIP)


def over_xy(v):
    return lax.ppermute(v, ("ctx", "x"), [(i, 3 - i) for i in range(4)])


def over_core(v):
    return lax.ppermute(v, "core", FLIP)


def over_z(v):
    return lax.all_to_all(v, "shard", split_axis=0, concat_axis=0, tiled=True)


def after(values, *results):
    return lax.optimization_barrier((values, results))[0]


def layout(chunks, n):
    full = [(z, k) for z in range(n) for k in range(chunks)]
    h = len(full) // 2
    return [(0, 0, full), (1, 0, full), (0, 1, full), (1, 1, full[:h]), (1, 1, full[h:])]


class Gather:
    def __init__(self, owns, n, shifts=False):
        self.own, self.n, self.shifts = jnp.stack(owns), n, shifts

    def stage_z(self, *deps):
        own, n = self.own, self.n
        if self.shifts:
            own = after(own, *deps)
            self.z = [own] + [
                lax.ppermute(own, "shard", [((i + d) % n, i) for i in range(n)])
                for d in range(1, n)
            ]
            return self.z[1:]
        spread = lax.optimization_barrier(jnp.broadcast_to(own[None], (n,) + own.shape))
        self.z = [over_z(after(spread, *deps))]
        return self.z

    def stage_xy(self, *deps):
        z = after(tuple(self.z), *deps)
        self.blk = jnp.concatenate([v.reshape((-1,) + v.shape[-2:]) for v in z], axis=0)
        self.x, self.y = over_x(self.blk), over_y(self.blk)
        self.sent = [self.blk]
        return [self.x, self.y]

    def stage_rest(self, *deps):
        h = self.blk.shape[0] // 2
        x, y = after((self.x, self.y), *deps)
        self.sent = [x[:h], y[h:]]
        self.rest = [over_y(self.sent[0]), over_x(self.sent[1])]
        self.far = [over_core(v) for v in (self.blk, x, y)]
        return self.rest

    def stage_core(self, *deps):
        rest = after(tuple(self.rest), *deps)
        return [self.blk, self.x, self.y] + self.rest + self.far + [over_core(v) for v in rest]


def block_sums(name, outs):
    terms = [t for ts, _, _ in outs for t in ts]
    tail = terms[0][0].shape[1:]

    def kernel(*refs):
        ins, res = refs[: len(terms)], refs[len(terms) :]
        k = 0
        for (ts, count, dtype), out in zip(outs, res):
            for i in range(count):
                acc = None
                for j, (_, blocks, _, first) in enumerate(ts):
                    if first <= i < first + blocks:
                        v = ins[k + j][i - first].astype(F32)
                        acc = v if acc is None else acc + v
                out[i] = acc.astype(dtype)
            k += len(ts)

    def spec(blocks, index):
        return pl.BlockSpec((blocks,) + tail, lambda i: (index, 0, 0))

    return pl.pallas_call(
        kernel,
        name=name,
        grid=(1,),
        in_specs=[spec(blocks, index) for _, blocks, index, _ in terms],
        out_specs=[pl.BlockSpec((count,) + tail, lambda i: (0, 0, 0)) for _, count, _ in outs],
        out_shape=[jax.ShapeDtypeStruct((count,) + tail, dt) for _, count, dt in outs],
        compiler_params=pltpu.CompilerParams(vmem_limit_bytes=24 * 2**20),
        cost_estimate=pl.CostEstimate(flops=10**8, bytes_accessed=10**5, transcendentals=0),
    )(*[t[0] for t in terms])


class Reduce:
    def __init__(self, parts, n, name, shifts=False):
        self.near, self.far = parts
        self.shifts = shifts
        self.n, self.name = n, name
        self.size = self.near.shape[0] // 4

    def stage_core(self, *deps):
        self.got = over_core(after(self.far, *deps))
        return [self.got]

    def stage_rest(self, *deps):
        h = self.size // 2
        self.got = after(self.got, *deps)
        lo, hi = block_sums(
            self.name + "_rest",
            [([(v, h, k, 0) for v in (self.near, self.got)], h, B16) for k in (6, 7)],
        )
        self.sent = [lo, hi]
        self.rest = [over_y(lo), over_x(hi)]
        return self.rest

    def stage_xy(self, *deps):
        size, h = self.size, self.size // 2
        lo, hi = after(tuple(self.rest), *deps)
        both = (self.near, self.got)
        sx, sy = block_sums(
            self.name + "_xy",
            [
                ([(v, size, 1, 0) for v in both] + [(lo, h, 0, 0)], size, B16),
                ([(v, size, 2, 0) for v in both] + [(hi, h, 0, h)], size, B16),
            ],
        )
        self.sent = [sx, sy]
        self.xy = [over_x(sx), over_y(sy)]
        return self.xy

    def stage_z(self, *deps):
        rx, ry = after(tuple(self.xy), *deps)
        all_four = (self.near, self.got, rx, ry)
        if self.shifts:
            own, *self.sent = block_sums(
                self.name + "_z",
                [
                    ([(v, 1, d, 0) for v in all_four], 1, B16 if d else F32)
                    for d in range(self.n)
                ],
            )
            self.z = [own] + [
                lax.ppermute(v, "shard", [(i, (i + d) % self.n) for i in range(self.n)])
                for d, v in enumerate(self.sent, 1)
            ]
            return self.z[1:]
        self.sent = block_sums(
            self.name + "_z", [([(v, self.size, 0, 0) for v in all_four], self.size, B16)]
        )
        v = self.sent[0]
        self.z = over_z(v.reshape((self.n, self.size // self.n) + v.shape[1:]))
        return [self.z]

    def results(self, *deps):
        if self.shifts:
            z = after(tuple(self.z), *deps)
            return [functools.reduce(lambda a, b: a + b, [v[0].astype(F32) for v in z])]
        z = jnp.sum(after(self.z, *deps).astype(F32), axis=0)
        return [z[k] for k in range(z.shape[0])]


EVERY = ("x", "core", "shard", "ctx")


def gather_whole(own):
    return lax.all_gather(own, EVERY, axis=0, tiled=False)


def reduce_whole(parts):
    return lax.psum_scatter(parts, EVERY, scatter_dimension=0, tiled=False).astype(F32)


class GatherWhole:
    sent = ()

    def __init__(self, owns, n, shifts=False):
        d = owns[0].shape[1]
        self.out = [gather_whole(v).reshape(4, d, d) for v in owns]

    def stage_z(self, *deps):
        return []

    stage_xy = stage_rest = stage_z

    def stage_core(self, *deps):
        return self.out


class ReduceWhole:
    sent = ()

    def __init__(self, parts, n, name, shifts=False):
        self.parts = parts

    def stage_z(self, *deps):
        return []

    stage_core = stage_rest = stage_xy = stage_z

    def results(self, *deps):
        rows = self.parts[0].shape[1] // (2 * lax.axis_size("shard"))
        return [reduce_whole(p.reshape(-1, rows, p.shape[2]).astype(F32)) for p in self.parts]


def dot(a, b):
    return jnp.dot(a, b, preferred_element_type=F32)


def dot_nt(a, b):
    return lax.dot_general(a, b, NT_DIMS, preferred_element_type=F32)


def dot_tn(a, b):
    return lax.dot_general(a, b, TN_DIMS, preferred_element_type=F32)


def low_lanes(shape):
    return lax.broadcasted_iota(jnp.int32, shape, 1) % 128 < 64


def keep_low(v):
    return jnp.where(low_lanes(v.shape), v, jnp.zeros_like(v))


def keep_high(v):
    return jnp.where(low_lanes(v.shape), jnp.zeros_like(v), v)


def swap_halves(v):
    return jnp.concatenate([v[:, 64:], v[:, :64]], axis=1)


def norm_parts(x):
    centred = x - jnp.mean(x, axis=-1, keepdims=True)
    rstd = lax.rsqrt(jnp.mean(centred * centred, axis=-1, keepdims=True) + EPSILON)
    return centred * rstd, rstd


def norm_back(x, gain, up):
    unit, rstd = norm_parts(x)
    w = up * gain
    inner = jnp.mean(w * unit, axis=-1, keepdims=True)
    down = rstd * (w - jnp.mean(w, axis=-1, keepdims=True) - unit * inner)
    return down, jnp.sum(up * unit, axis=0, keepdims=True), jnp.sum(up, axis=0, keepdims=True)


def weight_copies(meta, bufs, w_refs, sems, n, back=False, shifts=False):
    moves = []
    if bufs[0].shape == w_refs[0].shape:
        moves = list(zip(bufs, w_refs))
    else:
        x, y, c = meta[0], meta[1], meta[2]
        rows = bufs[0].shape[1]
        for dc in range(2):
            first = 0
            for k, (dx, dy, blocks) in enumerate(layout(len(w_refs), n)):
                tp = 2 * (x ^ dx) + (c ^ dc)
                for i, (z, chunk) in enumerate(blocks):
                    if shifts:
                        z = lax.rem(meta[3] + z, n)
                    row = pl.multiple_of((z * 2 + (y ^ dy)) * rows, rows)
                    piece = bufs[dc].at[first + i] if back else bufs[dc * 5 + k].at[i]
                    moves.append((piece, w_refs[chunk].at[tp, pl.ds(row, rows), :]))
                first += len(blocks)
    if back:
        moves = [(whole, piece) for piece, whole in moves]
    return [pltpu.make_async_copy(*m, sems.at[i]) for i, m in enumerate(moves)]


def copy_sems(sz, chunks):
    return pltpu.SemaphoreType.DMA((8 * chunks * sz["n"],))


def start_all(copies):
    for c in copies:
        c.start()


def wait_all(copies):
    for c in copies:
        c.wait()


def take_blocks(blocks, dst, places):
    for k, blk in enumerate(blocks):
        dx, dy = k % 2, k // 2
        for f in range(2):
            row = (2 * dx + f) * 2 * PAD + dy * PAD
            dst[row + PAD - 8 : row + PAD, :] = jnp.zeros((8, dst.shape[1]), dst.dtype)
            dst[row : row + places, :] = blk[f].astype(dst.dtype)


def give_blocks(src, blocks, places):
    for k, blk in enumerate(blocks):
        dx, dy = k % 2, k // 2
        for f in range(2):
            row = (2 * dx + f) * 2 * PAD + dy * PAD
            blk[f] = src[row : row + places, :].astype(blk.dtype)


def project_heads(normed, w_ref, q_out, kv_out, rows, step):
    @pl.loop(0, 2)
    def _(u):
        @pl.loop(0, rows // step)
        def _(r):
            at = pl.ds(pl.multiple_of(r * step, step), step)
            xn = normed[at, :]
            thirds = []
            for t in (2 * u, 2 * u + 1):
                y = dot(xn, w_ref[t, :, 0:512]).astype(B16)
                q_out[t, at, :] = y[:, 0:128]
                kv_out[t, at, :] = y[:, 128:256]
                kv_out[6 + t, at, :] = y[:, 256:384]
                thirds.append((y[:, 384:512], dot(xn, w_ref[t, :, 640:768]).astype(B16)))
            (a3, a5), (b3, b5) = thirds
            low = low_lanes(a3.shape)
            q_out[4 + u, at, :] = jnp.where(low, a3, b3)
            kv_out[4 + u, at, :] = swap_halves(jnp.where(low, b3, a3))
            kv_out[10 + u, at, :] = swap_halves(jnp.where(low, b5, a5))


def third_head(v, t):
    return keep_low(v) if t % 2 == 0 else keep_high(v)


def project_out(mixed, w_ref, stream, bias, out, rows, step):
    @pl.loop(0, rows // step)
    def _(r):
        at = pl.ds(pl.multiple_of(r * step, step), step)
        acc = stream[at, :] + bias
        for t in range(4):
            m = jnp.concatenate([mixed[t, at, :], third_head(mixed[4 + t // 2, at, :], t)], axis=1)
            acc = acc + dot_nt(m, w_ref[t, :, 512:768])
        out[at, :] = acc


def run(kernel, name, ins, outs, scratch, micros):
    space = {
        "v": pl.BlockSpec(memory_space=pltpu.VMEM),
        "s": pl.BlockSpec(memory_space=pltpu.SMEM),
        "a": pl.BlockSpec(memory_space=pl.ANY),
    }
    return pl.pallas_call(
        kernel,
        name=name,
        in_specs=[space[s] for _, s in ins],
        out_specs=[space[s] for _, _, s in outs],
        out_shape=[jax.ShapeDtypeStruct(s, d) for s, d, _ in outs],
        scratch_shapes=scratch,
        compiler_params=pltpu.CompilerParams(vmem_limit_bytes=VMEM_LIMIT),
        cost_estimate=pl.CostEstimate(
            flops=micros * 10**9, bytes_accessed=micros * 3 * 10**6, transcendentals=0
        ),
    )(*[a for a, _ in ins])


def row_slices(r, step=208):
    return pl.ds(pl.multiple_of(r * step, step), step)


def time_qkv(sz, meta, vec, blocks, weights):
    rows, d = sz["rows"], sz["d"]
    nb, nw = len(blocks), len(weights)

    def kernel(*refs):
        meta, vec = refs[0], refs[1]
        blks, bufs = refs[2 : 2 + nb], refs[2 + nb : 2 + nb + nw]
        x, normed, q, kv, w, sems = refs[2 + nb + nw :]
        copies = weight_copies(meta, bufs, [w], sems, sz["n"], shifts=True)
        start_all(copies)
        take_blocks(blks, x, sz["places"])

        @pl.loop(0, 4)
        def _(r):
            at = row_slices(r)
            unit, _ = norm_parts(x[at, :])
            normed[at, :] = (unit * vec[0:1, :] + vec[1:2, :]).astype(B16)

        wait_all(copies)
        project_heads(normed, w, q, kv, rows, 416)

    ins = [(meta, "s"), (vec, "v")] + [(b, "v") for b in blocks] + [(w, "a") for w in weights]
    outs = [
        ((rows, d), F32, "v"),
        ((rows, d), B16, "v"),
        ((6, rows, 128), B16, "v"),
        ((12, rows, 128), B16, "v"),
    ]
    scratch = [pltpu.VMEM((4, d, d), B16), copy_sems(sz, 1)]
    return run(kernel, "time_qkv", ins, outs, scratch, 12)


def head_sums(ref):
    for f in range(4):
        for j in range(6):
            col = lax.broadcasted_iota(jnp.int32, (128, 128), 1)
            lane = lax.broadcasted_iota(jnp.int32, (128, 128), 0)
            hit = col == 16 * f + 2 * j + lane // 64
            ref[(f * 6 + j) * 128 : (f * 6 + j) * 128 + 128, :] = hit.astype(F32).astype(B16)


def head_spreads(ref):
    for f in range(4):
        for j in range(6):
            row = lax.broadcasted_iota(jnp.int32, (128, 128), 0)
            lane = lax.broadcasted_iota(jnp.int32, (128, 128), 1)
            hit = row == 16 * f + 2 * j + lane // 64
            ref[:, (f * 6 + j) * 128 : (f * 6 + j) * 128 + 128] = hit.astype(F32).astype(B16)


def pair_sums(a_ref, b_ref, b_tile, g, sums):
    at = row_slices(g)
    products = [
        a_ref[j, f * 208 : f * 208 + 208, :] * b_ref[b_tile + j, at, :]
        for f in range(4)
        for j in range(6)
    ]
    return dot(jnp.concatenate(products, axis=1), sums[...])


def two_tiles(ref, tile, at):
    return jnp.concatenate([ref[tile, at, :], ref[tile + 1, at, :]], axis=1).astype(F32)


def time_mix(sz, meta, vec, stream, q, kv, kvo, weights):
    rows, d = sz["rows"], sz["d"]
    nw = len(weights)

    def kernel(*refs):
        meta, vec, stream, q, kv, kvo = refs[:6]
        bufs = refs[6 : 6 + nw]
        mixed, out, prob, w, sums, spreads, acc, sems = refs[6 + nw :]
        copies = weight_copies(meta, bufs, [w], sems, sz["n"], shifts=True)
        start_all(copies)
        head_sums(sums)
        head_spreads(spreads)
        for h, ref in enumerate((kv, kvo)):

            @pl.loop(0, 4)
            def _(g):
                prob[4 * h + g] = pair_sums(q, ref, 0, g, sums) * SCALING

        @pl.loop(0, 13)
        def _(r):
            at = row_slices(r, 16)
            s = [prob[g, at, :] for g in range(8)]
            top = functools.reduce(jnp.maximum, s)
            e = [jnp.exp(v - top) for v in s]
            inv = 1.0 / functools.reduce(lambda a, b: a + b, e)
            for g in range(8):
                prob[g, at, :] = e[g] * inv

        acc[...] = jnp.zeros_like(acc)
        for h, ref in enumerate((kv, kvo)):

            @pl.loop(0, 4)
            def _(g):
                at = row_slices(g)
                p = prob[4 * h + g].astype(B16)
                for jj in range(3):
                    v = two_tiles(ref, 6 + 2 * jj, at)
                    for f in range(4):
                        lanes = slice(f * d + 256 * jj, f * d + 256 * jj + 256)
                        acc[f * 208 : f * 208 + 208, 256 * jj : 256 * jj + 256] += (
                            dot(p, spreads[:, lanes]) * v
                        )

        for j in range(6):
            mixed[j] = acc[:, 128 * j : 128 * j + 128].astype(B16)
        wait_all(copies)
        project_out(mixed, w, stream, vec[2:3, :], out, rows, 416)

    ins = [(meta, "s"), (vec, "v"), (stream, "v"), (q, "v"), (kv, "v"), (kvo, "v")]
    ins += [(w, "a") for w in weights]
    outs = [((6, rows, 128), B16, "v"), ((rows, d), F32, "v"), ((8, 208, 128), F32, "v")]
    scratch = [
        pltpu.VMEM((4, d, d), B16),
        pltpu.VMEM((4 * d, 128), B16),
        pltpu.VMEM((128, 4 * d), B16),
        pltpu.VMEM((rows, d), F32),
        copy_sems(sz, 1),
    ]
    return run(kernel, "time_mix", ins, outs, scratch, 17)


def space_mask(places):
    return lax.broadcasted_iota(jnp.int32, (208, 208), 0) % PAD < places


def space_forward(sz, meta, vec, stream, weights):
    rows, d, places = sz["rows"], sz["d"], sz["places"]
    nw = len(weights)

    def kernel(*refs):
        meta, vec, stream = refs[:3]
        bufs = refs[3 : 3 + nw]
        normed, q, kv, mixed, logs, out, w, sems = refs[3 + nw :]
        copies = weight_copies(meta, bufs, [w], sems, sz["n"])
        start_all(copies)

        @pl.loop(0, 4)
        def _(r):
            at = row_slices(r)
            unit, _ = norm_parts(stream[at, :])
            normed[at, :] = (unit * vec[3:4, :] + vec[4:5, :]).astype(B16)

        wait_all(copies)
        project_heads(normed, w, q, kv, rows, 416)

        @pl.loop(0, 6)
        def _(j):
            @pl.loop(0, 4)
            def _(f):
                at = row_slices(f)
                qj, kj, vj = q[j, at, :], kv[j, at, :], kv[6 + j, at, :]
                mask = space_mask(places)
                o = None
                for h, keep in enumerate((keep_low, keep_high)):
                    s = jnp.where(mask, dot_nt(kj, keep(qj)) * SCALING, NEGATIVE)
                    top = jnp.max(s, axis=0, keepdims=True)
                    e = jnp.exp(s - top)
                    size = jnp.sum(e, axis=0, keepdims=True)
                    logs[j * 4 + f, h : h + 1, :] = top + jnp.log(size)
                    part = dot_tn((e * (1.0 / size)).astype(B16), keep(vj))
                    o = part if o is None else o + part
                mixed[j, at, :] = o.astype(B16)

        project_out(mixed, w, stream, vec[5:6, :], out, rows, 416)

    ins = [(meta, "s"), (vec, "v"), (stream, "v")] + [(w, "a") for w in weights]
    outs = [
        ((rows, d), B16, "v"),
        ((6, rows, 128), B16, "v"),
        ((12, rows, 128), B16, "v"),
        ((6, rows, 128), B16, "v"),
        ((24, 8, 208), F32, "v"),
        ((rows, d), F32, "v"),
    ]
    scratch = [pltpu.VMEM((4, d, d), B16), copy_sems(sz, 1)]
    return run(kernel, "space_forward", ins, outs, scratch, 29)


def gradient_outs(sz, chunks, fast):
    d, n = sz["d"], sz["n"]
    if not fast:
        return [((4, d, d), B16, "a")] * chunks
    return [((4 * chunks * n, d // (2 * n), d), B16, "a")] * 2


def transpose_into(src, dst):
    for j in range(src.shape[1] // 128):
        dst[128 * j : 128 * j + 128, :] = src[:, 128 * j : 128 * j + 128].T


def gelu_pair(x):
    half = 0.5 * (1.0 + lax.erf(x * 0.7071067811865476))
    slope = half + x * (0.3989422804014327 * jnp.exp(-0.5 * x * x))
    return x * half, slope


def feed_forward(sz, meta, vec, stream, blocks, weights, fast):
    rows, d, places = sz["rows"], sz["d"], sz["places"]
    nb, nw = len(blocks), len(weights)
    g_outs = gradient_outs(sz, 2, fast)
    ng = len(g_outs)

    def kernel(*refs):
        meta, vec, stream = refs[:3]
        blks = refs[3 : 3 + nb]
        refs = refs[3 + nb :]
        bufs, refs = refs[:nw], refs[nw:]
        res, refs = refs[:nb], refs[nb:]
        d2, vgrad = refs[0], refs[1]
        g_bufs, refs = refs[2 : 2 + ng], refs[2 + ng :]
        w1, w2, dw1, dw2, dz, dzr, normed, normed_t, dzr_t, act, dpre, y, dn, sems = refs
        copies = weight_copies(meta, bufs, [w1, w2], sems, sz["n"])
        start_all(copies)
        take_blocks(blks, dz, places)
        vgrad[...] = jnp.zeros_like(vgrad)

        @pl.loop(0, 4)
        def _(r):
            at = pl.ds(pl.multiple_of(r * 208, 208), 208)
            unit, _ = norm_parts(stream[at, :])
            normed[at, :] = (unit * vec[6:7, :] + vec[7:8, :]).astype(B16)
            up = dz[at, :]
            dzr[at, :] = up.astype(B16)
            vgrad[2:3, :] += jnp.sum(up, axis=0, keepdims=True)
            y[at, :] = stream[at, :] + vec[8:9, :]
            dn[at, :] = jnp.zeros_like(up)

        transpose_into(normed, normed_t)
        transpose_into(dzr, dzr_t)
        wait_all(copies)

        @pl.loop(0, 4)
        def _(t):
            @pl.loop(0, rows // 208)
            def _(r):
                at = pl.ds(pl.multiple_of(r * 208, 208), 208)
                pre = dot(normed[at, :], w1[t]) + vec[pl.ds(9 + t, 1), :]
                a, slope = gelu_pair(pre)
                a = a.astype(B16)
                act[at, :] = a
                y[at, :] += dot_nt(a, w2[t])
                g = (dot(dzr[at, :], w2[t]) * slope).astype(B16)
                dpre[at, :] = g
                vgrad[pl.ds(4 + t, 1), :] += jnp.sum(g.astype(F32), axis=0, keepdims=True)
                dn[at, :] += dot_nt(g, w1[t])

            @pl.loop(0, d // 256)
            def _(m):
                at = pl.ds(pl.multiple_of(m * 256, 256), 256)
                dw1[t, at, :] = dot(normed_t[at, :], dpre[...]).astype(B16)
                dw2[t, at, :] = dot(dzr_t[at, :], act[...]).astype(B16)

        back = weight_copies(meta, g_bufs, [dw1, dw2], sems, sz["n"], back=True)
        start_all(back)
        give_blocks(y, res, places)

        @pl.loop(0, 4)
        def _(r):
            at = pl.ds(pl.multiple_of(r * 208, 208), 208)
            down, gg, gs = norm_back(stream[at, :], vec[6:7, :], dn[at, :])
            d2[at, :] = dz[at, :] + down
            vgrad[0:1, :] += gg
            vgrad[1:2, :] += gs

        wait_all(back)

    ins = [(meta, "s"), (vec, "v"), (stream, "v")] + [(b, "v") for b in blocks]
    ins += [(w, "a") for w in weights]
    outs = [((2, places, d), B16, "v")] * nb + [((rows, d), F32, "v"), ((8, d), F32, "v")]
    outs += g_outs
    scratch = [pltpu.VMEM((4, d, d), B16)] * 4
    scratch += [pltpu.VMEM((rows, d), F32), pltpu.VMEM((rows, d), B16), pltpu.VMEM((rows, d), B16)]
    scratch += [pltpu.VMEM((d, rows), B16)] * 2 + [pltpu.VMEM((rows, d), B16)] * 2
    scratch += [pltpu.VMEM((rows, d), F32)] * 2
    scratch += [copy_sems(sz, 2)]
    r = run(kernel, "feed_forward", ins, outs, scratch, 47)
    return r[:nb], r[nb], r[nb + 1], r[nb + 2 :]


def mixed_slopes(up, w_ref, dm, rows, step):
    @pl.loop(0, 2)
    def _(u):
        @pl.loop(0, rows // step)
        def _(r):
            at = pl.ds(pl.multiple_of(r * step, step), step)
            thirds = []
            for t in (2 * u, 2 * u + 1):
                v = dot(up[at, :], w_ref[t, :, 512:768]).astype(B16)
                dm[t, at, :] = v[:, 0:128]
                thirds.append(v[:, 128:256])
            dm[4 + u, at, :] = jnp.where(low_lanes(thirds[0].shape), *thirds)


def place_third(dq, dk, dv, dy, u, at):
    k, v = swap_halves(dk), swap_halves(dv)
    low = low_lanes(dq.shape)
    dy[2 * u, at, 384:512] = jnp.where(low, dq, k)
    dy[2 * u + 1, at, 384:512] = jnp.where(low, k, dq)
    dy[2 * u, at, 512:640] = keep_high(v)
    dy[2 * u + 1, at, 512:640] = keep_low(v)


def head_gradients(dw, normed_t, up_t, dy, mixed, d):
    @pl.loop(0, 2)
    def _(u):
        @pl.loop(0, d // 256)
        def _(m):
            at = pl.ds(pl.multiple_of(m * 256, 256), 256)
            nt, ut = normed_t[at, :], up_t[at, :]
            for odd in range(2):
                t = 2 * u + odd
                g = dot(nt, dy[t])
                dw[t, at, 0:512] = g[:, 0:512].astype(B16)
                m2 = jnp.concatenate([mixed[t], third_head(mixed[4 + u], odd)], axis=1)
                out = dot(ut, m2)
                dw[t, at, 512:640] = out[:, 0:128].astype(B16)
                dw[t, at, 640:768] = (out[:, 128:256] + g[:, 512:640]).astype(B16)


def norm_slopes(at, dy, w_ref):
    up = None
    for t in range(4):
        part = dot_nt(dy[t, at, 0:512], w_ref[t, :, 0:512]) + dot_nt(
            dy[t, at, 512:640], w_ref[t, :, 640:768]
        )
        up = part if up is None else up + part
    return up


def space_backward_scores(sz, meta, d2, q, kv, logs, weights):
    rows, d, places = sz["rows"], sz["d"], sz["places"]
    nw = len(weights)

    def kernel(*refs):
        meta, d2, q, kv, logs = refs[:5]
        bufs, refs = refs[5 : 5 + nw], refs[5 + nw :]
        up, dy, w, dm, third, sems = refs
        copies = weight_copies(meta, bufs, [w], sems, sz["n"])
        start_all(copies)

        @pl.loop(0, 4)
        def _(r):
            up[row_slices(r), :] = d2[row_slices(r), :].astype(B16)

        wait_all(copies)
        mixed_slopes(up, w, dm, rows, 416)

        def slopes(j, at, f):
            qj, kj, vj, mj = q[j, at, :], kv[j, at, :], kv[6 + j, at, :], dm[j, at, :]
            mask = space_mask(places)
            dq = dk = dv = None
            for h, keep in enumerate((keep_low, keep_high)):
                qh, mh = keep(qj), keep(mj)
                s = dot_nt(kj, qh) * SCALING - logs[j * 4 + f, h : h + 1, :]
                p = jnp.exp(jnp.where(mask, s, NEGATIVE))
                dp = dot_nt(vj, mh)
                inner = jnp.sum(p * dp, axis=0, keepdims=True)
                ds = (p * (dp - inner) * SCALING).astype(B16)
                a, b, c = dot_tn(ds, keep(kj)), dot(ds, qh), dot(p.astype(B16), mh)
                dq, dk, dv = (a, b, c) if dq is None else (dq + a, dk + b, dv + c)
            return dq.astype(B16), dk.astype(B16), dv.astype(B16)

        @pl.loop(0, 4)
        def _(j):
            @pl.loop(0, 4)
            def _(f):
                at = row_slices(f)
                dq, dk, dv = slopes(j, at, f)
                dy[j, at, 0:128] = dq
                dy[j, at, 128:256] = dk
                dy[j, at, 256:384] = dv

        @pl.loop(0, 2)
        def _(u):
            @pl.loop(0, 4)
            def _(f):
                at = row_slices(f)
                place_third(*slopes(4 + u, at, f), dy, u, at)

    ins = [(meta, "s")] + [(v, "v") for v in (d2, q, kv, logs)] + [(w, "a") for w in weights]
    outs = [((rows, d), B16, "v"), ((4, rows, 640), B16, "v")]
    scratch = [pltpu.VMEM((4, d, d), B16), pltpu.VMEM((6, rows, 128), B16)]
    scratch += [pltpu.VMEM((rows, 128), B16), copy_sems(sz, 1)]
    return run(kernel, "space_backward_scores", ins, outs, scratch, 30)


def weight_slopes(sz, name, meta, up, normed, mixed, slopes, fast):
    rows, d = sz["rows"], sz["d"]
    g_outs = gradient_outs(sz, 1, fast)
    join = len(slopes) == 3

    def kernel(*refs):
        meta, up, normed, mixed = refs[:4]
        given, refs = refs[4 : 4 + len(slopes)], refs[4 + len(slopes) :]
        dy = refs[0] if join else given[0]
        g_bufs, (dw, up_t, normed_t, sems) = refs[1 if join else 0 : -4], refs[-4:]
        if join:
            dq, dkv, got = given

            def both(j, at):
                return (dkv[j, at, :].astype(F32) + got[j, at, :].astype(F32)).astype(B16)

            @pl.loop(0, 4)
            def _(r):
                at = row_slices(r)
                for j in range(4):
                    dy[j, at, 0:128] = dq[j, at, :]
                    dy[j, at, 128:256] = both(j, at)
                    dy[j, at, 256:384] = both(6 + j, at)
                for u in range(2):
                    place_third(dq[4 + u, at, :], both(4 + u, at), both(10 + u, at), dy, u, at)

        transpose_into(normed, normed_t)
        transpose_into(up, up_t)
        head_gradients(dw, normed_t, up_t, dy, mixed, d)
        back = weight_copies(meta, g_bufs, [dw], sems, sz["n"], back=True, shifts=join)
        start_all(back)
        wait_all(back)

    ins = [(meta, "s")] + [(v, "v") for v in (up, normed, mixed, *slopes)]
    outs = ([((4, rows, 640), B16, "v")] if join else []) + g_outs
    scratch = [pltpu.VMEM((4, d, d), B16)] + [pltpu.VMEM((d, rows), B16)] * 2
    scratch += [copy_sems(sz, 1)]
    return run(kernel, name, ins, outs, scratch, 14)


def input_slopes(sz, name, meta, vec, up, stream, dy, weights, gain_row, blocks):
    rows, d, places = sz["rows"], sz["d"], sz["places"]
    nw = len(weights)

    def kernel(*refs):
        meta, vec, up, stream, dy = refs[:5]
        bufs, refs = refs[5 : 5 + nw], refs[5 + nw :]
        outs, vgrad, w, sems = refs[:-3], refs[-3], refs[-2], refs[-1]
        if blocks:
            outs, vgrad, dx, w, sems = refs[:4], refs[4], refs[5], refs[6], refs[7]
        else:
            dx = outs[0]
        copies = weight_copies(meta, bufs, [w], sems, sz["n"], shifts=bool(blocks))
        start_all(copies)
        vgrad[...] = jnp.zeros_like(vgrad)
        wait_all(copies)

        @pl.loop(0, 4)
        def _(r):
            at = row_slices(r)
            v = up[at, :]
            gain = vec[gain_row : gain_row + 1, :]
            down, gg, gs = norm_back(stream[at, :], gain, norm_slopes(at, dy, w))
            dx[at, :] = v + down
            vgrad[0:1, :] += gg
            vgrad[1:2, :] += gs
            vgrad[2:3, :] += jnp.sum(v, axis=0, keepdims=True)

        if blocks:
            give_blocks(dx, outs, places)

    ins = [(meta, "s")] + [(v, "v") for v in (vec, up, stream, dy)] + [(w, "a") for w in weights]
    outs = [((rows, d), F32, "v")]
    scratch = []
    if blocks:
        outs = [((2, places, d), F32, "v")] + [((2, places, d), B16, "v")] * 3
        scratch = [pltpu.VMEM((rows, d), F32)]
    outs += [((8, d), F32, "v")]
    scratch += [pltpu.VMEM((4, d, d), B16), copy_sems(sz, 1)]
    return run(kernel, name, ins, outs, scratch, 14)


def time_backward_scores(sz, meta, d1, q, kv, kvo, prob, weights):
    rows, d = sz["rows"], sz["d"]
    nw = len(weights)

    def kernel(*refs):
        meta, d1, q, kv, kvo, prob = refs[:6]
        bufs, refs = refs[6 : 6 + nw], refs[6 + nw :]
        up, dq, dkv, dkvo, w, dm, sums, spreads, ds, acc, sems = refs
        copies = weight_copies(meta, bufs, [w], sems, sz["n"], shifts=True)
        start_all(copies)
        head_sums(sums)
        head_spreads(spreads)

        @pl.loop(0, 4)
        def _(r):
            up[row_slices(r), :] = d1[row_slices(r), :].astype(B16)

        wait_all(copies)
        mixed_slopes(up, w, dm, rows, 416)
        for h, ref in enumerate((kv, kvo)):

            @pl.loop(0, 4)
            def _(g):
                ds[4 * h + g] = pair_sums(dm, ref, 6, g, sums)

        @pl.loop(0, 13)
        def _(r):
            at = row_slices(r, 16)
            p = [prob[g, at, :] for g in range(8)]
            dp = [ds[g, at, :] for g in range(8)]
            inner = functools.reduce(lambda a, b: a + b, [a * b for a, b in zip(p, dp)])
            for g in range(8):
                ds[g, at, :] = p[g] * (dp[g] - inner) * SCALING

        acc[...] = jnp.zeros_like(acc)
        for h, (ref, out) in enumerate(((kv, dkv), (kvo, dkvo))):

            @pl.loop(0, 4)
            def _(g):
                at = row_slices(g)
                both = jnp.concatenate([ds[4 * h + g], prob[4 * h + g]], axis=0).astype(B16)
                for jj in range(3):
                    k = two_tiles(ref, 2 * jj, at)
                    dk = dv = None
                    for f in range(4):
                        fr = slice(f * 208, f * 208 + 208)
                        e = dot(both, spreads[:, f * d + 256 * jj : f * d + 256 * jj + 256])
                        se, pe = e[:208], e[208:]
                        acc[fr, 256 * jj : 256 * jj + 256] += se * k
                        a = se * two_tiles(q, 2 * jj, fr)
                        b = pe * two_tiles(dm, 2 * jj, fr)
                        dk, dv = (a, b) if dk is None else (dk + a, dv + b)
                    dk, dv = dk.astype(B16), dv.astype(B16)
                    for i in range(2):
                        out[2 * jj + i, at, :] = dk[:, 128 * i : 128 * i + 128]
                        out[6 + 2 * jj + i, at, :] = dv[:, 128 * i : 128 * i + 128]

        for j in range(6):
            dq[j] = acc[:, 128 * j : 128 * j + 128].astype(B16)

    ins = [(meta, "s")] + [(v, "v") for v in (d1, q, kv, kvo, prob)] + [(w, "a") for w in weights]
    outs = [
        ((rows, d), B16, "v"),
        ((6, rows, 128), B16, "v"),
        ((12, rows, 128), B16, "v"),
        ((12, rows, 128), B16, "v"),
    ]
    scratch = [
        pltpu.VMEM((4, d, d), B16),
        pltpu.VMEM((6, rows, 128), B16),
        pltpu.VMEM((4 * d, 128), B16),
        pltpu.VMEM((128, 4 * d), B16),
        pltpu.VMEM((8, 208, 128), F32),
        pltpu.VMEM((rows, d), F32),
        copy_sems(sz, 1),
    ]
    return run(kernel, "time_backward_scores", ins, outs, scratch, 23)


def pack_heads(qkv, proj, odd):
    q, k, v = qkv[:, 0], qkv[:, 1], qkv[:, 2]
    o = proj.T
    first = [q[:, :128], k[:, :128], v[:, :128]]
    even = first + [q[:, 128:], k[:, 128:], o[:, :128], o[:, 128:], v[:, 128:]]
    other = first + [k[:, 128:], q[:, 128:], o[:, :128], v[:, 128:], o[:, 128:]]
    return jnp.where(odd, jnp.concatenate(other, axis=1), jnp.concatenate(even, axis=1))


def unpack_heads(g, odd):
    def pick(a, b):
        return jnp.where(odd, g[:, b : b + 64], g[:, a : a + 64])

    q = jnp.concatenate([g[:, 0:128], pick(384, 448)], axis=1)
    k = jnp.concatenate([g[:, 128:256], pick(448, 384)], axis=1)
    v = jnp.concatenate([g[:, 256:384], pick(704, 640)], axis=1)
    o = jnp.concatenate([g[:, 512:640], pick(640, 704)], axis=1)
    return jnp.stack([q, k, v], axis=1), o.T


def local(mesh_shape, video, cotangent, *params):
    qkv_time, proj_time, qkv_space, proj_space, fc_in, fc_out = params[:6]
    vectors = params[6:]
    n = mesh_shape["shard"]
    d = proj_time.shape[0] * 4
    places = video.shape[2]
    rows_here = fc_in.shape[0]
    fast = rows_here % 16 == 0
    sz = {"n": n, "d": d, "places": places, "rows": 8 * PAD}
    x, y = lax.axis_index("x"), lax.axis_index("ctx")
    c, z = lax.axis_index("core"), lax.axis_index("shard")
    meta = jnp.stack([x, y, c, z]).astype(jnp.int32)
    every = ("shard", "ctx", "x", "core")
    count = 8 * n

    share = jnp.concatenate([v.reshape(1, -1) for v in vectors], axis=1)
    share = jnp.broadcast_to(share, (count, share.shape[1]))
    shares = lax.all_to_all(share, every, split_axis=0, concat_axis=0, tiled=True)
    per = d // count
    order = [0, 1, 2, 3, 4, 5, 6, 7, 9]
    starts = [per * i for i in range(9)] + [per * 12]
    vec = jnp.stack([shares[:, starts[i] : starts[i] + per].reshape(d) for i in order])
    hidden = shares[:, starts[8] : starts[8] + 4 * per].reshape(4, d)
    vec = jnp.concatenate([vec, hidden, jnp.zeros((3, d), F32)], axis=0)

    def clips_of(v):
        return [
            lax.dynamic_index_in_dim(v, 2 * (x ^ dx) + (y ^ dy), 0, keepdims=False)
            for dx, dy in ((0, 0), (1, 0), (0, 1), (1, 1))
        ]

    def frames_back(blocks):
        return [blocks[0], over_x(blocks[1]), over_y(blocks[2]), over_xy(blocks[3])]

    def join_clips(blocks, dtype):
        out = jnp.zeros((4,) + blocks[0].shape, dtype)
        for k, b in enumerate(blocks):
            at = 2 * (x ^ (k % 2)) + (y ^ (k // 2))
            out = lax.dynamic_update_slice_in_dim(out, b.astype(dtype)[None], at, 0)
        return out

    gather, reduce = (Gather, Reduce) if fast else (GatherWhole, ReduceWhole)

    g_t = gather([pack_heads(qkv_time, proj_time, c == 1)], n, True)
    g_s = gather([pack_heads(qkv_space, proj_space, c == 1)], n)
    g_m = gather([fc_in, fc_out.T], n)
    t_z = g_t.stage_z()
    clips = clips_of(video)
    video_blocks = [clips[0], over_x(clips[1]), over_y(clips[2])]
    t_xy = g_t.stage_xy(*video_blocks[1:])
    video_blocks.append(over_xy(after(clips[3], *t_z)))
    s_z = g_s.stage_z(vec)
    t_rest = g_t.stage_rest(*s_z)
    s_xy = g_s.stage_xy(*t_rest)
    m_z = g_m.stage_z(*s_z)
    w_time = g_t.stage_core()
    cot_sent = clips_of(after(cotangent, *t_xy))
    vec_t = after(vec, *g_s.sent, *cot_sent)
    stream0, normed_t, q_t, kv_t = time_qkv(sz, meta, vec_t, video_blocks, w_time)

    kv_o = over_core(after(kv_t, *s_xy))
    s_rest = g_s.stage_rest(kv_t)
    cot_blocks = frames_back(after(tuple(cot_sent), kv_t))
    kv_o = after(kv_o, *g_s.sent)
    mixed_t, stream1, prob_t = time_mix(sz, meta, vec, stream0, q_t, kv_t, kv_o, w_time)

    w_space = g_s.stage_core(stream1)
    m_xy = g_m.stage_xy(stream1)
    stream1s = after(stream1, *g_m.sent, *cot_blocks)
    normed_s, q_s, kv_s, mixed_s, logs, stream2 = space_forward(sz, meta, vec, stream1s, w_space)

    m_rest = g_m.stage_rest(stream2)
    w_mlp = g_m.stage_core()
    res, d2, vg_m, parts_m = feed_forward(sz, meta, vec, stream2, cot_blocks, w_mlp, fast)

    r_m = reduce(parts_m, n, "mlp")
    m_core = r_m.stage_core()
    result_back = frames_back(res)
    up_s, dy_s = space_backward_scores(sz, meta, d2, q_s, kv_s, logs, w_space)

    m_rest = r_m.stage_rest(up_s)
    dy_s = after(dy_s, *result_back, *r_m.sent)
    parts_s = weight_slopes(sz, "space_weights", meta, up_s, normed_s, mixed_s, [dy_s], fast)
    r_s = reduce(parts_s, n, "space")
    s_core = r_s.stage_core(*m_rest)
    m_xy = r_m.stage_xy(*parts_s)
    d2b = after(d2, *parts_s, *r_m.sent)
    d1, vg_s = input_slopes(sz, "space_input", meta, vec, d2b, stream1, dy_s, w_space, 3, False)
    s_rest = r_s.stage_rest(d1)
    d1b = after(d1, *r_s.sent)
    up_t, dq, dkv, dkvo = time_backward_scores(sz, meta, d1b, q_t, kv_t, kv_o, prob_t, w_time)

    dkv_got = over_core(after(dkvo, *m_xy, *s_rest))
    m_z = r_m.stage_z(dkvo)
    s_xy = r_s.stage_xy(dkvo)
    dkv_got = after(dkv_got, *r_s.sent, *r_m.sent)
    dy_t, *parts_t = weight_slopes(
        sz, "time_weights", meta, up_t, normed_t, mixed_t, [dq, dkv, dkv_got], fast
    )

    r_t = reduce(parts_t, n, "time", True)
    t_core = r_t.stage_core(*m_z, *s_xy)
    s_z = r_s.stage_z(*parts_t)
    t_rest = r_t.stage_rest(*r_s.sent)
    d1c = after(d1, *r_s.sent, *r_t.sent)
    *dx, vg_t = input_slopes(sz, "time_input", meta, vec, d1c, stream0, dy_t, w_time, 0, True)

    t_xy = r_t.stage_xy(vg_t)
    t_z = r_t.stage_z()
    vg_t2 = after(vg_t, *r_t.sent)
    video_back = frames_back(after(tuple(dx), *r_t.sent))
    result = join_clips(after(tuple(result_back), vg_t), B16)
    grad_video = join_clips(video_back, F32)
    grad_in, grad_out = r_m.results(*parts_t)
    (grad_s,) = r_s.results(vg_t)
    (grad_t,) = r_t.results()

    rows = jnp.concatenate([vg_t2[0:3], vg_s[0:3], vg_m[0:2]], axis=0)
    parts = jnp.concatenate(
        [
            rows.reshape(8, count, per).transpose(1, 0, 2).reshape(count, 8 * per),
            vg_m[4:8].reshape(count, 4 * per),
            vg_m[2].reshape(count, per),
        ],
        axis=1,
    )
    got = lax.all_to_all(parts, every, split_axis=0, concat_axis=0, tiled=True)
    sums = jnp.sum(got, axis=0)
    cuts = [sums[starts[i] : starts[i] + (4 * per if i == 8 else per)] for i in range(10)]

    qkv_t_grad, proj_t_grad = unpack_heads(grad_t, c == 1)
    qkv_s_grad, proj_s_grad = unpack_heads(grad_s, c == 1)
    return (
        result,
        grad_video,
        qkv_t_grad,
        proj_t_grad,
        qkv_s_grad,
        proj_s_grad,
        grad_in,
        grad_out.T,
        *cuts,
    )


def solution(mesh):
    shape = dict(mesh.shape)
    fine = Mesh(
        mesh.devices.reshape(shape["shard"], shape["ctx"], 2, shape["tp"] // 2),
        ("shard", "ctx", "x", "core"),
    )
    tp = ("x", "core")
    sc = ("shard", "ctx")
    tokens = P("shard", tp, "ctx", None)
    weights = (P(sc, None, tp), P(tp, sc), P(sc, None, tp), P(tp, sc), P(sc, tp), P(tp, sc))
    vectors = (P(("shard", "ctx", "x", "core")),) * 10
    return jax.shard_map(
        functools.partial(local, shape),
        mesh=fine,
        in_specs=(tokens, tokens) + weights + vectors,
        out_specs=(tokens, tokens) + weights + vectors,
        check_vma=False,
    )
```

profile of v0, /device:TPU:0, one launch (start us, length us, event | category | flops | bytes accessed | tf_op | source)
XLA Modules:
  0.0 462.1 jit_solution(12000887414836299794)
XLA Ops:
  2.9 5.1 %collective-permute-start = (bf16[1,96,768]{2,1,0:T(8,128)(2,1)S(1)}, bf16[1,96,768]{2,1,0:T(8,128)(2,1)S(1)}, u32[]{:S(2)}, u32[]{:S(2)}) collective-permute-start(bf16[1,96,768]{2,1,0:T(8,128)(2,1)S(1)} %broadcast_select_fusion.1), channel_id=1, source_target_pairs={{8,0},{16,8},{24,16},{0,24},{9,1},{17,9},{25,17},{1,25},{10,2},{18... | collective-permute-start | bytes 442376 | tf_op jit(solution)/shard_map/ppermute | solution.py:63
  10.0 1.6 collective-permute-start.3
  11.6 1.6 collective-permute-start.4
  14.0 3.2 all-to-all-start
  18.8 5.8 %all-to-all-done = f32[32,1,312]{2,1,0:T(1,128)S(1)} async-done(((f32[32,1,312]{2,1,0:T(1,128)}), f32[32,1,312]{2,1,0:T(1,128)S(1)}, u32[]{:S(2)}, u32[]{:S(2)}) %all-to-all-start) | async-done | bytes 39968 | tf_op jit(solution)/shard_map/all_to_all | solution.py:978
  26.9 4.1 all-to-all-start.1
  35.1 14.3 %collective-permute-done.5.refs_7_.refs_6_ = bf16[4,96,768]{2,1,0:T(8,128)(2,1)S(1)} collective-permute-done((bf16[4,96,768]{2,1,0:T(8,128)(2,1)}, bf16[4,96,768]{2,1,0:T(8,128)(2,1)S(1)}, u32[]{:S(2)}, u32[]{:S(2)}) %collective-permute-start.5) | collective-permute-done | bytes 589856 | tf_op jit(solution)/shard_map/ppermute | solution.py:25
  50.4 2.4 collective-permute-start.9
  53.9 10.7 %collective-permute-done.7.refs_9_.refs_8_ = bf16[2,96,768]{2,1,0:T(8,128)(2,1)S(1)} collective-permute-done((bf16[2,96,768]{2,1,0:T(8,128)(2,1)S(1)}, bf16[2,96,768]{2,1,0:T(8,128)(2,1)S(1)}, u32[]{:S(2)}, u32[]{:S(2)}) %collective-permute-start.7) | collective-permute-done | bytes 294944 | tf_op jit(solution)/shard_map/ppermute | solution.py:29
  74.4 12.0 %time_qkv.1 = (f32[832,768]{1,0:T(8,128)}, bf16[832,768]{1,0:T(8,128)(2,1)}, bf16[6,832,128]{2,1,0:T(8,128)(2,1)}, bf16[12,832,128]{2,1,0:T(8,128)(2,1)}) custom-call(s32[4]{0:T(128)} %pad_add_fusion.refs_0_, f32[16,768]{1,0:T(8,128)} %concatenate.97.refs_1_, bf16[2,98,768]{2,1,0:T(8,128)(2,1)} %bitcast.133, bf16[2,98,768]{2,1,0:T(8,128)(2,1)} %copy-done.44, ...), custom_call_target="tpu_custom_call" | custom-call | flops 12000000000 | bytes 36000000 | tf_op jit(solution)/shard_map/time_qkv/pallas_call | solution.py:372
  86.4 1.6 collective-permute-done.15.refs_4_.refs_6_
  94.9 4.6 all-to-all-start.2
  99.6 1.6 collective-permute-start.19
  101.8 4.4 collective-permute-done.22.refs_7_.refs_9_
  106.2 16.8 %time_mix.1 = (bf16[6,832,128]{2,1,0:T(8,128)(2,1)}, f32[832,768]{1,0:T(8,128)}, f32[8,208,128]{2,1,0:T(8,128)}) custom-call(s32[4]{0:T(128)} %pad_add_fusion.refs_0_, f32[16,768]{1,0:T(8,128)} %concatenate.97.refs_1_, f32[832,768]{1,0:T(8,128)} %get-tuple-element.154.refs_2_.refs_3_, bf16[6,832,128]{2,1,0:T(8,128)(2,1)} %get-tuple-element.155.refs_3_.refs_2_, ...), custom_call_target="tpu_custom_call" | custom-call | flops 16999999488 | bytes 51000000 | tf_op jit(solution)/shard_map/time_mix/pallas_call | solution.py:372
  123.6 4.5 all-to-all-done.2
  130.2 28.8 %space_forward.1 = (bf16[832,768]{1,0:T(8,128)(2,1)}, bf16[6,832,128]{2,1,0:T(8,128)(2,1)}, bf16[12,832,128]{2,1,0:T(8,128)(2,1)}, bf16[6,832,128]{2,1,0:T(8,128...) custom-call(s32[4]{0:T(128)} %pad_add_fusion.refs_0_, f32[16,768]{1,0:T(8,128)} %concatenate.97.refs_1_, ...), custom_call_target="tpu_custom_call" | custom-call | flops 28999999488 | bytes 87000000 | tf_op jit(solution)/shard_map/space_forward/pallas_call | solution.py:372
  163.8 10.2 %collective-permute-done.30.refs_10_ = bf16[4,96,768]{2,1,0:T(8,128)(2,1)S(1)} collective-permute-done((bf16[4,96,768]{2,1,0:T(8,128)(2,1)S(1)}, bf16[4,96,768]{2,1,0:T(8,128)(2,1)S(1)}, u32[]{:S(2)}, u32[]{:S(2)}) %collective-permute-start.30) | collective-permute-done | bytes 589856 | tf_op jit(solution)/shard_map/ppermute | solution.py:29
  179.0 46.6 %feed_forward.1 = (bf16[2,98,768]{2,1,0:T(8,128)(2,1)}, bf16[2,98,768]{2,1,0:T(8,128)(2,1)}, bf16[2,98,768]{2,1,0:T(8,128)(2,1)}, bf16[2,98,768]{2,1,0:T(8,128)(...) custom-call(s32[4]{0:T(128)} %pad_add_fusion.refs_0_, ...), custom_call_target="tpu_custom_call" | custom-call | flops 46999998464 | bytes 141000000 | tf_op jit(solution)/shard_map/feed_forward/pallas_call | solution.py:372
  229.4 29.0 %space_backward_scores.1 = (bf16[832,768]{1,0:T(8,128)(2,1)}, bf16[4,832,640]{2,1,0:T(8,128)(2,1)}) custom-call(s32[4]{0:T(128)} %pad_add_fusion.refs_0_, f32[832,768]{1,0:T(8,128)} %get-tuple-element.200.refs_1_.refs_2_, bf16[6,832,128]{2,1,0:T(8,128)(2,1)} %get-tuple-element.181.refs_2_, bf16[12,832,128]{2,1,0:T(8,128)(2,1)} %get-tuple-element.182.refs_3_, ...), custom_call_target="tpu_custom_call" | custom-call | flops 30000001024 | bytes 90000000 | tf_op jit(solution)/shard_map/space_backward_scores/pallas_call | solution.py:372
  258.4 2.3 copy-done.4
  260.7 2.4 mlp_rest.1
  266.1 14.0 %space_weights.1 = (bf16[16,96,768]{2,1,0:T(8,128)(2,1)}, bf16[16,96,768]{2,1,0:T(8,128)(2,1)}) custom-call(s32[4]{0:T(128)} %pad_add_fusion.refs_0_, bf16[832,768]{1,0:T(8,128)(2,1)} %get-tuple-element.184.refs_1_, bf16[832,768]{1,0:T(8,128)(2,1)} %get-tuple-element.185.refs_2_, bf16[6,832,128]{2,1,0:T(8,128)(2,1)} %get-tuple-element.186.refs_3_, ...), custom_call_target="tpu_custom_call" | custom-call | flops 14000000000 | bytes 42000000 | tf_op jit(solution)/shard_map/space_weights/pallas_call | solution.py:372
  280.2 2.3 copy-done.5
  282.5 3.7 mlp_xy.1
  287.4 14.4 %space_input.1 = (f32[832,768]{1,0:T(8,128)}, f32[8,768]{1,0:T(8,128)}) custom-call(s32[4]{0:T(128)} %pad_add_fusion.refs_0_, f32[16,768]{1,0:T(8,128)} %concatenate.97.refs_1_, f32[832,768]{1,0:T(8,128)} %get-tuple-element.200.refs_1_.refs_2_, f32[832,768]{1,0:T(8,128)} %get-tuple-element.168.refs_2_.refs_3_, ...), custom_call_target="tpu_custom_call" | custom-call | flops 14000000000 | bytes 42000000 | tf_op jit(solution)/shard_map/space_input/pallas_call | solution.py:372
  301.8 1.7 copy-done.7
  303.5 1.9 space_rest.1
  308.3 22.8 %time_backward_scores.1 = (bf16[832,768]{1,0:T(8,128)(2,1)}, bf16[6,832,128]{2,1,0:T(8,128)(2,1)}, bf16[12,832,128]{2,1,0:T(8,128)(2,1)}, bf16[12,832,128]{2,1,0:T(8,128)(2,1)}) custom-call(s32[4]{0:T(128)} %pad_add_fusion.refs_0_, f32[832,768]{1,0:T(8,128)} %get-tuple-element.230.refs_1_.refs_2_, bf16[6,832,128]{2,1,0:T(8,128)(2,1)} %get-tuple-element.155.refs_3_.refs_2_, ...), custom_call_target="tpu_custom_call" | custom-call | flops 23000000512 | bytes 69000000 | tf_op jit(solution)/shard_map/time_backward_scores/pallas_call | solution.py:372
  331.2 2.3 copy-done.6
  333.6 3.6 mlp_z.1
  337.1 4.7 %all-to-all-start.3 = ((bf16[4,2,96,768]{3,2,1,0:T(8,128)(2,1)}), bf16[4,2,96,768]{3,2,1,0:T(8,128)(2,1)}, u32[]{:S(2)}, u32[]{:S(2)}) async-start(bf16[4,2,96,768]{3,2,1,0:T(8,128)(2,1)} %bitcast.44), calls=%async_computation.3 | async-start | bytes 2359296 | tf_op jit(solution)/shard_map/all_to_all | solution.py:41
  341.8 2.7 space_xy.1
  345.7 17.6 %time_weights.1 = (bf16[4,832,640]{2,1,0:T(8,128)(2,1)}, bf16[16,96,768]{2,1,0:T(8,128)(2,1)}, bf16[16,96,768]{2,1,0:T(8,128)(2,1)}) custom-call(s32[4]{0:T(128)} %pad_add_fusion.refs_0_, bf16[832,768]{1,0:T(8,128)(2,1)} %get-tuple-element.213.refs_1_, bf16[832,768]{1,0:T(8,128)(2,1)} %get-tuple-element.214.refs_2_, ...), custom_call_target="tpu_custom_call" | custom-call | flops 14000000000 | bytes 42000000 | tf_op jit(solution)/shard_map/time_weights/pallas_call | solution.py:372
  363.3 8.0 %all-to-all-done.3 = bf16[4,2,96,768]{3,2,1,0:T(8,128)(2,1)} async-done(((bf16[4,2,96,768]{3,2,1,0:T(8,128)(2,1)}), bf16[4,2,96,768]{3,2,1,0:T(8,128)(2,1)}, u32[]{:S(2)}, u32[]{:S(2)}) %all-to-all-start.3) | async-done | bytes 1179680 | tf_op jit(solution)/shard_map/all_to_all | solution.py:41
  376.9 1.7 copy-done.9
  378.5 2.5 space_z.1
  381.1 4.2 all-to-all-start.4
  385.2 1.6 convert_reduce_fusion
  390.6 14.0 %time_input.1 = (f32[2,98,768]{2,1,0:T(8,128)}, bf16[2,98,768]{2,1,0:T(8,128)(2,1)}, bf16[2,98,768]{2,1,0:T(8,128)(2,1)}, bf16[2,98,768]{2,1,0:T(8,128)(2,1)}, f32[8,768]{1,0:T(8,128)}) custom-call(s32[4]{0:T(128)} %pad_add_fusion.refs_0_, f32[16,768]{1,0:T(8,128)} %concatenate.97.refs_1_, f32[832,768]{1,0:T(8,128)} %get-tuple-element.230.refs_1_.refs_2_, ...), custom_call_target="tpu_custom_call" | custom-call | flops 14000000000 | bytes 42000000 | tf_op jit(solution)/shard_map/time_input/pallas_call | solution.py:372
  408.3 1.7 copy-done.3
  417.5 9.1 %collective-permute-done.54.refs_2_.refs_6_.refs_10_.refs_14_ = bf16[4,96,768]{2,1,0:T(8,128)(2,1)S(1)} collective-permute-done((bf16[4,96,768]{2,1,0:T(8,128)(2,1)S(1)}, bf16[4,96,768]{2,1,0:T(8,128)(2,1)S(1)}, u32[]{:S(2)}, u32[]{:S(2)}) %collective-permute-start.54) | collective-permute-done | bytes 589856 | tf_op jit(solution)/shard_map/ppermute | solution.py:25
  427.9 1.7 collective-permute-start.59
  429.7 2.4 collective-permute-start.60
  434.6 3.5 all-to-all-start.5
  438.2 1.8 collective-permute-start.56
  442.5 3.5 all-to-all-done.5
  456.7 2.0 collective-permute-done.58
  (325 shorter events, 96.7 us)
Async XLA Ops:
  2.9 28.2 %collective-permute-start = (bf16[1,96,768]{2,1,0:T(8,128)(2,1)S(1)}, bf16[1,96,768]{2,1,0:T(8,128)(2,1)S(1)}, u32[]{:S(2)}, u32[]{:S(2)}) collective-permute-start(bf16[1,96,768]{2,1,0:T(8,128)(2,1)S(1)} %broadcast_select_fusion.1), channel_id=1, source_target_pairs={{8,0},{16,8},{24,16},{0,24},{9,1},{17,9},{25,17},{1,25},{10,2},{18... | collective-permute-start | bytes 442376 | tf_op jit(solution)/shard_map/ppermute | solution.py:63
  8.0 23.1 %collective-permute-start.1 = (bf16[1,96,768]{2,1,0:T(8,128)(2,1)S(1)}, bf16[1,96,768]{2,1,0:T(8,128)(2,1)S(1)}, u32[]{:S(2)}, u32[]{:S(2)}) collective-permute-start(bf16[1,96,768]{2,1,0:T(8,128)(2,1)S(1)} %broadcast_select_fusion.1), channel_id=1, source_target_pairs={{16,0},{24,8},{0,16},{8,24},{17,1},{25,9},{1,17},{9,25},{18,2},{26... | collective-permute-start | bytes 442376 | tf_op jit(solution)/shard_map/ppermute | solution.py:63
  8.0 23.1 %collective-permute-start.2 = (bf16[1,96,768]{2,1,0:T(8,128)(2,1)S(1)}, bf16[1,96,768]{2,1,0:T(8,128)(2,1)S(1)}, u32[]{:S(2)}, u32[]{:S(2)}) collective-permute-start(bf16[1,96,768]{2,1,0:T(8,128)(2,1)S(1)} %broadcast_select_fusion.1), channel_id=1, source_target_pairs={{24,0},{0,8},{8,16},{16,24},{25,1},{1,9},{9,17},{17,25},{26,2},{2,... | collective-permute-start | bytes 442376 | tf_op jit(solution)/shard_map/ppermute | solution.py:63
  10.0 21.1 %collective-permute-start.3 = (bf16[2,98,768]{2,1,0:T(8,128)(2,1)S(1)}, bf16[2,98,768]{2,1,0:T(8,128)(2,1)S(1)}, u32[]{:S(2)}, u32[]{:S(2)}) collective-permute-start(bf16[2,98,768]{2,1,0:T(8,128)(2,1)S(1)} %bitcast.130), channel_id=1, source_target_pairs={{0,2},{2,0},{1,3},{3,1},{4,6},{6,4},{5,7},{7,5},{8,10},{10,8},{9,1... | collective-permute-start | bytes 903176 | tf_op jit(solution)/shard_map/ppermute | solution.py:25
  11.6 19.5 %collective-permute-start.4 = (bf16[2,98,768]{2,1,0:T(8,128)(2,1)S(1)}, bf16[2,98,768]{2,1,0:T(8,128)(2,1)S(1)}, u32[]{:S(2)}, u32[]{:S(2)}) collective-permute-start(bf16[2,98,768]{2,1,0:T(8,128)(2,1)S(1)} %bitcast.131), channel_id=1, source_target_pairs={{0,4},{4,0},{1,5},{5,1},{2,6},{6,2},{3,7},{7,3},{8,12},{12,8},{9,1... | collective-permute-start | bytes 903176 | tf_op jit(solution)/shard_map/ppermute | solution.py:29
  26.9 22.7 %all-to-all-start.1 = ((bf16[4,1,96,768]{3,2,1,0:T(8,128)(2,1)}), bf16[4,1,96,768]{3,2,1,0:T(8,128)(2,1)}, u32[]{:S(2)}, u32[]{:S(2)}) async-start(bf16[4,1,96,768]{3,2,1,0:T(8,128)(2,1)} %broadcast_in_dim.61), calls=%async_computation.1 | async-start | bytes 1179648 | tf_op jit(solution)/shard_map/all_to_all | solution.py:41
  33.9 15.6 %collective-permute-start.5 = (bf16[4,96,768]{2,1,0:T(8,128)(2,1)}, bf16[4,96,768]{2,1,0:T(8,128)(2,1)S(1)}, u32[]{:S(2)}, u32[]{:S(2)}) collective-permute-start(bf16[4,96,768]{2,1,0:T(8,128)(2,1)} %constant_dynamic-update-slice_fusion.15.refs_6_.refs_5_), channel_id=1, source_target_pairs={{0,2},{2,0},{1,3},{3,1},{4,6},{6,4},{5,7},{7,5},{8,10},{10,8},{9,1... | collective-permute-start | bytes 1769480 | tf_op jit(solution)/shard_map/ppermute | solution.py:25
  34.4 15.3 %collective-permute-start.6 = (bf16[4,96,768]{2,1,0:T(8,128)(2,1)}, bf16[4,96,768]{2,1,0:T(8,128)(2,1)S(1)}, u32[]{:S(2)}, u32[]{:S(2)}) collective-permute-start(bf16[4,96,768]{2,1,0:T(8,128)(2,1)} %constant_dynamic-update-slice_fusion.15.refs_6_.refs_5_), channel_id=1, source_target_pairs={{0,4},{4,0},{1,5},{5,1},{2,6},{6,2},{3,7},{7,3},{8,12},{12,8},{9,1... | collective-permute-start | bytes 1769480 | tf_op jit(solution)/shard_map/ppermute | solution.py:29
  49.7 14.9 %collective-permute-start.7 = (bf16[2,96,768]{2,1,0:T(8,128)(2,1)S(1)}, bf16[2,96,768]{2,1,0:T(8,128)(2,1)S(1)}, u32[]{:S(2)}, u32[]{:S(2)}) collective-permute-start(bf16[2,96,768]{2,1,0:T(8,128)(2,1)S(1)} %slice.265), channel_id=1, source_target_pairs={{0,4},{4,0},{1,5},{5,1},{2,6},{6,2},{3,7},{7,3},{8,12},{12,8},{9,1... | collective-permute-start | bytes 884744 | tf_op jit(solution)/shard_map/ppermute | solution.py:29
  50.4 15.6 %collective-permute-start.9 = (bf16[2,98,768]{2,1,0:T(8,128)(2,1)S(1)}, bf16[2,98,768]{2,1,0:T(8,128)(2,1)S(1)}, u32[]{:S(2)}, u32[]{:S(2)}) collective-permute-start(bf16[2,98,768]{2,1,0:T(8,128)(2,1)S(1)} %bitcast.134), channel_id=1, source_target_pairs={{0,6},{2,4},{4,2},{6,0},{1,7},{3,5},{5,3},{7,1},{8,14},{10,12},{12... | collective-permute-start | bytes 903176 | tf_op jit(solution)/shard_map/ppermute | solution.py:33
  53.4 19.1 %collective-permute-start.10 = (bf16[4,96,768]{2,1,0:T(8,128)(2,1)}, bf16[4,96,768]{2,1,0:T(8,128)(2,1)}, u32[]{:S(2)}, u32[]{:S(2)}) collective-permute-start(bf16[4,96,768]{2,1,0:T(8,128)(2,1)} %constant_dynamic-update-slice_fusion.15.refs_6_.refs_5_), channel_id=1, source_target_pairs={{0,1},{1,0},{2,3},{3,2},{4,5},{5,4},{6,7},{7,6},{8,9},{9,8},{10,11... | collective-permute-start | bytes 1769480 | tf_op jit(solution)/shard_map/ppermute | solution.py:37
  53.4 20.5 %collective-permute-start.11 = (bf16[4,96,768]{2,1,0:T(8,128)(2,1)S(1)}, bf16[4,96,768]{2,1,0:T(8,128)(2,1)}, u32[]{:S(2)}, u32[]{:S(2)}) collective-permute-start(bf16[4,96,768]{2,1,0:T(8,128)(2,1)S(1)} %collective-permute-done.5.refs_7_.refs_6_), channel_id=1, source_target_pairs={{0,1},{1,0},{2,3},{3,2},{4,5},{5,4},{6,7},{7,6},{8,9},{9,8},{10,11... | collective-permute-start | bytes 1769480 | tf_op jit(solution)/shard_map/ppermute | solution.py:37
  72.5 15.6 %collective-permute-start.15 = (bf16[4,96,768]{2,1,0:T(8,128)(2,1)}, bf16[4,96,768]{2,1,0:T(8,128)(2,1)}, u32[]{:S(2)}, u32[]{:S(2)}) collective-permute-start(bf16[4,96,768]{2,1,0:T(8,128)(2,1)} %bitcast.33.refs_3_.refs_5_), channel_id=1, source_target_pairs={{0,2},{2,0},{1,3},{3,1},{4,6},{6,4},{5,7},{7,5},{8,10},{10,8},{9,1... | collective-permute-start | bytes 1769480 | tf_op jit(solution)/shard_map/ppermute | solution.py:25
  73.9 15.3 %collective-permute-start.16 = (bf16[4,96,768]{2,1,0:T(8,128)(2,1)}, bf16[4,96,768]{2,1,0:T(8,128)(2,1)}, u32[]{:S(2)}, u32[]{:S(2)}) collective-permute-start(bf16[4,96,768]{2,1,0:T(8,128)(2,1)} %bitcast.33.refs_3_.refs_5_), channel_id=1, source_target_pairs={{0,4},{4,0},{1,5},{5,1},{2,6},{6,2},{3,7},{7,3},{8,12},{12,8},{9,1... | collective-permute-start | bytes 1769480 | tf_op jit(solution)/shard_map/ppermute | solution.py:29
  94.9 33.1 %all-to-all-start.2 = ((bf16[4,2,96,768]{3,2,1,0:T(8,128)(2,1)}), bf16[4,2,96,768]{3,2,1,0:T(8,128)(2,1)}, u32[]{:S(2)}, u32[]{:S(2)}) async-start(bf16[4,2,96,768]{3,2,1,0:T(8,128)(2,1)} %broadcast_in_dim.62), calls=%async_computation.2 | async-start | bytes 2359296 | tf_op jit(solution)/shard_map/all_to_all | solution.py:41
  99.5 28.5 %collective-permute-start.23 = (bf16[4,96,768]{2,1,0:T(8,128)(2,1)}, bf16[4,96,768]{2,1,0:T(8,128)(2,1)}, u32[]{:S(2)}, u32[]{:S(2)}) collective-permute-start(bf16[4,96,768]{2,1,0:T(8,128)(2,1)} %bitcast.33.refs_3_.refs_5_), channel_id=1, source_target_pairs={{0,1},{1,0},{2,3},{3,2},{4,5},{5,4},{6,7},{7,6},{8,9},{9,8},{10,11... | collective-permute-start | bytes 1769480 | tf_op jit(solution)/shard_map/ppermute | solution.py:37
  99.6 23.3 %collective-permute-start.19 = (bf16[2,98,768]{2,1,0:T(8,128)(2,1)}, bf16[2,98,768]{2,1,0:T(8,128)(2,1)}, u32[]{:S(2)}, u32[]{:S(2)}) collective-permute-start(bf16[2,98,768]{2,1,0:T(8,128)(2,1)} %bitcast.116), channel_id=1, source_target_pairs={{0,4},{4,0},{1,5},{5,1},{2,6},{6,2},{3,7},{7,3},{8,12},{12,8},{9,1... | collective-permute-start | bytes 903176 | tf_op jit(solution)/shard_map/ppermute | solution.py:29
  101.2 22.2 %collective-permute-start.20 = (bf16[2,98,768]{2,1,0:T(8,128)(2,1)}, bf16[2,98,768]{2,1,0:T(8,128)(2,1)}, u32[]{:S(2)}, u32[]{:S(2)}) collective-permute-start(bf16[2,98,768]{2,1,0:T(8,128)(2,1)} %bitcast.115), channel_id=1, source_target_pairs={{0,6},{2,4},{4,2},{6,0},{1,7},{3,5},{5,3},{7,1},{8,14},{10,12},{12... | collective-permute-start | bytes 903176 | tf_op jit(solution)/shard_map/ppermute | solution.py:33
  101.8 26.9 %collective-permute-start.24 = (bf16[4,96,768]{2,1,0:T(8,128)(2,1)}, bf16[4,96,768]{2,1,0:T(8,128)(2,1)}, u32[]{:S(2)}, u32[]{:S(2)}) collective-permute-start(bf16[4,96,768]{2,1,0:T(8,128)(2,1)} %collective-permute-done.15.refs_4_.refs_6_), channel_id=1, source_target_pairs={{0,1},{1,0},{2,3},{3,2},{4,5},{5,4},{6,7},{7,6},{8,9},{9,8},{10,11... | collective-permute-start | bytes 1769480 | tf_op jit(solution)/shard_map/ppermute | solution.py:37
  106.1 24.1 %collective-permute-start.25 = (bf16[4,96,768]{2,1,0:T(8,128)(2,1)}, bf16[4,96,768]{2,1,0:T(8,128)(2,1)}, u32[]{:S(2)}, u32[]{:S(2)}) collective-permute-start(bf16[4,96,768]{2,1,0:T(8,128)(2,1)} %collective-permute-done.16.refs_5_.refs_7_), channel_id=1, source_target_pairs={{0,1},{1,0},{2,3},{3,2},{4,5},{5,4},{6,7},{7,6},{8,9},{9,8},{10,11... | collective-permute-start | bytes 1769480 | tf_op jit(solution)/shard_map/ppermute | solution.py:37
  128.1 31.0 %collective-permute-start.28 = (bf16[8,96,768]{2,1,0:T(8,128)(2,1)}, bf16[8,96,768]{2,1,0:T(8,128)(2,1)}, u32[]{:S(2)}, u32[]{:S(2)}) collective-permute-start(bf16[8,96,768]{2,1,0:T(8,128)(2,1)} %bitcast.43.refs_7_), channel_id=1, source_target_pairs={{0,2},{2,0},{1,3},{3,1},{4,6},{6,4},{5,7},{7,5},{8,10},{10,8},{9,1... | collective-permute-start | bytes 3538952 | tf_op jit(solution)/shard_map/ppermute | solution.py:25
  128.7 30.4 %collective-permute-start.29 = (bf16[8,96,768]{2,1,0:T(8,128)(2,1)}, bf16[8,96,768]{2,1,0:T(8,128)(2,1)}, u32[]{:S(2)}, u32[]{:S(2)}) collective-permute-start(bf16[8,96,768]{2,1,0:T(8,128)(2,1)} %bitcast.43.refs_7_), channel_id=1, source_target_pairs={{0,4},{4,0},{1,5},{5,1},{2,6},{6,2},{3,7},{7,3},{8,12},{12,8},{9,1... | collective-permute-start | bytes 3538952 | tf_op jit(solution)/shard_map/ppermute | solution.py:29
  163.8 15.2 %collective-permute-start.34 = (bf16[8,96,768]{2,1,0:T(8,128)(2,1)}, bf16[8,96,768]{2,1,0:T(8,128)(2,1)}, u32[]{:S(2)}, u32[]{:S(2)}) collective-permute-start(bf16[8,96,768]{2,1,0:T(8,128)(2,1)} %collective-permute-done.29.refs_9_), channel_id=1, source_target_pairs={{0,1},{1,0},{2,3},{3,2},{4,5},{5,4},{6,7},{7,6},{8,9},{9,8},{10,11... | collective-permute-start | bytes 3538952 | tf_op jit(solution)/shard_map/ppermute | solution.py:37
  225.7 32.7 %collective-permute-start.40 = (bf16[32,96,768]{2,1,0:T(8,128)(2,1)}, bf16[32,96,768]{2,1,0:T(8,128)(2,1)}, u32[]{:S(2)}, u32[]{:S(2)}) collective-permute-start(bf16[32,96,768]{2,1,0:T(8,128)(2,1)} %get-tuple-element.189), channel_id=1, source_target_pairs={{0,1},{1,0},{2,3},{3,2},{4,5},{5,4},{6,7},{7,6},{8,9},{9,8},{10,11... | collective-permute-start | bytes 14155784 | tf_op jit(solution)/shard_map/ppermute | solution.py:37
  225.9 40.2 %collective-permute-start.37 = (bf16[2,98,768]{2,1,0:T(8,128)(2,1)}, bf16[2,98,768]{2,1,0:T(8,128)(2,1)}, u32[]{:S(2)}, u32[]{:S(2)}) collective-permute-start(bf16[2,98,768]{2,1,0:T(8,128)(2,1)} %get-tuple-element.177), channel_id=1, source_target_pairs={{0,2},{2,0},{1,3},{3,1},{4,6},{6,4},{5,7},{7,5},{8,10},{10,8},{9,1... | collective-permute-start | bytes 903176 | tf_op jit(solution)/shard_map/ppermute | solution.py:25
  227.3 38.8 %collective-permute-start.38 = (bf16[2,98,768]{2,1,0:T(8,128)(2,1)}, bf16[2,98,768]{2,1,0:T(8,128)(2,1)}, u32[]{:S(2)}, u32[]{:S(2)}) collective-permute-start(bf16[2,98,768]{2,1,0:T(8,128)(2,1)} %get-tuple-element.178), channel_id=1, source_target_pairs={{0,4},{4,0},{1,5},{5,1},{2,6},{6,2},{3,7},{7,3},{8,12},{12,8},{9,1... | collective-permute-start | bytes 903176 | tf_op jit(solution)/shard_map/ppermute | solution.py:29
  228.8 37.3 %collective-permute-start.39 = (bf16[2,98,768]{2,1,0:T(8,128)(2,1)}, bf16[2,98,768]{2,1,0:T(8,128)(2,1)}, u32[]{:S(2)}, u32[]{:S(2)}) collective-permute-start(bf16[2,98,768]{2,1,0:T(8,128)(2,1)} %get-tuple-element.179), channel_id=1, source_target_pairs={{0,6},{2,4},{4,2},{6,0},{1,7},{3,5},{5,3},{7,1},{8,14},{10,12},{12... | collective-permute-start | bytes 903176 | tf_op jit(solution)/shard_map/ppermute | solution.py:33
  263.1 17.0 %collective-permute-start.41 = (bf16[4,96,768]{2,1,0:T(8,128)(2,1)}, bf16[4,96,768]{2,1,0:T(8,128)(2,1)}, u32[]{:S(2)}, u32[]{:S(2)}) collective-permute-start(bf16[4,96,768]{2,1,0:T(8,128)(2,1)} %get-tuple-element.191), channel_id=1, source_target_pairs={{0,4},{4,0},{1,5},{5,1},{2,6},{6,2},{3,7},{7,3},{8,12},{12,8},{9,1... | collective-permute-start | bytes 1769480 | tf_op jit(solution)/shard_map/ppermute | solution.py:29
  264.7 15.4 %collective-permute-start.42 = (bf16[4,96,768]{2,1,0:T(8,128)(2,1)}, bf16[4,96,768]{2,1,0:T(8,128)(2,1)}, u32[]{:S(2)}, u32[]{:S(2)}) collective-permute-start(bf16[4,96,768]{2,1,0:T(8,128)(2,1)} %get-tuple-element.192), channel_id=1, source_target_pairs={{0,2},{2,0},{1,3},{3,1},{4,6},{6,4},{5,7},{7,5},{8,10},{10,8},{9,1... | collective-permute-start | bytes 1769480 | tf_op jit(solution)/shard_map/ppermute | solution.py:25
  280.1 21.7 %collective-permute-start.43 = (bf16[16,96,768]{2,1,0:T(8,128)(2,1)}, bf16[16,96,768]{2,1,0:T(8,128)(2,1)}, u32[]{:S(2)}, u32[]{:S(2)}) collective-permute-start(bf16[16,96,768]{2,1,0:T(8,128)(2,1)} %get-tuple-element.202), channel_id=1, source_target_pairs={{0,1},{1,0},{2,3},{3,2},{4,5},{5,4},{6,7},{7,6},{8,9},{9,8},{10,11... | collective-permute-start | bytes 7077896 | tf_op jit(solution)/shard_map/ppermute | solution.py:37
  286.2 44.9 %collective-permute-start.48 = (bf16[8,96,768]{2,1,0:T(8,128)(2,1)}, bf16[8,96,768]{2,1,0:T(8,128)(2,1)}, u32[]{:S(2)}, u32[]{:S(2)}) collective-permute-start(bf16[8,96,768]{2,1,0:T(8,128)(2,1)} %get-tuple-element.198), channel_id=1, source_target_pairs={{0,2},{2,0},{1,3},{3,1},{4,6},{6,4},{5,7},{7,5},{8,10},{10,8},{9,1... | collective-permute-start | bytes 3538952 | tf_op jit(solution)/shard_map/ppermute | solution.py:25
  286.9 44.2 %collective-permute-start.49 = (bf16[8,96,768]{2,1,0:T(8,128)(2,1)}, bf16[8,96,768]{2,1,0:T(8,128)(2,1)}, u32[]{:S(2)}, u32[]{:S(2)}) collective-permute-start(bf16[8,96,768]{2,1,0:T(8,128)(2,1)} %get-tuple-element.199), channel_id=1, source_target_pairs={{0,4},{4,0},{1,5},{5,1},{2,6},{6,2},{3,7},{7,3},{8,12},{12,8},{9,1... | collective-permute-start | bytes 3538952 | tf_op jit(solution)/shard_map/ppermute | solution.py:29
  305.4 25.7 %collective-permute-start.44 = (bf16[2,96,768]{2,1,0:T(8,128)(2,1)}, bf16[2,96,768]{2,1,0:T(8,128)(2,1)}, u32[]{:S(2)}, u32[]{:S(2)}) collective-permute-start(bf16[2,96,768]{2,1,0:T(8,128)(2,1)} %get-tuple-element.204), channel_id=1, source_target_pairs={{0,4},{4,0},{1,5},{5,1},{2,6},{6,2},{3,7},{7,3},{8,12},{12,8},{9,1... | collective-permute-start | bytes 884744 | tf_op jit(solution)/shard_map/ppermute | solution.py:29
  306.9 24.2 %collective-permute-start.45 = (bf16[2,96,768]{2,1,0:T(8,128)(2,1)}, bf16[2,96,768]{2,1,0:T(8,128)(2,1)}, u32[]{:S(2)}, u32[]{:S(2)}) collective-permute-start(bf16[2,96,768]{2,1,0:T(8,128)(2,1)} %get-tuple-element.205), channel_id=1, source_target_pairs={{0,2},{2,0},{1,3},{3,1},{4,6},{6,4},{5,7},{7,5},{8,10},{10,8},{9,1... | collective-permute-start | bytes 884744 | tf_op jit(solution)/shard_map/ppermute | solution.py:25
  337.1 34.2 %all-to-all-start.3 = ((bf16[4,2,96,768]{3,2,1,0:T(8,128)(2,1)}), bf16[4,2,96,768]{3,2,1,0:T(8,128)(2,1)}, u32[]{:S(2)}, u32[]{:S(2)}) async-start(bf16[4,2,96,768]{3,2,1,0:T(8,128)(2,1)} %bitcast.44), calls=%async_computation.3 | async-start | bytes 2359296 | tf_op jit(solution)/shard_map/all_to_all | solution.py:41
  344.5 18.8 %collective-permute-start.46 = (bf16[4,96,768]{2,1,0:T(8,128)(2,1)}, bf16[4,96,768]{2,1,0:T(8,128)(2,1)}, u32[]{:S(2)}, u32[]{:S(2)}) collective-permute-start(bf16[4,96,768]{2,1,0:T(8,128)(2,1)} %get-tuple-element.211), channel_id=1, source_target_pairs={{0,2},{2,0},{1,3},{3,1},{4,6},{6,4},{5,7},{7,5},{8,10},{10,8},{9,1... | collective-permute-start | bytes 1769480 | tf_op jit(solution)/shard_map/ppermute | solution.py:25
  345.2 18.1 %collective-permute-start.47 = (bf16[4,96,768]{2,1,0:T(8,128)(2,1)}, bf16[4,96,768]{2,1,0:T(8,128)(2,1)}, u32[]{:S(2)}, u32[]{:S(2)}) collective-permute-start(bf16[4,96,768]{2,1,0:T(8,128)(2,1)} %get-tuple-element.212), channel_id=1, source_target_pairs={{0,4},{4,0},{1,5},{5,1},{2,6},{6,2},{3,7},{7,3},{8,12},{12,8},{9,1... | collective-permute-start | bytes 1769480 | tf_op jit(solution)/shard_map/ppermute | solution.py:29
  371.3 16.4 %collective-permute-start.51 = (bf16[16,96,768]{2,1,0:T(8,128)(2,1)}, bf16[16,96,768]{2,1,0:T(8,128)(2,1)S(1)}, u32[]{:S(2)}, u32[]{:S(2)}) collective-permute-start(bf16[16,96,768]{2,1,0:T(8,128)(2,1)} %get-tuple-element.226), channel_id=1, source_target_pairs={{0,1},{1,0},{2,3},{3,2},{4,5},{5,4},{6,7},{7,6},{8,9},{9,8},{10,11... | collective-permute-start | bytes 7077896 | tf_op jit(solution)/shard_map/ppermute | solution.py:37
  381.1 23.5 %all-to-all-start.4 = ((bf16[4,1,96,768]{3,2,1,0:T(8,128)(2,1)}), bf16[4,1,96,768]{3,2,1,0:T(8,128)(2,1)}, u32[]{:S(2)}, u32[]{:S(2)}) async-start(bf16[4,1,96,768]{3,2,1,0:T(8,128)(2,1)} %bitcast.59), calls=%async_computation.4 | async-start | bytes 1179648 | tf_op jit(solution)/shard_map/all_to_all | solution.py:41
  389.4 18.8 %collective-permute-start.52 = (bf16[2,96,768]{2,1,0:T(8,128)(2,1)}, bf16[2,96,768]{2,1,0:T(8,128)(2,1)}, u32[]{:S(2)}, u32[]{:S(2)}) collective-permute-start(bf16[2,96,768]{2,1,0:T(8,128)(2,1)} %get-tuple-element.228), channel_id=1, source_target_pairs={{0,4},{4,0},{1,5},{5,1},{2,6},{6,2},{3,7},{7,3},{8,12},{12,8},{9,1... | collective-permute-start | bytes 884744 | tf_op jit(solution)/shard_map/ppermute | solution.py:29
  389.9 18.4 %collective-permute-start.53 = (bf16[2,96,768]{2,1,0:T(8,128)(2,1)}, bf16[2,96,768]{2,1,0:T(8,128)(2,1)}, u32[]{:S(2)}, u32[]{:S(2)}) collective-permute-start(bf16[2,96,768]{2,1,0:T(8,128)(2,1)} %get-tuple-element.229), channel_id=1, source_target_pairs={{0,2},{2,0},{1,3},{3,1},{4,6},{6,4},{5,7},{7,5},{8,10},{10,8},{9,1... | collective-permute-start | bytes 884744 | tf_op jit(solution)/shard_map/ppermute | solution.py:25
  411.3 15.2 %collective-permute-start.54 = (bf16[4,96,768]{2,1,0:T(8,128)(2,1)S(1)}, bf16[4,96,768]{2,1,0:T(8,128)(2,1)S(1)}, u32[]{:S(2)}, u32[]{:S(2)}) collective-permute-start(bf16[4,96,768]{2,1,0:T(8,128)(2,1)S(1)} %get-tuple-element.243), channel_id=1, source_target_pairs={{0,2},{2,0},{1,3},{3,1},{4,6},{6,4},{5,7},{7,5},{8,10},{10,8},{9,1... | collective-permute-start | bytes 1769480 | tf_op jit(solution)/shard_map/ppermute | solution.py:25
  412.7 14.9 %collective-permute-start.55 = (bf16[4,96,768]{2,1,0:T(8,128)(2,1)S(1)}, bf16[4,96,768]{2,1,0:T(8,128)(2,1)S(1)}, u32[]{:S(2)}, u32[]{:S(2)}) collective-permute-start(bf16[4,96,768]{2,1,0:T(8,128)(2,1)S(1)} %get-tuple-element.244), channel_id=1, source_target_pairs={{0,4},{4,0},{1,5},{5,1},{2,6},{6,2},{3,7},{7,3},{8,12},{12,8},{9,1... | collective-permute-start | bytes 1769480 | tf_op jit(solution)/shard_map/ppermute | solution.py:29
  427.9 20.1 %collective-permute-start.59 = (bf16[1,96,768]{2,1,0:T(8,128)(2,1)S(1)}, bf16[1,96,768]{2,1,0:T(8,128)(2,1)}, u32[]{:S(2)}, u32[]{:S(2)}) collective-permute-start(bf16[1,96,768]{2,1,0:T(8,128)(2,1)S(1)} %get-tuple-element.247), channel_id=1, source_target_pairs={{0,8},{8,16},{16,24},{24,0},{1,9},{9,17},{17,25},{25,1},{2,10},{10... | collective-permute-start | bytes 442376 | tf_op jit(solution)/shard_map/ppermute | solution.py:172
  429.7 19.9 %collective-permute-start.60 = (bf16[1,96,768]{2,1,0:T(8,128)(2,1)S(1)}, bf16[1,96,768]{2,1,0:T(8,128)(2,1)}, u32[]{:S(2)}, u32[]{:S(2)}) collective-permute-start(bf16[1,96,768]{2,1,0:T(8,128)(2,1)S(1)} %get-tuple-element.248), channel_id=1, source_target_pairs={{0,16},{8,24},{16,0},{24,8},{1,17},{9,25},{17,1},{25,9},{2,18},{10... | collective-permute-start | bytes 442376 | tf_op jit(solution)/shard_map/ppermute | solution.py:172
  432.0 17.5 %collective-permute-start.61 = (bf16[1,96,768]{2,1,0:T(8,128)(2,1)S(1)}, bf16[1,96,768]{2,1,0:T(8,128)(2,1)}, u32[]{:S(2)}, u32[]{:S(2)}) collective-permute-start(bf16[1,96,768]{2,1,0:T(8,128)(2,1)S(1)} %get-tuple-element.249), channel_id=1, source_target_pairs={{0,24},{8,0},{16,8},{24,16},{1,25},{9,1},{17,9},{25,17},{2,26},{10... | collective-permute-start | bytes 442376 | tf_op jit(solution)/shard_map/ppermute | solution.py:172
  438.2 15.8 %collective-permute-start.56 = (bf16[2,98,768]{2,1,0:T(8,128)(2,1)}, bf16[2,98,768]{2,1,0:T(8,128)(2,1)}, u32[]{:S(2)}, u32[]{:S(2)}) collective-permute-start(bf16[2,98,768]{2,1,0:T(8,128)(2,1)} %get-tuple-element.251), channel_id=1, source_target_pairs={{0,2},{2,0},{1,3},{3,1},{4,6},{6,4},{5,7},{7,5},{8,10},{10,8},{9,1... | collective-permute-start | bytes 903176 | tf_op jit(solution)/shard_map/ppermute | solution.py:25
  440.0 15.3 %collective-permute-start.57 = (bf16[2,98,768]{2,1,0:T(8,128)(2,1)}, bf16[2,98,768]{2,1,0:T(8,128)(2,1)}, u32[]{:S(2)}, u32[]{:S(2)}) collective-permute-start(bf16[2,98,768]{2,1,0:T(8,128)(2,1)} %get-tuple-element.252), channel_id=1, source_target_pairs={{0,4},{4,0},{1,5},{5,1},{2,6},{6,2},{3,7},{7,3},{8,12},{12,8},{9,1... | collective-permute-start | bytes 903176 | tf_op jit(solution)/shard_map/ppermute | solution.py:29
  (69 other events, 521.9 us)
where the time goes:
time: 469 us; the launch traced here: 462 us
  Pallas kernels  235 us (50%)
  waiting for transfers between devices  81.6 us (17%)
  starting transfers between devices  78.6 us (17%)
  local copies, waits for them, and re-layouts  53.6 us (11%)
  other arithmetic  10.3 us (2%)
    pallas_call x10, Pallas kernels, run(): pl.pallas_call(kernel, name=name, in_specs=[space[s] for _, s in ins], ou...  216 us
    ppermute x16, waiting for transfers between devices, over_x(): return lax.ppermute(v, 'x', FLIP)  32.2 us
    ppermute x16, waiting for transfers between devices, over_y(): return lax.ppermute(v, 'ctx', FLIP)  23.2 us
    unnamed x117, local copies, waits for them, and re-layouts  20.9 us
    pallas_call x9, Pallas kernels, block_sums(): pl.pallas_call(kernel, name=name, grid=(1,), in_specs=[spec(blocks, index...  19.5 us
    ppermute x16, starting transfers between devices, over_x(): return lax.ppermute(v, 'x', FLIP)  17.6 us
    all_to_all x4, starting transfers between devices, over_z(): return lax.all_to_all(v, 'shard', split_axis=0, concat_axis=0, tiled=True)  17.6 us
    ppermute x16, starting transfers between devices, over_y(): return lax.ppermute(v, 'ctx', FLIP)  16.9 us
  transfers between devices with their start and end apart: 68, of which 18 were waited for; matrix products, arithmetic and copies ran while one was open for 9% of the time, Pallas kernels for 41%

commit v1 on v0

--- a/solution.py
+++ b/solution.py
@@ -52,25 +52,18 @@
 
 
 class Gather:
-    def __init__(self, owns, n, shifts=False):
-        self.own, self.n, self.shifts = jnp.stack(owns), n, shifts
+    def __init__(self, owns, n):
+        own = jnp.stack(owns)
+        self.n = n
+        self.spread = lax.optimization_barrier(jnp.broadcast_to(own[None], (n,) + own.shape))
 
     def stage_z(self, *deps):
-        own, n = self.own, self.n
-        if self.shifts:
-            own = after(own, *deps)
-            self.z = [own] + [
-                lax.ppermute(own, "shard", [((i + d) % n, i) for i in range(n)])
-                for d in range(1, n)
-            ]
-            return self.z[1:]
-        spread = lax.optimization_barrier(jnp.broadcast_to(own[None], (n,) + own.shape))
-        self.z = [over_z(after(spread, *deps))]
+        self.z = [over_z(after(self.spread, *deps))]
         return self.z
 
     def stage_xy(self, *deps):
         z = after(tuple(self.z), *deps)
-        self.blk = jnp.concatenate([v.reshape((-1,) + v.shape[-2:]) for v in z], axis=0)
+        self.blk = z[0].reshape((-1,) + z[0].shape[-2:])
         self.x, self.y = over_x(self.blk), over_y(self.blk)
         self.sent = [self.blk]
         return [self.x, self.y]
@@ -115,7 +108,7 @@
         in_specs=[spec(blocks, index) for _, blocks, index, _ in terms],
         out_specs=[pl.BlockSpec((count,) + tail, lambda i: (0, 0, 0)) for _, count, _ in outs],
         out_shape=[jax.ShapeDtypeStruct((count,) + tail, dt) for _, count, dt in outs],
-        compiler_params=pltpu.CompilerParams(vmem_limit_bytes=24 * 2**20),
+        compiler_params=pltpu.CompilerParams(vmem_limit_bytes=VMEM_LIMIT),
         cost_estimate=pl.CostEstimate(flops=10**8, bytes_accessed=10**5, transcendentals=0),
     )(*[t[0] for t in terms])
 
@@ -177,15 +170,25 @@
             self.name + "_z", [([(v, self.size, 0, 0) for v in all_four], self.size, B16)]
         )
         v = self.sent[0]
-        self.z = over_z(v.reshape((self.n, self.size // self.n) + v.shape[1:]))
-        return [self.z]
+        self.z = [over_z(v.reshape((self.n, self.size // self.n) + v.shape[1:]))]
+        return self.z
 
     def results(self, *deps):
+        z = after(tuple(self.z), *deps)
         if self.shifts:
-            z = after(tuple(self.z), *deps)
             return [functools.reduce(lambda a, b: a + b, [v[0].astype(F32) for v in z])]
-        z = jnp.sum(after(self.z, *deps).astype(F32), axis=0)
+        z = jnp.sum(z[0].astype(F32), axis=0)
         return [z[k] for k in range(z.shape[0])]
+
+
+def joint_z(parts, n, name):
+    terms, count = [], len(parts)
+    for i, (r, k) in enumerate(parts):
+        chunks = r.size // n
+        for z in range(n):
+            terms += [(v, 1, z * chunks + k, z * count + i) for v in (r.near, r.got, *r.xy)]
+    (v,) = block_sums(name, [(terms, n * count, B16)])
+    return v.reshape((n, count) + v.shape[1:])
 
 
 EVERY = ("x", "core", "shard", "ctx")
@@ -201,8 +204,9 @@
 
 class GatherWhole:
     sent = ()
-
-    def __init__(self, owns, n, shifts=False):
+    spread = ()
+
+    def __init__(self, owns, n):
         d = owns[0].shape[1]
         self.out = [gather_whole(v).reshape(4, d, d) for v in owns]
 
@@ -279,7 +283,7 @@
         moves = list(zip(bufs, w_refs))
     else:
         x, y, c = meta[0], meta[1], meta[2]
-        rows = bufs[0].shape[1]
+        rows = w_refs[0].shape[1] // (2 * n)
         for dc in range(2):
             first = 0
             for k, (dx, dy, blocks) in enumerate(layout(len(w_refs), n)):
@@ -288,7 +292,7 @@
                     if shifts:
                         z = lax.rem(meta[3] + z, n)
                     row = pl.multiple_of((z * 2 + (y ^ dy)) * rows, rows)
-                    piece = bufs[dc].at[first + i] if back else bufs[dc * 5 + k].at[i]
+                    piece = bufs[dc].at[first + i] if back else bufs[dc * 5 + k].at[i, 0:rows, :]
                     moves.append((piece, w_refs[chunk].at[tp, pl.ds(row, rows), :]))
                 first += len(blocks)
     if back:
@@ -327,40 +331,36 @@
             blk[f] = src[row : row + places, :].astype(blk.dtype)
 
 
-def project_heads(normed, w_ref, q_out, kv_out, rows, step):
+def project_heads(normed, w_ref, q_out, kv_out):
     @pl.loop(0, 2)
     def _(u):
-        @pl.loop(0, rows // step)
-        def _(r):
-            at = pl.ds(pl.multiple_of(r * step, step), step)
-            xn = normed[at, :]
-            thirds = []
-            for t in (2 * u, 2 * u + 1):
-                y = dot(xn, w_ref[t, :, 0:512]).astype(B16)
-                q_out[t, at, :] = y[:, 0:128]
-                kv_out[t, at, :] = y[:, 128:256]
-                kv_out[6 + t, at, :] = y[:, 256:384]
-                thirds.append((y[:, 384:512], dot(xn, w_ref[t, :, 640:768]).astype(B16)))
-            (a3, a5), (b3, b5) = thirds
-            low = low_lanes(a3.shape)
-            q_out[4 + u, at, :] = jnp.where(low, a3, b3)
-            kv_out[4 + u, at, :] = swap_halves(jnp.where(low, b3, a3))
-            kv_out[10 + u, at, :] = swap_halves(jnp.where(low, b5, a5))
+        thirds = []
+        for t in (2 * u, 2 * u + 1):
+            xn = normed[...]
+            y = dot(xn, w_ref[t, :, 0:512]).astype(B16)
+            q_out[t] = y[:, 0:128]
+            kv_out[t] = y[:, 128:256]
+            kv_out[6 + t] = y[:, 256:384]
+            thirds.append((y[:, 384:512], dot(xn, w_ref[t, :, 640:768]).astype(B16)))
+        (a3, a5), (b3, b5) = thirds
+        low = low_lanes(a3.shape)
+        q_out[4 + u] = jnp.where(low, a3, b3)
+        kv_out[4 + u] = swap_halves(jnp.where(low, b3, a3))
+        kv_out[10 + u] = swap_halves(jnp.where(low, b5, a5))
 
 
 def third_head(v, t):
     return keep_low(v) if t % 2 == 0 else keep_high(v)
 
 
-def project_out(mixed, w_ref, stream, bias, out, rows, step):
-    @pl.loop(0, rows // step)
-    def _(r):
-        at = pl.ds(pl.multiple_of(r * step, step), step)
-        acc = stream[at, :] + bias
+def project_out(mixed, w_ref, stream, bias, out):
+    for n in range(3):
+        cols = slice(256 * n, 256 * n + 256)
+        acc = stream[:, cols] + bias[:, cols]
         for t in range(4):
-            m = jnp.concatenate([mixed[t, at, :], third_head(mixed[4 + t // 2, at, :], t)], axis=1)
-            acc = acc + dot_nt(m, w_ref[t, :, 512:768])
-        out[at, :] = acc
+            m = jnp.concatenate([mixed[t], third_head(mixed[4 + t // 2], t)], axis=1)
+            acc = acc + dot_nt(m, w_ref[t, cols, 512:768])
+        out[:, cols] = acc
 
 
 def run(kernel, name, ins, outs, scratch, micros):
@@ -387,6 +387,61 @@
     return pl.ds(pl.multiple_of(r * step, step), step)
 
 
+VECTORS = 9
+
+
+def norm_vectors(sz, meta, weights):
+    d, n, nw = sz["d"], sz["n"], len(weights)
+    count, rows = 8 * n, d // (2 * n)
+    per = d // count
+    hidden = VECTORS * per
+
+    def kernel(*refs):
+        meta, bufs = refs[0], refs[1 : 1 + nw]
+        out, shares, sems = refs[1 + nw :]
+        x, y, c = meta[0], meta[1], meta[2]
+        copies = []
+        for dc in range(2):
+            for k, (dx, dy, blocks) in enumerate(layout(1, n)):
+                tp = 2 * (x ^ dx) + (c ^ dc)
+                for i, (z, _) in enumerate(blocks):
+                    dev = (z * 2 + (y ^ dy)) * 4 + tp
+                    piece = bufs[dc * 5 + k].at[i, rows : rows + 8, :]
+                    copies.append(
+                        pltpu.make_async_copy(piece, shares.at[dev], sems.at[len(copies)])
+                    )
+        start_all(copies)
+        lane = lax.broadcasted_iota(jnp.int32, (128, d), 1)
+        row = lax.broadcasted_iota(jnp.int32, (128, d), 0)
+        one = ((lane % per == row) & (row < per)).astype(F32).astype(B16)
+        four = ((lane % (4 * per) == row) & (row < 4 * per)).astype(F32).astype(B16)
+        dev = lax.broadcasted_iota(jnp.int32, (count, d), 0)
+        lanes = lax.broadcasted_iota(jnp.int32, (count, d), 1)
+        mine = lanes // per == dev
+        ours = lanes // (4 * per) == dev % 8
+        wait_all(copies)
+        rows_in = shares[:, 0, :].astype(F32)
+        pad = jnp.zeros((count, 128), F32)
+        rows_in = jnp.concatenate([rows_in, pad], axis=1)
+
+        def spread(first, pick):
+            parts = [rows_in[:, o + first : o + first + 128].astype(B16) for o in (0, 384)]
+            return dot(parts[0], pick) + dot(parts[1], pick)
+
+        for v in range(VECTORS):
+            got = jnp.where(mine, spread(v * per, one), 0.0)
+            out[v : v + 1, :] = jnp.sum(got, axis=0, keepdims=True)
+        got = jnp.where(ours, spread(hidden, four), 0.0)
+        for t in range(4):
+            part = got[t * 8 : t * 8 + 8] if count == 32 else got
+            out[VECTORS + t : VECTORS + t + 1, :] = jnp.sum(part, axis=0, keepdims=True)
+
+    ins = [(meta, "s")] + [(w, "a") for w in weights]
+    outs = [((16, d), F32, "v")]
+    scratch = [pltpu.VMEM((count, 8, d), B16), copy_sems(sz, 1)]
+    return run(kernel, "norm_vectors", ins, outs, scratch, 2)[0]
+
+
 def time_qkv(sz, meta, vec, blocks, weights):
     rows, d = sz["rows"], sz["d"]
     nb, nw = len(blocks), len(weights)
@@ -395,7 +450,7 @@
         meta, vec = refs[0], refs[1]
         blks, bufs = refs[2 : 2 + nb], refs[2 + nb : 2 + nb + nw]
         x, normed, q, kv, w, sems = refs[2 + nb + nw :]
-        copies = weight_copies(meta, bufs, [w], sems, sz["n"], shifts=True)
+        copies = weight_copies(meta, bufs, [w], sems, sz["n"])
         start_all(copies)
         take_blocks(blks, x, sz["places"])
 
@@ -406,7 +461,7 @@
             normed[at, :] = (unit * vec[0:1, :] + vec[1:2, :]).astype(B16)
 
         wait_all(copies)
-        project_heads(normed, w, q, kv, rows, 416)
+        project_heads(normed, w, q, kv)
 
     ins = [(meta, "s"), (vec, "v")] + [(b, "v") for b in blocks] + [(w, "a") for w in weights]
     outs = [
@@ -459,7 +514,7 @@
         meta, vec, stream, q, kv, kvo = refs[:6]
         bufs = refs[6 : 6 + nw]
         mixed, out, prob, w, sums, spreads, acc, sems = refs[6 + nw :]
-        copies = weight_copies(meta, bufs, [w], sems, sz["n"], shifts=True)
+        copies = weight_copies(meta, bufs, [w], sems, sz["n"])
         start_all(copies)
         head_sums(sums)
         head_spreads(spreads)
@@ -497,7 +552,7 @@
         for j in range(6):
             mixed[j] = acc[:, 128 * j : 128 * j + 128].astype(B16)
         wait_all(copies)
-        project_out(mixed, w, stream, vec[2:3, :], out, rows, 416)
+        project_out(mixed, w, stream, vec[2:3, :], out)
 
     ins = [(meta, "s"), (vec, "v"), (stream, "v"), (q, "v"), (kv, "v"), (kvo, "v")]
     ins += [(w, "a") for w in weights]
@@ -516,14 +571,14 @@
     return lax.broadcasted_iota(jnp.int32, (208, 208), 0) % PAD < places
 
 
-def space_forward(sz, meta, vec, stream, weights):
-    rows, d, places = sz["rows"], sz["d"], sz["places"]
+def space_qkv(sz, meta, vec, stream, weights):
+    rows, d = sz["rows"], sz["d"]
     nw = len(weights)
 
     def kernel(*refs):
         meta, vec, stream = refs[:3]
         bufs = refs[3 : 3 + nw]
-        normed, q, kv, mixed, logs, out, w, sems = refs[3 + nw :]
+        normed, q, kv, w, sems = refs[3 + nw :]
         copies = weight_copies(meta, bufs, [w], sems, sz["n"])
         start_all(copies)
 
@@ -534,7 +589,24 @@
             normed[at, :] = (unit * vec[3:4, :] + vec[4:5, :]).astype(B16)
 
         wait_all(copies)
-        project_heads(normed, w, q, kv, rows, 416)
+        project_heads(normed, w, q, kv)
+
+    ins = [(meta, "s"), (vec, "v"), (stream, "v")] + [(w, "a") for w in weights]
+    outs = [((rows, d), B16, "v"), ((6, rows, 128), B16, "v"), ((12, rows, 128), B16, "v")]
+    scratch = [pltpu.VMEM((4, d, d), B16), copy_sems(sz, 1)]
+    return run(kernel, "space_qkv", ins, outs, scratch, 12)
+
+
+def space_mix(sz, meta, vec, stream, q, kv, weights):
+    rows, d, places = sz["rows"], sz["d"], sz["places"]
+    nw = len(weights)
+
+    def kernel(*refs):
+        meta, vec, stream, q, kv = refs[:5]
+        bufs = refs[5 : 5 + nw]
+        mixed, logs, out, w, sems = refs[5 + nw :]
+        copies = weight_copies(meta, bufs, [w], sems, sz["n"])
+        start_all(copies)
 
         @pl.loop(0, 6)
         def _(j):
@@ -554,19 +626,14 @@
                     o = part if o is None else o + part
                 mixed[j, at, :] = o.astype(B16)
 
-        project_out(mixed, w, stream, vec[5:6, :], out, rows, 416)
-
-    ins = [(meta, "s"), (vec, "v"), (stream, "v")] + [(w, "a") for w in weights]
-    outs = [
-        ((rows, d), B16, "v"),
-        ((6, rows, 128), B16, "v"),
-        ((12, rows, 128), B16, "v"),
-        ((6, rows, 128), B16, "v"),
-        ((24, 8, 208), F32, "v"),
-        ((rows, d), F32, "v"),
-    ]
+        wait_all(copies)
+        project_out(mixed, w, stream, vec[5:6, :], out)
+
+    ins = [(meta, "s"), (vec, "v"), (stream, "v"), (q, "v"), (kv, "v")]
+    ins += [(w, "a") for w in weights]
+    outs = [((6, rows, 128), B16, "v"), ((24, 8, 208), F32, "v"), ((rows, d), F32, "v")]
     scratch = [pltpu.VMEM((4, d, d), B16), copy_sems(sz, 1)]
-    return run(kernel, "space_forward", ins, outs, scratch, 29)
+    return run(kernel, "space_mix", ins, outs, scratch, 17)
 
 
 def gradient_outs(sz, chunks, fast):
@@ -574,11 +641,6 @@
     if not fast:
         return [((4, d, d), B16, "a")] * chunks
     return [((4 * chunks * n, d // (2 * n), d), B16, "a")] * 2
-
-
-def transpose_into(src, dst):
-    for j in range(src.shape[1] // 128):
-        dst[128 * j : 128 * j + 128, :] = src[:, 128 * j : 128 * j + 128].T
 
 
 def gelu_pair(x):
@@ -601,7 +663,7 @@
         res, refs = refs[:nb], refs[nb:]
         d2, vgrad = refs[0], refs[1]
         g_bufs, refs = refs[2 : 2 + ng], refs[2 + ng :]
-        w1, w2, dw1, dw2, dz, dzr, normed, normed_t, dzr_t, act, dpre, y, dn, sems = refs
+        w1, w2, dw1, dw2, dz, dzr, normed, act, dpre, y, dn, sems = refs
         copies = weight_copies(meta, bufs, [w1, w2], sems, sz["n"])
         start_all(copies)
         take_blocks(blks, dz, places)
@@ -618,30 +680,24 @@
             y[at, :] = stream[at, :] + vec[8:9, :]
             dn[at, :] = jnp.zeros_like(up)
 
-        transpose_into(normed, normed_t)
-        transpose_into(dzr, dzr_t)
         wait_all(copies)
 
         @pl.loop(0, 4)
         def _(t):
-            @pl.loop(0, rows // 208)
-            def _(r):
-                at = pl.ds(pl.multiple_of(r * 208, 208), 208)
-                pre = dot(normed[at, :], w1[t]) + vec[pl.ds(9 + t, 1), :]
+            thirds = [slice(256 * i, 256 * i + 256) for i in range(3)]
+            for cols in thirds:
+                pre = dot(normed[...], w1[t, :, cols]) + vec[pl.ds(9 + t, 1), cols]
                 a, slope = gelu_pair(pre)
-                a = a.astype(B16)
-                act[at, :] = a
-                y[at, :] += dot_nt(a, w2[t])
-                g = (dot(dzr[at, :], w2[t]) * slope).astype(B16)
-                dpre[at, :] = g
-                vgrad[pl.ds(4 + t, 1), :] += jnp.sum(g.astype(F32), axis=0, keepdims=True)
-                dn[at, :] += dot_nt(g, w1[t])
-
-            @pl.loop(0, d // 256)
-            def _(m):
-                at = pl.ds(pl.multiple_of(m * 256, 256), 256)
-                dw1[t, at, :] = dot(normed_t[at, :], dpre[...]).astype(B16)
-                dw2[t, at, :] = dot(dzr_t[at, :], act[...]).astype(B16)
+                act[:, cols] = a.astype(B16)
+                g = (dot(dzr[...], w2[t, :, cols]) * slope).astype(B16)
+                dpre[:, cols] = g
+                vgrad[pl.ds(4 + t, 1), cols] += jnp.sum(g.astype(F32), axis=0, keepdims=True)
+            for cols in thirds:
+                y[:, cols] += dot_nt(act[...], w2[t, cols, :])
+                dn[:, cols] += dot_nt(dpre[...], w1[t, cols, :])
+            for cols in thirds:
+                dw1[t, :, cols] = dot_tn(normed[...], dpre[:, cols]).astype(B16)
+                dw2[t, :, cols] = dot_tn(dzr[...], act[:, cols]).astype(B16)
 
         back = weight_copies(meta, g_bufs, [dw1, dw2], sems, sz["n"], back=True)
         start_all(back)
@@ -663,25 +719,20 @@
     outs += g_outs
     scratch = [pltpu.VMEM((4, d, d), B16)] * 4
     scratch += [pltpu.VMEM((rows, d), F32), pltpu.VMEM((rows, d), B16), pltpu.VMEM((rows, d), B16)]
-    scratch += [pltpu.VMEM((d, rows), B16)] * 2 + [pltpu.VMEM((rows, d), B16)] * 2
-    scratch += [pltpu.VMEM((rows, d), F32)] * 2
+    scratch += [pltpu.VMEM((rows, d), B16)] * 2 + [pltpu.VMEM((rows, d), F32)] * 2
     scratch += [copy_sems(sz, 2)]
     r = run(kernel, "feed_forward", ins, outs, scratch, 47)
     return r[:nb], r[nb], r[nb + 1], r[nb + 2 :]
 
 
-def mixed_slopes(up, w_ref, dm, rows, step):
-    @pl.loop(0, 2)
-    def _(u):
-        @pl.loop(0, rows // step)
-        def _(r):
-            at = pl.ds(pl.multiple_of(r * step, step), step)
-            thirds = []
-            for t in (2 * u, 2 * u + 1):
-                v = dot(up[at, :], w_ref[t, :, 512:768]).astype(B16)
-                dm[t, at, :] = v[:, 0:128]
-                thirds.append(v[:, 128:256])
-            dm[4 + u, at, :] = jnp.where(low_lanes(thirds[0].shape), *thirds)
+def mixed_slopes(up, w_ref, dm):
+    for u in range(2):
+        thirds = []
+        for t in (2 * u, 2 * u + 1):
+            v = dot(up[...], w_ref[t, :, 512:768]).astype(B16)
+            dm[t] = v[:, 0:128]
+            thirds.append(v[:, 128:256])
+        dm[4 + u] = jnp.where(low_lanes(thirds[0].shape), *thirds)
 
 
 def place_third(dq, dk, dv, dy, u, at):
@@ -693,31 +744,28 @@
     dy[2 * u + 1, at, 512:640] = keep_low(v)
 
 
-def head_gradients(dw, normed_t, up_t, dy, mixed, d):
+def head_gradients(dw, normed, up, dy, mixed):
     @pl.loop(0, 2)
     def _(u):
-        @pl.loop(0, d // 256)
-        def _(m):
-            at = pl.ds(pl.multiple_of(m * 256, 256), 256)
-            nt, ut = normed_t[at, :], up_t[at, :]
-            for odd in range(2):
-                t = 2 * u + odd
-                g = dot(nt, dy[t])
-                dw[t, at, 0:512] = g[:, 0:512].astype(B16)
-                m2 = jnp.concatenate([mixed[t], third_head(mixed[4 + u], odd)], axis=1)
-                out = dot(ut, m2)
-                dw[t, at, 512:640] = out[:, 0:128].astype(B16)
-                dw[t, at, 640:768] = (out[:, 128:256] + g[:, 512:640]).astype(B16)
-
-
-def norm_slopes(at, dy, w_ref):
-    up = None
-    for t in range(4):
-        part = dot_nt(dy[t, at, 0:512], w_ref[t, :, 0:512]) + dot_nt(
-            dy[t, at, 512:640], w_ref[t, :, 640:768]
-        )
-        up = part if up is None else up + part
-    return up
+        for odd in range(2):
+            t = 2 * u + odd
+            dw[t, :, 0:512] = dot_tn(normed[...], dy[t, :, 0:512]).astype(B16)
+            m2 = jnp.concatenate([mixed[t], third_head(mixed[4 + u], odd)], axis=1)
+            out = dot_tn(up[...], m2)
+            dw[t, :, 512:640] = out[:, 0:128].astype(B16)
+            third = dot_tn(normed[...], dy[t, :, 512:640])
+            dw[t, :, 640:768] = (out[:, 128:256] + third).astype(B16)
+
+
+def norm_slopes(dy, w_ref, out):
+    for n in range(3):
+        cols = slice(256 * n, 256 * n + 256)
+        acc = None
+        for t in range(4):
+            part = dot_nt(dy[t, :, 0:512], w_ref[t, cols, 0:512])
+            part = part + dot_nt(dy[t, :, 512:640], w_ref[t, cols, 640:768])
+            acc = part if acc is None else acc + part
+        out[:, cols] = acc
 
 
 def space_backward_scores(sz, meta, d2, q, kv, logs, weights):
@@ -736,7 +784,7 @@
             up[row_slices(r), :] = d2[row_slices(r), :].astype(B16)
 
         wait_all(copies)
-        mixed_slopes(up, w, dm, rows, 416)
+        mixed_slopes(up, w, dm)
 
         def slopes(j, at, f):
             qj, kj, vj, mj = q[j, at, :], kv[j, at, :], kv[6 + j, at, :], dm[j, at, :]
@@ -786,7 +834,7 @@
         meta, up, normed, mixed = refs[:4]
         given, refs = refs[4 : 4 + len(slopes)], refs[4 + len(slopes) :]
         dy = refs[0] if join else given[0]
-        g_bufs, (dw, up_t, normed_t, sems) = refs[1 if join else 0 : -4], refs[-4:]
+        g_bufs, (dw, sems) = refs[1 if join else 0 : -2], refs[-2:]
         if join:
             dq, dkv, got = given
 
@@ -803,17 +851,14 @@
                 for u in range(2):
                     place_third(dq[4 + u, at, :], both(4 + u, at), both(10 + u, at), dy, u, at)
 
-        transpose_into(normed, normed_t)
-        transpose_into(up, up_t)
-        head_gradients(dw, normed_t, up_t, dy, mixed, d)
+        head_gradients(dw, normed, up, dy, mixed)
         back = weight_copies(meta, g_bufs, [dw], sems, sz["n"], back=True, shifts=join)
         start_all(back)
         wait_all(back)
 
     ins = [(meta, "s")] + [(v, "v") for v in (up, normed, mixed, *slopes)]
     outs = ([((4, rows, 640), B16, "v")] if join else []) + g_outs
-    scratch = [pltpu.VMEM((4, d, d), B16)] + [pltpu.VMEM((d, rows), B16)] * 2
-    scratch += [copy_sems(sz, 1)]
+    scratch = [pltpu.VMEM((4, d, d), B16), copy_sems(sz, 1)]
     return run(kernel, name, ins, outs, scratch, 14)
 
 
@@ -824,22 +869,23 @@
     def kernel(*refs):
         meta, vec, up, stream, dy = refs[:5]
         bufs, refs = refs[5 : 5 + nw], refs[5 + nw :]
-        outs, vgrad, w, sems = refs[:-3], refs[-3], refs[-2], refs[-1]
+        w, dn, sems = refs[-3:]
         if blocks:
-            outs, vgrad, dx, w, sems = refs[:4], refs[4], refs[5], refs[6], refs[7]
+            outs, vgrad, dx = refs[:4], refs[4], refs[5]
         else:
-            dx = outs[0]
-        copies = weight_copies(meta, bufs, [w], sems, sz["n"], shifts=bool(blocks))
+            dx, vgrad = refs[:2]
+        copies = weight_copies(meta, bufs, [w], sems, sz["n"])
         start_all(copies)
         vgrad[...] = jnp.zeros_like(vgrad)
         wait_all(copies)
+        norm_slopes(dy, w, dn)
 
         @pl.loop(0, 4)
         def _(r):
             at = row_slices(r)
             v = up[at, :]
             gain = vec[gain_row : gain_row + 1, :]
-            down, gg, gs = norm_back(stream[at, :], gain, norm_slopes(at, dy, w))
+            down, gg, gs = norm_back(stream[at, :], gain, dn[at, :])
             dx[at, :] = v + down
             vgrad[0:1, :] += gg
             vgrad[1:2, :] += gs
@@ -855,7 +901,7 @@
         outs = [((2, places, d), F32, "v")] + [((2, places, d), B16, "v")] * 3
         scratch = [pltpu.VMEM((rows, d), F32)]
     outs += [((8, d), F32, "v")]
-    scratch += [pltpu.VMEM((4, d, d), B16), copy_sems(sz, 1)]
+    scratch += [pltpu.VMEM((4, d, d), B16), pltpu.VMEM((rows, d), F32), copy_sems(sz, 1)]
     return run(kernel, name, ins, outs, scratch, 14)
 
 
@@ -867,7 +913,7 @@
         meta, d1, q, kv, kvo, prob = refs[:6]
         bufs, refs = refs[6 : 6 + nw], refs[6 + nw :]
         up, dq, dkv, dkvo, w, dm, sums, spreads, ds, acc, sems = refs
-        copies = weight_copies(meta, bufs, [w], sems, sz["n"], shifts=True)
+        copies = weight_copies(meta, bufs, [w], sems, sz["n"])
         start_all(copies)
         head_sums(sums)
         head_spreads(spreads)
@@ -877,7 +923,7 @@
             up[row_slices(r), :] = d1[row_slices(r), :].astype(B16)
 
         wait_all(copies)
-        mixed_slopes(up, w, dm, rows, 416)
+        mixed_slopes(up, w, dm)
         for h, ref in enumerate((kv, kvo)):
 
             @pl.loop(0, 4)
@@ -973,15 +1019,17 @@
     every = ("shard", "ctx", "x", "core")
     count = 8 * n
 
-    share = jnp.concatenate([v.reshape(1, -1) for v in vectors], axis=1)
-    share = jnp.broadcast_to(share, (count, share.shape[1]))
-    shares = lax.all_to_all(share, every, split_axis=0, concat_axis=0, tiled=True)
+    gather, reduce = (Gather, Reduce) if fast else (GatherWhole, ReduceWhole)
     per = d // count
-    order = [0, 1, 2, 3, 4, 5, 6, 7, 9]
-    starts = [per * i for i in range(9)] + [per * 12]
-    vec = jnp.stack([shares[:, starts[i] : starts[i] + per].reshape(d) for i in order])
-    hidden = shares[:, starts[8] : starts[8] + 4 * per].reshape(4, d)
-    vec = jnp.concatenate([vec, hidden, jnp.zeros((3, d), F32)], axis=0)
+    order = [0, 1, 2, 3, 4, 5, 6, 7, 9, 8]
+    share = jnp.concatenate([vectors[i] for i in order])
+    first_rows = pack_heads(qkv_time, proj_time, c == 1)
+    if fast:
+        kept = lax.reduce_precision(share, exponent_bits=8, mantissa_bits=7)
+        high, low = kept.astype(B16), (share - kept).astype(B16)
+        gap = jnp.zeros((384 - share.shape[0],), B16)
+        row = jnp.concatenate([high, gap, low, gap])[None]
+        first_rows = jnp.concatenate([first_rows, row, jnp.zeros((7, d), B16)], axis=0)
 
     def clips_of(v):
         return [
@@ -999,38 +1047,41 @@
             out = lax.dynamic_update_slice_in_dim(out, b.astype(dtype)[None], at, 0)
         return out
 
-    gather, reduce = (Gather, Reduce) if fast else (GatherWhole, ReduceWhole)
-
-    g_t = gather([pack_heads(qkv_time, proj_time, c == 1)], n, True)
+    g_t = gather([first_rows], n)
     g_s = gather([pack_heads(qkv_space, proj_space, c == 1)], n)
     g_m = gather([fc_in, fc_out.T], n)
     t_z = g_t.stage_z()
-    clips = clips_of(video)
-    video_blocks = [clips[0], over_x(clips[1]), over_y(clips[2])]
-    t_xy = g_t.stage_xy(*video_blocks[1:])
-    video_blocks.append(over_xy(after(clips[3], *t_z)))
-    s_z = g_s.stage_z(vec)
-    t_rest = g_t.stage_rest(*s_z)
+    cot_clips, video_clips = [clips_of(v) for v in after((cotangent, video), g_t.spread)]
+    cot_blocks, video_blocks = frames_back(cot_clips), frames_back(video_clips)
+    t_xy = g_t.stage_xy(*cot_blocks[1:], *video_blocks[1:3])
+    s_z = g_s.stage_z(*t_z)
+    t_rest = g_t.stage_rest()
+    m_z = g_m.stage_z(*s_z)
     s_xy = g_s.stage_xy(*t_rest)
-    m_z = g_m.stage_z(*s_z)
     w_time = g_t.stage_core()
-    cot_sent = clips_of(after(cotangent, *t_xy))
-    vec_t = after(vec, *g_s.sent, *cot_sent)
+    if fast:
+        vec = norm_vectors(sz, meta, w_time)
+    else:
+        shares = lax.all_gather(share, every, axis=0, tiled=False)
+        vec = shares[:, : VECTORS * per].reshape(count, VECTORS, per).transpose(1, 0, 2)
+        hidden = shares[:, VECTORS * per :].reshape(4, d)
+        vec = jnp.concatenate([vec.reshape(VECTORS, d), hidden, jnp.zeros((3, d), F32)], axis=0)
+    vec_t = after(vec, *g_s.sent, g_m.spread)
     stream0, normed_t, q_t, kv_t = time_qkv(sz, meta, vec_t, video_blocks, w_time)
 
-    kv_o = over_core(after(kv_t, *s_xy))
+    kv_o = over_core(after(kv_t, *s_xy, *m_z))
     s_rest = g_s.stage_rest(kv_t)
-    cot_blocks = frames_back(after(tuple(cot_sent), kv_t))
-    kv_o = after(kv_o, *g_s.sent)
+    m_xy = g_m.stage_xy(kv_t)
+    kv_o = after(kv_o, *s_rest, *g_m.sent)
     mixed_t, stream1, prob_t = time_mix(sz, meta, vec, stream0, q_t, kv_t, kv_o, w_time)
 
-    w_space = g_s.stage_core(stream1)
-    m_xy = g_m.stage_xy(stream1)
-    stream1s = after(stream1, *g_m.sent, *cot_blocks)
-    normed_s, q_s, kv_s, mixed_s, logs, stream2 = space_forward(sz, meta, vec, stream1s, w_space)
-
-    m_rest = g_m.stage_rest(stream2)
-    w_mlp = g_m.stage_core()
+    w_space = g_s.stage_core()
+    normed_s, q_s, kv_s = space_qkv(sz, meta, vec, stream1, w_space)
+    m_rest = g_m.stage_rest(kv_s)
+    kv_sb = after(kv_s, *g_m.sent)
+    mixed_s, logs, stream2 = space_mix(sz, meta, vec, stream1, q_s, kv_sb, w_space)
+
+    w_mlp = g_m.stage_core(stream2)
     res, d2, vg_m, parts_m = feed_forward(sz, meta, vec, stream2, cot_blocks, w_mlp, fast)
 
     r_m = reduce(parts_m, n, "mlp")
@@ -1051,29 +1102,35 @@
     up_t, dq, dkv, dkvo = time_backward_scores(sz, meta, d1b, q_t, kv_t, kv_o, prob_t, w_time)
 
     dkv_got = over_core(after(dkvo, *m_xy, *s_rest))
-    m_z = r_m.stage_z(dkvo)
+    first_z = ()
+    if fast:
+        r_m.xy = after(tuple(m_xy), dkvo)
+        first_sent = joint_z([(r_m, 0)], n, "mlp_z")
+        first_z = (over_z(first_sent),)
     s_xy = r_s.stage_xy(dkvo)
-    dkv_got = after(dkv_got, *r_s.sent, *r_m.sent)
+    dkv_got = after(dkv_got, *r_s.sent, first_sent) if fast else dkv_got
     dy_t, *parts_t = weight_slopes(
         sz, "time_weights", meta, up_t, normed_t, mixed_t, [dq, dkv, dkv_got], fast
     )
 
     r_t = reduce(parts_t, n, "time", True)
-    t_core = r_t.stage_core(*m_z, *s_xy)
-    s_z = r_s.stage_z(*parts_t)
-    t_rest = r_t.stage_rest(*r_s.sent)
-    d1c = after(d1, *r_s.sent, *r_t.sent)
+    t_core = r_t.stage_core(*s_xy, *first_z)
+    t_rest = r_t.stage_rest()
+    if fast:
+        r_s.xy = after(tuple(s_xy), *r_t.sent)
+        sent = joint_z([(r_s, 0), (r_m, 1)], n, "joint_z")
+        got = over_z(sent)
+    else:
+        sent = ()
+    t_xy = r_t.stage_xy(sent)
+    d1c = after(d1, *r_t.sent)
     *dx, vg_t = input_slopes(sz, "time_input", meta, vec, d1c, stream0, dy_t, w_time, 0, True)
 
-    t_xy = r_t.stage_xy(vg_t)
-    t_z = r_t.stage_z()
-    vg_t2 = after(vg_t, *r_t.sent)
-    video_back = frames_back(after(tuple(dx), *r_t.sent))
-    result = join_clips(after(tuple(result_back), vg_t), B16)
-    grad_video = join_clips(video_back, F32)
-    grad_in, grad_out = r_m.results(*parts_t)
-    (grad_s,) = r_s.results(vg_t)
-    (grad_t,) = r_t.results()
+    t_z = r_t.stage_z(vg_t)
+    vg_t2, result_back, dx = after((vg_t, tuple(result_back), tuple(dx)), *r_t.sent)
+    video_back = frames_back(dx)
+    if fast:
+        vg_t2 = after(vg_t2, got)
 
     rows = jnp.concatenate([vg_t2[0:3], vg_s[0:3], vg_m[0:2]], axis=0)
     parts = jnp.concatenate(
@@ -1084,8 +1141,23 @@
         ],
         axis=1,
     )
-    got = lax.all_to_all(parts, every, split_axis=0, concat_axis=0, tiled=True)
-    sums = jnp.sum(got, axis=0)
+    got_parts = lax.all_to_all(parts, every, split_axis=0, concat_axis=0, tiled=True)
+    result = join_clips(result_back, B16)
+    if fast:
+        vec_got, video_back, r_t.z, joint, first = lax.optimization_barrier(
+            (got_parts, tuple(video_back), tuple(r_t.z), got, first_z[0])
+        )
+        joint = jnp.sum(joint.astype(F32), axis=0)
+        grad_s, grad_out = joint[0], joint[1]
+        grad_in = jnp.sum(first.astype(F32), axis=0)[0]
+    else:
+        vec_got = got_parts
+        grad_in, grad_out = r_m.results()
+        (grad_s,) = r_s.results()
+    (grad_t,) = r_t.results()
+    grad_video = join_clips(video_back, F32)
+    sums = jnp.sum(vec_got, axis=0)
+    starts = [per * i for i in range(9)] + [per * 12]
     cuts = [sums[starts[i] : starts[i] + (4 * per if i == 8 else per)] for i in range(10)]
 
     qkv_t_grad, proj_t_grad = unpack_heads(grad_t, c == 1)

time: 469 us -> 419 us (0.89)
  waiting for transfers between devices: 81.6 us -> 53.3 us
  local copies, waits for them, and re-layouts: 53.6 us -> 34.9 us
    unnamed x117 -> x97, local copies, waits for them, and re-layouts: 20.9 us -> 3.75 us
    ppermute x16, waiting for transfers between devices: 32.2 us -> 16.6 us  [over_x(): return lax.ppermute(v, 'x', FLIP)]
    ppermute x16, waiting for transfers between devices: 23.2 us -> 11.5 us  [over_y(): return lax.ppermute(v, 'ctx', FLIP)]
    all_to_all x4 -> x5, starting transfers between devices: 17.6 us -> 25 us  [over_z(): return lax.all_to_all(v, 'shard', split_axis=0, concat_axis=0, tiled=True)]
    pallas_call x9, Pallas kernels: 19.5 us -> 26.8 us  [block_sums(): pl.pallas_call(kernel, name=name, grid=(1,), in_specs=[spec(blocks, index...]
    all_to_all x2 -> x1, waiting for transfers between devices: 9.24 us -> 2.56 us  [local(): lax.all_to_all(parts, every, split_axis=0, concat_axis=0, tiled=True)]
    ppermute x3 -> x0, starting transfers between devices: 6.11 us -> none  [stage_z(): lax.ppermute(own, 'shard', [((i + d) % n, i) for i in range(n)])]
    pallas_call x10 -> x12, Pallas kernels: 216 us -> 210 us  [run(): pl.pallas_call(kernel, name=name, in_specs=[space[s] for _, s in ins], ou...]
  transfers between devices with their start and end apart: 68 -> 65, of which waited for: 18 -> 17; matrix products, arithmetic and copies ran while one was open for 9% -> 6% of each run, Pallas kernels for 41% -> 47%
where the time goes in v1:
time: 419 us; the launch traced here: 413 us
  Pallas kernels  237 us (57%)
  starting transfers between devices  79.6 us (19%)
  waiting for transfers between devices  53.3 us (13%)
  local copies, waits for them, and re-layouts  34.9 us (8%)
  other arithmetic  6.43 us (2%)
    pallas_call x12, Pallas kernels, run(): pl.pallas_call(kernel, name=name, in_specs=[space[s] for _, s in ins], ou...  210 us
    pallas_call x9, Pallas kernels, block_sums(): pl.pallas_call(kernel, name=name, grid=(1,), in_specs=[spec(blocks, index...  26.8 us
    all_to_all x5, starting transfers between devices, over_z(): return lax.all_to_all(v, 'shard', split_axis=0, concat_axis=0, tiled=True)  25 us
    ppermute x16, waiting for transfers between devices, over_x(): return lax.ppermute(v, 'x', FLIP)  16.6 us
    ppermute x16, starting transfers between devices, over_x(): return lax.ppermute(v, 'x', FLIP)  16.5 us
    ppermute x16, starting transfers between devices, over_y(): return lax.ppermute(v, 'ctx', FLIP)  15.7 us
    all_to_all x5, waiting for transfers between devices, over_z(): return lax.all_to_all(v, 'shard', split_axis=0, concat_axis=0, tiled=True)  13.1 us
    ppermute x16, waiting for transfers between devices, over_y(): return lax.ppermute(v, 'ctx', FLIP)  11.5 us
  transfers between devices with their start and end apart: 65, of which 17 were waited for; matrix products, arithmetic and copies ran while one was open for 6% of the time, Pallas kernels for 47%

profile of v1, /device:TPU:0, one launch (start us, length us, event | category | flops | bytes accessed | tf_op | source)
XLA Modules:
  0.0 413.4 jit_solution(5409270376646220622)
XLA Ops:
  4.5 6.3 %all-to-all-start = ((bf16[4,1,104,768]{3,2,1,0:T(8,128)(2,1)}), bf16[4,1,104,768]{3,2,1,0:T(8,128)(2,1)S(1)}, u32[]{:S(2)}, u32[]{:S(2)}) async-start(bf16[4,1,104,768]{3,2,1,0:T(8,128)(2,1)} %broadcast_in_dim.68), calls=%async_computation | async-start | bytes 1277952 | tf_op jit(solution)/shard_map/all_to_all | solution.py:41
  13.3 1.6 collective-permute-start.4
  17.8 2.5 collective-permute-start.2
  21.3 6.5 %all-to-all-done = bf16[4,1,104,768]{3,2,1,0:T(8,128)(2,1)S(1)} async-done(((bf16[4,1,104,768]{3,2,1,0:T(8,128)(2,1)}), bf16[4,1,104,768]{3,2,1,0:T(8,128)(2,1)S(1)}, u32[]{:S(2)}, u32[]{:S(2)}) %all-to-all-start) | async-done | bytes 639008 | tf_op jit(solution)/shard_map/all_to_all | solution.py:41
  27.8 4.1 %all-to-all-start.1 = ((bf16[4,1,96,768]{3,2,1,0:T(8,128)(2,1)}), bf16[4,1,96,768]{3,2,1,0:T(8,128)(2,1)}, u32[]{:S(2)}, u32[]{:S(2)}) async-start(bf16[4,1,96,768]{3,2,1,0:T(8,128)(2,1)} %broadcast_in_dim.69), calls=%async_computation.1 | async-start | bytes 1179648 | tf_op jit(solution)/shard_map/all_to_all | solution.py:41
  32.0 3.9 collective-permute-done.1.refs_5_
  38.0 12.6 %collective-permute-done.5.refs_2_.refs_7_.refs_6_ = bf16[4,104,768]{2,1,0:T(8,128)(2,1)S(1)} collective-permute-done((bf16[4,104,768]{2,1,0:T(8,128)(2,1)S(1)}, bf16[4,104,768]{2,1,0:T(8,128)(2,1)S(1)}, u32[]{:S(2)}, u32[]{:S(2)}) %collective-permute-start.5) | collective-permute-done | bytes 639008 | tf_op jit(solution)/shard_map/ppermute | solution.py:25
  54.7 5.4 %all-to-all-start.2 = ((bf16[4,2,96,768]{3,2,1,0:T(8,128)(2,1)}), bf16[4,2,96,768]{3,2,1,0:T(8,128)(2,1)}, u32[]{:S(2)}, u32[]{:S(2)}) async-start(bf16[4,2,96,768]{3,2,1,0:T(8,128)(2,1)} %broadcast_in_dim.70), calls=%async_computation.2 | async-start | bytes 2359296 | tf_op jit(solution)/shard_map/all_to_all | solution.py:41
  61.4 2.2 collective-permute-start.14
  66.3 3.0 norm_vectors.1.refs_1_
  69.3 3.7 collective-permute-done.14.refs_5_
  73.1 10.3 %time_qkv.1 = (f32[832,768]{1,0:T(8,128)}, bf16[832,768]{1,0:T(8,128)(2,1)}, bf16[6,832,128]{2,1,0:T(8,128)(2,1)}, bf16[12,832,128]{2,1,0:T(8,128)(2,1)}) custom-call(s32[4]{0:T(128)} %pad_add_fusion.refs_0_, f32[16,768]{1,0:T(8,128)} %norm_vectors.1.refs_1_, bf16[2,98,768]{2,1,0:T(8,128)(2,1)} %bitcast.108, ...), custom_call_target="tpu_custom_call" | custom-call | flops 12000000000 | bytes 36000000 | tf_op jit(solution)/shard_map/time_qkv/pallas_call | solution.py:372
  84.8 4.0 all-to-all-done.2
  93.7 5.6 %collective-permute-done.18.refs_6_.refs_8_ = bf16[2,96,768]{2,1,0:T(8,128)(2,1)S(1)} collective-permute-done((bf16[2,96,768]{2,1,0:T(8,128)(2,1)S(1)}, bf16[2,96,768]{2,1,0:T(8,128)(2,1)S(1)}, u32[]{:S(2)}, u32[]{:S(2)}) %collective-permute-start.18) | collective-permute-done | bytes 294944 | tf_op jit(solution)/shard_map/ppermute | solution.py:29
  99.3 2.2 collective-permute-done.19.refs_7_.refs_9_
  105.5 16.5 %time_mix.1 = (bf16[6,832,128]{2,1,0:T(8,128)(2,1)}, f32[832,768]{1,0:T(8,128)}, f32[8,208,128]{2,1,0:T(8,128)}) custom-call(s32[4]{0:T(128)} %pad_add_fusion.refs_0_, f32[16,768]{1,0:T(8,128)} %norm_vectors.1.refs_1_, f32[832,768]{1,0:T(8,128)} %get-tuple-element.153.refs_2_.refs_3_, bf16[6,832,128]{2,1,0:T(8,128)(2,1)} %get-tuple-element.154.refs_3_.refs_2_, ...), custom_call_target="tpu_custom_call" | custom-call | flops 16999999488 | bytes 51000000 | tf_op jit(solution)/shard_map/time_mix/pallas_call | solution.py:372
  122.1 10.8 %space_qkv.1 = (bf16[832,768]{1,0:T(8,128)(2,1)}, bf16[6,832,128]{2,1,0:T(8,128)(2,1)}, bf16[12,832,128]{2,1,0:T(8,128)(2,1)}) custom-call(s32[4]{0:T(128)} %pad_add_fusion.refs_0_, f32[16,768]{1,0:T(8,128)} %norm_vectors.1.refs_1_, f32[832,768]{1,0:T(8,128)} %get-tuple-element.162.refs_2_.refs_3_, bf16[4,96,768]{2,1,0:T(8,128)(2,1)} %bitcast.18.refs_3_.refs_5_, ...), custom_call_target="tpu_custom_call" | custom-call | flops 12000000000 | bytes 36000000 | tf_op jit(solution)/shard_map/space_qkv/pallas_call | solution.py:372
  132.9 1.9 slice.229
  134.8 1.9 slice.230
  139.4 21.4 %space_mix.1 = (bf16[6,832,128]{2,1,0:T(8,128)(2,1)}, f32[24,8,208]{2,1,0:T(8,128)}, f32[832,768]{1,0:T(8,128)}) custom-call(s32[4]{0:T(128)} %pad_add_fusion.refs_0_, f32[16,768]{1,0:T(8,128)} %norm_vectors.1.refs_1_, f32[832,768]{1,0:T(8,128)} %get-tuple-element.162.refs_2_.refs_3_, bf16[6,832,128]{2,1,0:T(8,128)(2,1)} %get-tuple-element.165.refs_3_.refs_2_, ...), custom_call_target="tpu_custom_call" | custom-call | flops 16999999488 | bytes 51000000 | tf_op jit(solution)/shard_map/space_mix/pallas_call | solution.py:372
  161.5 1.7 copy.144
  164.2 40.2 %feed_forward.1 = (bf16[2,98,768]{2,1,0:T(8,128)(2,1)}, bf16[2,98,768]{2,1,0:T(8,128)(2,1)}, bf16[2,98,768]{2,1,0:T(8,128)(2,1)}, bf16[2,98,768]{2,1,0:T(8,128)(...) custom-call(s32[4]{0:T(128)} %pad_add_fusion.refs_0_, ...), custom_call_target="tpu_custom_call" | custom-call | flops 46999998464 | bytes 141000000 | tf_op jit(solution)/shard_map/feed_forward/pallas_call | solution.py:372
  208.1 28.4 %space_backward_scores.1 = (bf16[832,768]{1,0:T(8,128)(2,1)}, bf16[4,832,640]{2,1,0:T(8,128)(2,1)}) custom-call(s32[4]{0:T(128)} %pad_add_fusion.refs_0_, f32[832,768]{1,0:T(8,128)} %get-tuple-element.195.refs_1_.refs_2_, bf16[6,832,128]{2,1,0:T(8,128)(2,1)} %get-tuple-element.165.refs_3_.refs_2_, bf16[12,832,128]{2,1,0:T(8,128)(2,1)} %get-tuple-element.169.refs_4_.refs_3_, ...), custom_call_target="tpu_custom_call" | custom-call | flops 30000001024 | bytes 90000000 | tf_op jit(solution)/shard_map/space_backward_scores/pallas_call | solution.py:372
  236.5 2.7 mlp_rest.1
  241.2 12.6 %space_weights.1 = (bf16[16,96,768]{2,1,0:T(8,128)(2,1)}, bf16[16,96,768]{2,1,0:T(8,128)(2,1)}) custom-call(s32[4]{0:T(128)} %pad_add_fusion.refs_0_, bf16[832,768]{1,0:T(8,128)(2,1)} %get-tuple-element.175.refs_1_, bf16[832,768]{1,0:T(8,128)(2,1)} %get-tuple-element.176.refs_2_, bf16[6,832,128]{2,1,0:T(8,128)(2,1)} %get-tuple-element.177.refs_3_, ...), custom_call_target="tpu_custom_call" | custom-call | flops 14000000000 | bytes 42000000 | tf_op jit(solution)/shard_map/space_weights/pallas_call | solution.py:372
  254.9 4.5 %mlp_xy.1 = (bf16[8,96,768]{2,1,0:T(8,128)(2,1)}, bf16[8,96,768]{2,1,0:T(8,128)(2,1)}) custom-call(bf16[32,96,768]{2,1,0:T(8,128)(2,1)} %get-tuple-element.183.refs_0_.refs_2_.refs_3_.refs_4_.refs_8_.refs_12_.refs_16_.refs_20_.refs_24_.refs_28_, ...), custom_call_target="tpu_custom_call" | custom-call | flops 100000000 | bytes 100000 | tf_op jit(solution)/shard_map/mlp_xy/pallas_call | solution.py:104
  261.7 14.2 %space_input.1 = (f32[832,768]{1,0:T(8,128)}, f32[8,768]{1,0:T(8,128)}) custom-call(s32[4]{0:T(128)} %pad_add_fusion.refs_0_, f32[16,768]{1,0:T(8,128)} %norm_vectors.1.refs_1_, f32[832,768]{1,0:T(8,128)} %get-tuple-element.195.refs_1_.refs_2_, f32[832,768]{1,0:T(8,128)} %get-tuple-element.162.refs_2_.refs_3_, ...), custom_call_target="tpu_custom_call" | custom-call | flops 14000000000 | bytes 42000000 | tf_op jit(solution)/shard_map/space_input/pallas_call | solution.py:372
  275.8 2.1 space_rest.1
  279.8 22.7 %time_backward_scores.1 = (bf16[832,768]{1,0:T(8,128)(2,1)}, bf16[6,832,128]{2,1,0:T(8,128)(2,1)}, bf16[12,832,128]{2,1,0:T(8,128)(2,1)}, bf16[12,832,128]{2,1,0:T(8,128)(2,1)}) custom-call(s32[4]{0:T(128)} %pad_add_fusion.refs_0_, f32[832,768]{1,0:T(8,128)} %get-tuple-element.228.refs_1_.refs_2_, bf16[6,832,128]{2,1,0:T(8,128)(2,1)} %get-tuple-element.154.refs_3_.refs_2_, ...), custom_call_target="tpu_custom_call" | custom-call | flops 23000000512 | bytes 69000000 | tf_op jit(solution)/shard_map/time_backward_scores/pallas_call | solution.py:372
  302.6 2.8 mlp_z.1
  305.4 4.1 %all-to-all-start.3 = ((bf16[4,1,96,768]{3,2,1,0:T(8,128)(2,1)}), bf16[4,1,96,768]{3,2,1,0:T(8,128)(2,1)}, u32[]{:S(2)}, u32[]{:S(2)}) async-start(bf16[4,1,96,768]{3,2,1,0:T(8,128)(2,1)} %bitcast.94), calls=%async_computation.3 | async-start | bytes 1179648 | tf_op jit(solution)/shard_map/all_to_all | solution.py:41
  309.6 3.0 space_xy.1
  314.8 16.2 %time_weights.1 = (bf16[4,832,640]{2,1,0:T(8,128)(2,1)}, bf16[16,96,768]{2,1,0:T(8,128)(2,1)}, bf16[16,96,768]{2,1,0:T(8,128)(2,1)}) custom-call(s32[4]{0:T(128)} %pad_add_fusion.refs_0_, bf16[832,768]{1,0:T(8,128)(2,1)} %get-tuple-element.203.refs_1_, bf16[832,768]{1,0:T(8,128)(2,1)} %get-tuple-element.204.refs_2_, ...), custom_call_target="tpu_custom_call" | custom-call | flops 14000000000 | bytes 42000000 | tf_op jit(solution)/shard_map/time_weights/pallas_call | solution.py:372
  331.1 4.9 %collective-permute-done.48.refs_1_.refs_3_.refs_4_.refs_5_.refs_9_.refs_13_ = bf16[16,96,768]{2,1,0:T(8,128)(2,1)} collective-permute-done((bf16[16,96,768]{2,1,0:T(8,128)(2,1)}, bf16[16,96,768]{2,1,0:T(8,128)(2,1)}, u32[]{:S(2)}, u32[]{:S(2)}) %collective-permute-start.48) | collective-permute-done | bytes 2359328 | tf_op jit(solution)/shard_map/ppermute | solution.py:37
  336.0 2.1 time_rest.1
  345.4 4.0 joint_z.1
  349.4 5.1 %all-to-all-start.4 = ((bf16[4,2,96,768]{3,2,1,0:T(8,128)(2,1)}), bf16[4,2,96,768]{3,2,1,0:T(8,128)(2,1)}, u32[]{:S(2)}, u32[]{:S(2)}) async-start(bf16[4,2,96,768]{3,2,1,0:T(8,128)(2,1)} %bitcast.93), calls=%async_computation.4 | async-start | bytes 2359296 | tf_op jit(solution)/shard_map/all_to_all | solution.py:41
  354.5 3.0 time_xy.1
  359.7 13.8 %time_input.1 = (f32[2,98,768]{2,1,0:T(8,128)}, bf16[2,98,768]{2,1,0:T(8,128)(2,1)}, bf16[2,98,768]{2,1,0:T(8,128)(2,1)}, bf16[2,98,768]{2,1,0:T(8,128)(2,1)}, f32[8,768]{1,0:T(8,128)}) custom-call(s32[4]{0:T(128)} %pad_add_fusion.refs_0_, f32[16,768]{1,0:T(8,128)} %norm_vectors.1.refs_1_, f32[832,768]{1,0:T(8,128)} %get-tuple-element.228.refs_1_.refs_2_, ...), custom_call_target="tpu_custom_call" | custom-call | flops 14000000000 | bytes 42000000 | tf_op jit(solution)/shard_map/time_input/pallas_call | solution.py:372
  373.6 2.7 time_z.1
  376.2 2.2 collective-permute-start.56
  378.5 2.4 collective-permute-start.57
  382.6 1.7 collective-permute-start.55
  387.7 2.5 all-to-all-done.4
  391.4 2.6 all-to-all-start.5
  394.0 3.7 collective-permute-start.58
  398.9 2.6 all-to-all-done.5
  407.1 1.9 convert_reduce_fusion.1
  (285 shorter events, 74.5 us)
Async XLA Ops:
  4.5 23.3 %all-to-all-start = ((bf16[4,1,104,768]{3,2,1,0:T(8,128)(2,1)}), bf16[4,1,104,768]{3,2,1,0:T(8,128)(2,1)S(1)}, u32[]{:S(2)}, u32[]{:S(2)}) async-start(bf16[4,1,104,768]{3,2,1,0:T(8,128)(2,1)} %broadcast_in_dim.68), calls=%async_computation | async-start | bytes 1277952 | tf_op jit(solution)/shard_map/all_to_all | solution.py:41
  11.7 20.2 %collective-permute-start.3 = (bf16[2,98,768]{2,1,0:T(8,128)(2,1)S(1)}, bf16[2,98,768]{2,1,0:T(8,128)(2,1)}, u32[]{:S(2)}, u32[]{:S(2)}) collective-permute-start(bf16[2,98,768]{2,1,0:T(8,128)(2,1)S(1)} %bitcast.105), channel_id=1, source_target_pairs={{0,2},{2,0},{1,3},{3,1},{4,6},{6,4},{5,7},{7,5},{8,10},{10,8},{9,1... | collective-permute-start | bytes 903176 | tf_op jit(solution)/shard_map/ppermute | solution.py:25
  13.3 18.6 %collective-permute-start.4 = (bf16[2,98,768]{2,1,0:T(8,128)(2,1)S(1)}, bf16[2,98,768]{2,1,0:T(8,128)(2,1)}, u32[]{:S(2)}, u32[]{:S(2)}) collective-permute-start(bf16[2,98,768]{2,1,0:T(8,128)(2,1)S(1)} %bitcast.106), channel_id=1, source_target_pairs={{0,4},{4,0},{1,5},{5,1},{2,6},{6,2},{3,7},{7,3},{8,12},{12,8},{9,1... | collective-permute-start | bytes 903176 | tf_op jit(solution)/shard_map/ppermute | solution.py:29
  16.5 15.5 %collective-permute-start = (bf16[2,98,768]{2,1,0:T(8,128)(2,1)S(1)}, bf16[2,98,768]{2,1,0:T(8,128)(2,1)}, u32[]{:S(2)}, u32[]{:S(2)}) collective-permute-start(bf16[2,98,768]{2,1,0:T(8,128)(2,1)S(1)} %bitcast.107), channel_id=1, source_target_pairs={{0,2},{2,0},{1,3},{3,1},{4,6},{6,4},{5,7},{7,5},{8,10},{10,8},{9,1... | collective-permute-start | bytes 903176 | tf_op jit(solution)/shard_map/ppermute | solution.py:25
  17.1 18.8 %collective-permute-start.1 = (bf16[2,98,768]{2,1,0:T(8,128)(2,1)S(1)}, bf16[2,98,768]{2,1,0:T(8,128)(2,1)}, u32[]{:S(2)}, u32[]{:S(2)}) collective-permute-start(bf16[2,98,768]{2,1,0:T(8,128)(2,1)S(1)} %bitcast.110), channel_id=1, source_target_pairs={{0,4},{4,0},{1,5},{5,1},{2,6},{6,2},{3,7},{7,3},{8,12},{12,8},{9,1... | collective-permute-start | bytes 903176 | tf_op jit(solution)/shard_map/ppermute | solution.py:29
  17.8 18.2 %collective-permute-start.2 = (bf16[2,98,768]{2,1,0:T(8,128)(2,1)S(1)}, bf16[2,98,768]{2,1,0:T(8,128)(2,1)}, u32[]{:S(2)}, u32[]{:S(2)}) collective-permute-start(bf16[2,98,768]{2,1,0:T(8,128)(2,1)S(1)} %bitcast.111), channel_id=1, source_target_pairs={{0,6},{2,4},{4,2},{6,0},{1,7},{3,5},{5,3},{7,1},{8,14},{10,12},{12... | collective-permute-start | bytes 903176 | tf_op jit(solution)/shard_map/ppermute | solution.py:33
  27.8 26.9 %all-to-all-start.1 = ((bf16[4,1,96,768]{3,2,1,0:T(8,128)(2,1)}), bf16[4,1,96,768]{3,2,1,0:T(8,128)(2,1)}, u32[]{:S(2)}, u32[]{:S(2)}) async-start(bf16[4,1,96,768]{3,2,1,0:T(8,128)(2,1)} %broadcast_in_dim.69), calls=%async_computation.1 | async-start | bytes 1179648 | tf_op jit(solution)/shard_map/all_to_all | solution.py:41
  35.9 14.6 %collective-permute-start.5 = (bf16[4,104,768]{2,1,0:T(8,128)(2,1)S(1)}, bf16[4,104,768]{2,1,0:T(8,128)(2,1)S(1)}, u32[]{:S(2)}, u32[]{:S(2)}) collective-permute-start(bf16[4,104,768]{2,1,0:T(8,128)(2,1)S(1)} %bitcast.95), channel_id=1, source_target_pairs={{0,2},{2,0},{1,3},{3,1},{4,6},{6,4},{5,7},{7,5},{8,10},{10,8},{9,1... | collective-permute-start | bytes 1916936 | tf_op jit(solution)/shard_map/ppermute | solution.py:25
  37.1 14.7 %collective-permute-start.6 = (bf16[4,104,768]{2,1,0:T(8,128)(2,1)S(1)}, bf16[4,104,768]{2,1,0:T(8,128)(2,1)S(1)}, u32[]{:S(2)}, u32[]{:S(2)}) collective-permute-start(bf16[4,104,768]{2,1,0:T(8,128)(2,1)S(1)} %bitcast.96), channel_id=1, source_target_pairs={{0,4},{4,0},{1,5},{5,1},{2,6},{6,2},{3,7},{7,3},{8,12},{12,8},{9,1... | collective-permute-start | bytes 1916936 | tf_op jit(solution)/shard_map/ppermute | solution.py:29
  38.0 23.4 %collective-permute-start.9 = (bf16[4,104,768]{2,1,0:T(8,128)(2,1)S(1)}, bf16[4,104,768]{2,1,0:T(8,128)(2,1)}, u32[]{:S(2)}, u32[]{:S(2)}) collective-permute-start(bf16[4,104,768]{2,1,0:T(8,128)(2,1)S(1)} %bitcast.97), channel_id=1, source_target_pairs={{0,1},{1,0},{2,3},{3,2},{4,5},{5,4},{6,7},{7,6},{8,9},{9,8},{10,11... | collective-permute-start | bytes 1916936 | tf_op jit(solution)/shard_map/ppermute | solution.py:37
  53.0 13.3 %collective-permute-start.11 = (bf16[4,104,768]{2,1,0:T(8,128)(2,1)S(1)}, bf16[4,104,768]{2,1,0:T(8,128)(2,1)}, u32[]{:S(2)}, u32[]{:S(2)}) collective-permute-start(bf16[4,104,768]{2,1,0:T(8,128)(2,1)S(1)} %collective-permute-done.6.refs_3_.refs_8_.refs_7_), channel_id=1, source_target_pairs={{0,1},{1,0},{2,3},{3,2},{4,5},{5,4},{6,7},{7,6},{8,9},{9,8},{10,11... | collective-permute-start | bytes 1916936 | tf_op jit(solution)/shard_map/ppermute | solution.py:37
  54.7 34.2 %all-to-all-start.2 = ((bf16[4,2,96,768]{3,2,1,0:T(8,128)(2,1)}), bf16[4,2,96,768]{3,2,1,0:T(8,128)(2,1)}, u32[]{:S(2)}, u32[]{:S(2)}) async-start(bf16[4,2,96,768]{3,2,1,0:T(8,128)(2,1)} %broadcast_in_dim.70), calls=%async_computation.2 | async-start | bytes 2359296 | tf_op jit(solution)/shard_map/all_to_all | solution.py:41
  64.9 19.7 %collective-permute-start.15 = (bf16[4,96,768]{2,1,0:T(8,128)(2,1)}, bf16[4,96,768]{2,1,0:T(8,128)(2,1)}, u32[]{:S(2)}, u32[]{:S(2)}) collective-permute-start(bf16[4,96,768]{2,1,0:T(8,128)(2,1)} %bitcast.18.refs_3_.refs_5_), channel_id=1, source_target_pairs={{0,2},{2,0},{1,3},{3,1},{4,6},{6,4},{5,7},{7,5},{8,10},{10,8},{9,1... | collective-permute-start | bytes 1769480 | tf_op jit(solution)/shard_map/ppermute | solution.py:25
  65.5 19.3 %collective-permute-start.16 = (bf16[4,96,768]{2,1,0:T(8,128)(2,1)}, bf16[4,96,768]{2,1,0:T(8,128)(2,1)}, u32[]{:S(2)}, u32[]{:S(2)}) collective-permute-start(bf16[4,96,768]{2,1,0:T(8,128)(2,1)} %bitcast.18.refs_3_.refs_5_), channel_id=1, source_target_pairs={{0,4},{4,0},{1,5},{5,1},{2,6},{6,2},{3,7},{7,3},{8,12},{12,8},{9,1... | collective-permute-start | bytes 1769480 | tf_op jit(solution)/shard_map/ppermute | solution.py:29
  101.5 20.6 %collective-permute-start.21 = (bf16[4,96,768]{2,1,0:T(8,128)(2,1)}, bf16[4,96,768]{2,1,0:T(8,128)(2,1)}, u32[]{:S(2)}, u32[]{:S(2)}) collective-permute-start(bf16[4,96,768]{2,1,0:T(8,128)(2,1)} %collective-permute-done.15.refs_4_.refs_6_), channel_id=1, source_target_pairs={{0,1},{1,0},{2,3},{3,2},{4,5},{5,4},{6,7},{7,6},{8,9},{9,8},{10,11... | collective-permute-start | bytes 1769480 | tf_op jit(solution)/shard_map/ppermute | solution.py:37
  102.0 20.1 %collective-permute-start.22 = (bf16[4,96,768]{2,1,0:T(8,128)(2,1)}, bf16[4,96,768]{2,1,0:T(8,128)(2,1)}, u32[]{:S(2)}, u32[]{:S(2)}) collective-permute-start(bf16[4,96,768]{2,1,0:T(8,128)(2,1)} %collective-permute-done.16.refs_5_.refs_7_), channel_id=1, source_target_pairs={{0,1},{1,0},{2,3},{3,2},{4,5},{5,4},{6,7},{7,6},{8,9},{9,8},{10,11... | collective-permute-start | bytes 1769480 | tf_op jit(solution)/shard_map/ppermute | solution.py:37
  102.0 20.0 %collective-permute-start.24 = (bf16[2,96,768]{2,1,0:T(8,128)(2,1)}, bf16[2,96,768]{2,1,0:T(8,128)(2,1)}, u32[]{:S(2)}, u32[]{:S(2)}) collective-permute-start(bf16[2,96,768]{2,1,0:T(8,128)(2,1)} %collective-permute-done.19.refs_7_.refs_9_), channel_id=1, source_target_pairs={{0,1},{1,0},{2,3},{3,2},{4,5},{5,4},{6,7},{7,6},{8,9},{9,8},{10,11... | collective-permute-start | bytes 884744 | tf_op jit(solution)/shard_map/ppermute | solution.py:37
  102.5 30.4 %collective-permute-start.25 = (bf16[8,96,768]{2,1,0:T(8,128)(2,1)}, bf16[8,96,768]{2,1,0:T(8,128)(2,1)}, u32[]{:S(2)}, u32[]{:S(2)}) collective-permute-start(bf16[8,96,768]{2,1,0:T(8,128)(2,1)} %bitcast.24.refs_7_), channel_id=1, source_target_pairs={{0,2},{2,0},{1,3},{3,1},{4,6},{6,4},{5,7},{7,5},{8,10},{10,8},{9,1... | collective-permute-start | bytes 3538952 | tf_op jit(solution)/shard_map/ppermute | solution.py:25
  104.7 28.3 %collective-permute-start.26 = (bf16[8,96,768]{2,1,0:T(8,128)(2,1)}, bf16[8,96,768]{2,1,0:T(8,128)(2,1)}, u32[]{:S(2)}, u32[]{:S(2)}) collective-permute-start(bf16[8,96,768]{2,1,0:T(8,128)(2,1)} %bitcast.24.refs_7_), channel_id=1, source_target_pairs={{0,4},{4,0},{1,5},{5,1},{2,6},{6,2},{3,7},{7,3},{8,12},{12,8},{9,1... | collective-permute-start | bytes 3538952 | tf_op jit(solution)/shard_map/ppermute | solution.py:29
  122.0 41.2 %collective-permute-start.29 = (bf16[8,96,768]{2,1,0:T(8,128)(2,1)}, bf16[8,96,768]{2,1,0:T(8,128)(2,1)}, u32[]{:S(2)}, u32[]{:S(2)}) collective-permute-start(bf16[8,96,768]{2,1,0:T(8,128)(2,1)} %bitcast.24.refs_7_), channel_id=1, source_target_pairs={{0,1},{1,0},{2,3},{3,2},{4,5},{5,4},{6,7},{7,6},{8,9},{9,8},{10,11... | collective-permute-start | bytes 3538952 | tf_op jit(solution)/shard_map/ppermute | solution.py:37
  136.8 24.1 %collective-permute-start.27 = (bf16[4,96,768]{2,1,0:T(8,128)(2,1)}, bf16[4,96,768]{2,1,0:T(8,128)(2,1)}, u32[]{:S(2)}, u32[]{:S(2)}) collective-permute-start(bf16[4,96,768]{2,1,0:T(8,128)(2,1)} %slice.229), channel_id=1, source_target_pairs={{0,4},{4,0},{1,5},{5,1},{2,6},{6,2},{3,7},{7,3},{8,12},{12,8},{9,1... | collective-permute-start | bytes 1769480 | tf_op jit(solution)/shard_map/ppermute | solution.py:29
  138.0 22.9 %collective-permute-start.28 = (bf16[4,96,768]{2,1,0:T(8,128)(2,1)}, bf16[4,96,768]{2,1,0:T(8,128)(2,1)}, u32[]{:S(2)}, u32[]{:S(2)}) collective-permute-start(bf16[4,96,768]{2,1,0:T(8,128)(2,1)} %slice.230), channel_id=1, source_target_pairs={{0,2},{2,0},{1,3},{3,1},{4,6},{6,4},{5,7},{7,5},{8,10},{10,8},{9,1... | collective-permute-start | bytes 1769480 | tf_op jit(solution)/shard_map/ppermute | solution.py:25
  138.9 24.3 %collective-permute-start.30 = (bf16[8,96,768]{2,1,0:T(8,128)(2,1)}, bf16[8,96,768]{2,1,0:T(8,128)(2,1)}, u32[]{:S(2)}, u32[]{:S(2)}) collective-permute-start(bf16[8,96,768]{2,1,0:T(8,128)(2,1)} %collective-permute-done.25.refs_8_), channel_id=1, source_target_pairs={{0,1},{1,0},{2,3},{3,2},{4,5},{5,4},{6,7},{7,6},{8,9},{9,8},{10,11... | collective-permute-start | bytes 3538952 | tf_op jit(solution)/shard_map/ppermute | solution.py:37
  138.9 24.3 %collective-permute-start.31 = (bf16[8,96,768]{2,1,0:T(8,128)(2,1)}, bf16[8,96,768]{2,1,0:T(8,128)(2,1)}, u32[]{:S(2)}, u32[]{:S(2)}) collective-permute-start(bf16[8,96,768]{2,1,0:T(8,128)(2,1)} %collective-permute-done.26.refs_9_), channel_id=1, source_target_pairs={{0,1},{1,0},{2,3},{3,2},{4,5},{5,4},{6,7},{7,6},{8,9},{9,8},{10,11... | collective-permute-start | bytes 3538952 | tf_op jit(solution)/shard_map/ppermute | solution.py:37
  204.4 32.1 %collective-permute-start.37 = (bf16[32,96,768]{2,1,0:T(8,128)(2,1)}, bf16[32,96,768]{2,1,0:T(8,128)(2,1)}, u32[]{:S(2)}, u32[]{:S(2)}) collective-permute-start(bf16[32,96,768]{2,1,0:T(8,128)(2,1)} %get-tuple-element.184), channel_id=1, source_target_pairs={{0,1},{1,0},{2,3},{3,2},{4,5},{5,4},{6,7},{7,6},{8,9},{9,8},{10,11... | collective-permute-start | bytes 14155784 | tf_op jit(solution)/shard_map/ppermute | solution.py:37
  204.6 36.6 %collective-permute-start.34 = (bf16[2,98,768]{2,1,0:T(8,128)(2,1)}, bf16[2,98,768]{2,1,0:T(8,128)(2,1)}, u32[]{:S(2)}, u32[]{:S(2)}) collective-permute-start(bf16[2,98,768]{2,1,0:T(8,128)(2,1)} %get-tuple-element.180), channel_id=1, source_target_pairs={{0,2},{2,0},{1,3},{3,1},{4,6},{6,4},{5,7},{7,5},{8,10},{10,8},{9,1... | collective-permute-start | bytes 903176 | tf_op jit(solution)/shard_map/ppermute | solution.py:25
  205.7 35.5 %collective-permute-start.35 = (bf16[2,98,768]{2,1,0:T(8,128)(2,1)}, bf16[2,98,768]{2,1,0:T(8,128)(2,1)}, u32[]{:S(2)}, u32[]{:S(2)}) collective-permute-start(bf16[2,98,768]{2,1,0:T(8,128)(2,1)} %get-tuple-element.181), channel_id=1, source_target_pairs={{0,4},{4,0},{1,5},{5,1},{2,6},{6,2},{3,7},{7,3},{8,12},{12,8},{9,1... | collective-permute-start | bytes 903176 | tf_op jit(solution)/shard_map/ppermute | solution.py:29
  206.5 34.7 %collective-permute-start.36 = (bf16[2,98,768]{2,1,0:T(8,128)(2,1)}, bf16[2,98,768]{2,1,0:T(8,128)(2,1)}, u32[]{:S(2)}, u32[]{:S(2)}) collective-permute-start(bf16[2,98,768]{2,1,0:T(8,128)(2,1)} %get-tuple-element.182), channel_id=1, source_target_pairs={{0,6},{2,4},{4,2},{6,0},{1,7},{3,5},{5,3},{7,1},{8,14},{10,12},{12... | collective-permute-start | bytes 903176 | tf_op jit(solution)/shard_map/ppermute | solution.py:33
  239.3 15.1 %collective-permute-start.38 = (bf16[4,96,768]{2,1,0:T(8,128)(2,1)}, bf16[4,96,768]{2,1,0:T(8,128)(2,1)}, u32[]{:S(2)}, u32[]{:S(2)}) collective-permute-start(bf16[4,96,768]{2,1,0:T(8,128)(2,1)} %get-tuple-element.186), channel_id=1, source_target_pairs={{0,4},{4,0},{1,5},{5,1},{2,6},{6,2},{3,7},{7,3},{8,12},{12,8},{9,1... | collective-permute-start | bytes 1769480 | tf_op jit(solution)/shard_map/ppermute | solution.py:29
  240.1 14.8 %collective-permute-start.39 = (bf16[4,96,768]{2,1,0:T(8,128)(2,1)}, bf16[4,96,768]{2,1,0:T(8,128)(2,1)}, u32[]{:S(2)}, u32[]{:S(2)}) collective-permute-start(bf16[4,96,768]{2,1,0:T(8,128)(2,1)} %get-tuple-element.187), channel_id=1, source_target_pairs={{0,2},{2,0},{1,3},{3,1},{4,6},{6,4},{5,7},{7,5},{8,10},{10,8},{9,1... | collective-permute-start | bytes 1769480 | tf_op jit(solution)/shard_map/ppermute | solution.py:25
  254.9 20.9 %collective-permute-start.40 = (bf16[16,96,768]{2,1,0:T(8,128)(2,1)}, bf16[16,96,768]{2,1,0:T(8,128)(2,1)}, u32[]{:S(2)}, u32[]{:S(2)}) collective-permute-start(bf16[16,96,768]{2,1,0:T(8,128)(2,1)} %get-tuple-element.197), channel_id=1, source_target_pairs={{0,1},{1,0},{2,3},{3,2},{4,5},{5,4},{6,7},{7,6},{8,9},{9,8},{10,11... | collective-permute-start | bytes 7077896 | tf_op jit(solution)/shard_map/ppermute | solution.py:37
  259.4 43.1 %collective-permute-start.41 = (bf16[8,96,768]{2,1,0:T(8,128)(2,1)}, bf16[8,96,768]{2,1,0:T(8,128)(2,1)}, u32[]{:S(2)}, u32[]{:S(2)}) collective-permute-start(bf16[8,96,768]{2,1,0:T(8,128)(2,1)} %get-tuple-element.193), channel_id=1, source_target_pairs={{0,2},{2,0},{1,3},{3,1},{4,6},{6,4},{5,7},{7,5},{8,10},{10,8},{9,1... | collective-permute-start | bytes 3538952 | tf_op jit(solution)/shard_map/ppermute | solution.py:25
  260.5 42.0 %collective-permute-start.42 = (bf16[8,96,768]{2,1,0:T(8,128)(2,1)}, bf16[8,96,768]{2,1,0:T(8,128)(2,1)}, u32[]{:S(2)}, u32[]{:S(2)}) collective-permute-start(bf16[8,96,768]{2,1,0:T(8,128)(2,1)} %get-tuple-element.194), channel_id=1, source_target_pairs={{0,4},{4,0},{1,5},{5,1},{2,6},{6,2},{3,7},{7,3},{8,12},{12,8},{9,1... | collective-permute-start | bytes 3538952 | tf_op jit(solution)/shard_map/ppermute | solution.py:29
  278.0 24.5 %collective-permute-start.43 = (bf16[2,96,768]{2,1,0:T(8,128)(2,1)}, bf16[2,96,768]{2,1,0:T(8,128)(2,1)}, u32[]{:S(2)}, u32[]{:S(2)}) collective-permute-start(bf16[2,96,768]{2,1,0:T(8,128)(2,1)} %get-tuple-element.199), channel_id=1, source_target_pairs={{0,4},{4,0},{1,5},{5,1},{2,6},{6,2},{3,7},{7,3},{8,12},{12,8},{9,1... | collective-permute-start | bytes 884744 | tf_op jit(solution)/shard_map/ppermute | solution.py:29
  278.8 23.7 %collective-permute-start.44 = (bf16[2,96,768]{2,1,0:T(8,128)(2,1)}, bf16[2,96,768]{2,1,0:T(8,128)(2,1)}, u32[]{:S(2)}, u32[]{:S(2)}) collective-permute-start(bf16[2,96,768]{2,1,0:T(8,128)(2,1)} %get-tuple-element.200), channel_id=1, source_target_pairs={{0,2},{2,0},{1,3},{3,1},{4,6},{6,4},{5,7},{7,5},{8,10},{10,8},{9,1... | collective-permute-start | bytes 884744 | tf_op jit(solution)/shard_map/ppermute | solution.py:25
  305.4 25.6 %all-to-all-start.3 = ((bf16[4,1,96,768]{3,2,1,0:T(8,128)(2,1)}), bf16[4,1,96,768]{3,2,1,0:T(8,128)(2,1)}, u32[]{:S(2)}, u32[]{:S(2)}) async-start(bf16[4,1,96,768]{3,2,1,0:T(8,128)(2,1)} %bitcast.94), calls=%async_computation.3 | async-start | bytes 1179648 | tf_op jit(solution)/shard_map/all_to_all | solution.py:41
  312.5 18.5 %collective-permute-start.46 = (bf16[4,96,768]{2,1,0:T(8,128)(2,1)}, bf16[4,96,768]{2,1,0:T(8,128)(2,1)}, u32[]{:S(2)}, u32[]{:S(2)}) collective-permute-start(bf16[4,96,768]{2,1,0:T(8,128)(2,1)} %get-tuple-element.212), channel_id=1, source_target_pairs={{0,2},{2,0},{1,3},{3,1},{4,6},{6,4},{5,7},{7,5},{8,10},{10,8},{9,1... | collective-permute-start | bytes 1769480 | tf_op jit(solution)/shard_map/ppermute | solution.py:25
  313.6 17.5 %collective-permute-start.47 = (bf16[4,96,768]{2,1,0:T(8,128)(2,1)}, bf16[4,96,768]{2,1,0:T(8,128)(2,1)}, u32[]{:S(2)}, u32[]{:S(2)}) collective-permute-start(bf16[4,96,768]{2,1,0:T(8,128)(2,1)} %get-tuple-element.213), channel_id=1, source_target_pairs={{0,4},{4,0},{1,5},{5,1},{2,6},{6,2},{3,7},{7,3},{8,12},{12,8},{9,1... | collective-permute-start | bytes 1769480 | tf_op jit(solution)/shard_map/ppermute | solution.py:29
  338.1 16.4 %collective-permute-start.49 = (bf16[2,96,768]{2,1,0:T(8,128)(2,1)}, bf16[2,96,768]{2,1,0:T(8,128)(2,1)}, u32[]{:S(2)}, u32[]{:S(2)}) collective-permute-start(bf16[2,96,768]{2,1,0:T(8,128)(2,1)} %get-tuple-element.220), channel_id=1, source_target_pairs={{0,4},{4,0},{1,5},{5,1},{2,6},{6,2},{3,7},{7,3},{8,12},{12,8},{9,1... | collective-permute-start | bytes 884744 | tf_op jit(solution)/shard_map/ppermute | solution.py:29
  338.9 15.6 %collective-permute-start.50 = (bf16[2,96,768]{2,1,0:T(8,128)(2,1)}, bf16[2,96,768]{2,1,0:T(8,128)(2,1)}, u32[]{:S(2)}, u32[]{:S(2)}) collective-permute-start(bf16[2,96,768]{2,1,0:T(8,128)(2,1)} %get-tuple-element.221), channel_id=1, source_target_pairs={{0,2},{2,0},{1,3},{3,1},{4,6},{6,4},{5,7},{7,5},{8,10},{10,8},{9,1... | collective-permute-start | bytes 884744 | tf_op jit(solution)/shard_map/ppermute | solution.py:25
  349.4 40.8 %all-to-all-start.4 = ((bf16[4,2,96,768]{3,2,1,0:T(8,128)(2,1)}), bf16[4,2,96,768]{3,2,1,0:T(8,128)(2,1)}, u32[]{:S(2)}, u32[]{:S(2)}) async-start(bf16[4,2,96,768]{3,2,1,0:T(8,128)(2,1)} %bitcast.93), calls=%async_computation.4 | async-start | bytes 2359296 | tf_op jit(solution)/shard_map/all_to_all | solution.py:41
  357.4 16.1 %collective-permute-start.51 = (bf16[4,96,768]{2,1,0:T(8,128)(2,1)}, bf16[4,96,768]{2,1,0:T(8,128)(2,1)}, u32[]{:S(2)}, u32[]{:S(2)}) collective-permute-start(bf16[4,96,768]{2,1,0:T(8,128)(2,1)} %get-tuple-element.226), channel_id=1, source_target_pairs={{0,2},{2,0},{1,3},{3,1},{4,6},{6,4},{5,7},{7,5},{8,10},{10,8},{9,1... | collective-permute-start | bytes 1769480 | tf_op jit(solution)/shard_map/ppermute | solution.py:25
  358.5 15.1 %collective-permute-start.52 = (bf16[4,96,768]{2,1,0:T(8,128)(2,1)}, bf16[4,96,768]{2,1,0:T(8,128)(2,1)}, u32[]{:S(2)}, u32[]{:S(2)}) collective-permute-start(bf16[4,96,768]{2,1,0:T(8,128)(2,1)} %get-tuple-element.227), channel_id=1, source_target_pairs={{0,4},{4,0},{1,5},{5,1},{2,6},{6,2},{3,7},{7,3},{8,12},{12,8},{9,1... | collective-permute-start | bytes 1769480 | tf_op jit(solution)/shard_map/ppermute | solution.py:29
  376.2 17.7 %collective-permute-start.56 = (bf16[1,96,768]{2,1,0:T(8,128)(2,1)}, bf16[1,96,768]{2,1,0:T(8,128)(2,1)S(1)}, u32[]{:S(2)}, u32[]{:S(2)}) collective-permute-start(bf16[1,96,768]{2,1,0:T(8,128)(2,1)} %get-tuple-element.237), channel_id=1, source_target_pairs={{0,8},{8,16},{16,24},{24,0},{1,9},{9,17},{17,25},{25,1},{2,10},{10... | collective-permute-start | bytes 442376 | tf_op jit(solution)/shard_map/ppermute | solution.py:165
  378.5 23.0 %collective-permute-start.57 = (bf16[1,96,768]{2,1,0:T(8,128)(2,1)}, bf16[1,96,768]{2,1,0:T(8,128)(2,1)S(1)}, u32[]{:S(2)}, u32[]{:S(2)}) collective-permute-start(bf16[1,96,768]{2,1,0:T(8,128)(2,1)} %get-tuple-element.238), channel_id=1, source_target_pairs={{0,16},{8,24},{16,0},{24,8},{1,17},{9,25},{17,1},{25,9},{2,18},{10... | collective-permute-start | bytes 442376 | tf_op jit(solution)/shard_map/ppermute | solution.py:165
  380.8 20.6 %collective-permute-start.53 = (bf16[2,98,768]{2,1,0:T(8,128)(2,1)}, bf16[2,98,768]{2,1,0:T(8,128)(2,1)S(1)}, u32[]{:S(2)}, u32[]{:S(2)}) collective-permute-start(bf16[2,98,768]{2,1,0:T(8,128)(2,1)} %get-tuple-element.249), channel_id=1, source_target_pairs={{0,2},{2,0},{1,3},{3,1},{4,6},{6,4},{5,7},{7,5},{8,10},{10,8},{9,1... | collective-permute-start | bytes 903176 | tf_op jit(solution)/shard_map/ppermute | solution.py:25
  381.8 19.7 %collective-permute-start.54 = (bf16[2,98,768]{2,1,0:T(8,128)(2,1)}, bf16[2,98,768]{2,1,0:T(8,128)(2,1)S(1)}, u32[]{:S(2)}, u32[]{:S(2)}) collective-permute-start(bf16[2,98,768]{2,1,0:T(8,128)(2,1)} %get-tuple-element.250), channel_id=1, source_target_pairs={{0,4},{4,0},{1,5},{5,1},{2,6},{6,2},{3,7},{7,3},{8,12},{12,8},{9,1... | collective-permute-start | bytes 903176 | tf_op jit(solution)/shard_map/ppermute | solution.py:29
  382.6 18.9 %collective-permute-start.55 = (bf16[2,98,768]{2,1,0:T(8,128)(2,1)}, bf16[2,98,768]{2,1,0:T(8,128)(2,1)S(1)}, u32[]{:S(2)}, u32[]{:S(2)}) collective-permute-start(bf16[2,98,768]{2,1,0:T(8,128)(2,1)} %get-tuple-element.251), channel_id=1, source_target_pairs={{0,6},{2,4},{4,2},{6,0},{1,7},{3,5},{5,3},{7,1},{8,14},{10,12},{12... | collective-permute-start | bytes 903176 | tf_op jit(solution)/shard_map/ppermute | solution.py:33
  (52 other events, 317.5 us)

commit v2 on v1

--- a/solution.py
+++ b/solution.py
@@ -277,13 +277,15 @@
     return down, jnp.sum(up * unit, axis=0, keepdims=True), jnp.sum(up, axis=0, keepdims=True)
 
 
-def weight_copies(meta, bufs, w_refs, sems, n, back=False, shifts=False):
+def weight_copies(meta, bufs, w_refs, sems, n, back=False, shifts=False, first_column=0):
     moves = []
     if bufs[0].shape == w_refs[0].shape:
         moves = list(zip(bufs, w_refs))
     else:
         x, y, c = meta[0], meta[1], meta[2]
         rows = w_refs[0].shape[1] // (2 * n)
+        groups = {}
+        cols = slice(first_column, w_refs[0].shape[2])
         for dc in range(2):
             first = 0
             for k, (dx, dy, blocks) in enumerate(layout(len(w_refs), n)):
@@ -292,9 +294,11 @@
                     if shifts:
                         z = lax.rem(meta[3] + z, n)
                     row = pl.multiple_of((z * 2 + (y ^ dy)) * rows, rows)
-                    piece = bufs[dc].at[first + i] if back else bufs[dc * 5 + k].at[i, 0:rows, :]
-                    moves.append((piece, w_refs[chunk].at[tp, pl.ds(row, rows), :]))
+                    piece = bufs[dc].at[first + i] if back else bufs[dc * 5 + k].at[i, 0:rows, cols]
+                    whole = w_refs[chunk].at[tp, pl.ds(row, rows), cols]
+                    groups.setdefault((dx, dc), []).append((piece, whole))
                 first += len(blocks)
+        moves = [m for g in sorted(groups) for m in groups[g]]
     if back:
         moves = [(whole, piece) for piece, whole in moves]
     return [pltpu.make_async_copy(*m, sems.at[i]) for i, m in enumerate(moves)]
@@ -363,19 +367,57 @@
         out[:, cols] = acc
 
 
+class Late:
+    def __init__(self, source, ref, sem):
+        self.ref, self.copy = ref, pltpu.make_async_copy(source, ref, sem)
+        self.copy.start()
+
+    def get(self):
+        self.copy.wait()
+        return self.ref
+
+
+class Early:
+    def __init__(self, ref, target, sem):
+        self.ref, self.copy = ref, pltpu.make_async_copy(ref, target, sem)
+
+    def send(self):
+        self.copy.start()
+
+
 def run(kernel, name, ins, outs, scratch, micros):
     space = {
         "v": pl.BlockSpec(memory_space=pltpu.VMEM),
         "s": pl.BlockSpec(memory_space=pltpu.SMEM),
         "a": pl.BlockSpec(memory_space=pl.ANY),
     }
+    space["l"] = space["e"] = space["a"]
+    late = [i for i, (_, k) in enumerate(ins) if k == "l"]
+    early = [i for i, (_, _, k) in enumerate(outs) if k == "e"]
+    extra = [pltpu.VMEM(ins[i][0].shape, ins[i][0].dtype) for i in late]
+    extra += [pltpu.VMEM(outs[i][0], outs[i][1]) for i in early]
+    if extra:
+        extra.append(pltpu.SemaphoreType.DMA((len(extra),)))
+
+    def body(*refs):
+        refs = list(refs)
+        held = refs[len(ins) + len(outs) + len(scratch) :]
+        refs = refs[: len(ins) + len(outs) + len(scratch)]
+        for j, i in enumerate(late):
+            refs[i] = Late(refs[i], held[j], held[-1].at[j])
+        for j, i in enumerate(early, len(late)):
+            refs[len(ins) + i] = Early(held[j], refs[len(ins) + i], held[-1].at[j])
+        kernel(*refs)
+        for i in early:
+            refs[len(ins) + i].copy.wait()
+
     return pl.pallas_call(
-        kernel,
+        body,
         name=name,
         in_specs=[space[s] for _, s in ins],
         out_specs=[space[s] for _, _, s in outs],
         out_shape=[jax.ShapeDtypeStruct(s, d) for s, d, _ in outs],
-        scratch_shapes=scratch,
+        scratch_shapes=list(scratch) + extra,
         compiler_params=pltpu.CompilerParams(vmem_limit_bytes=VMEM_LIMIT),
         cost_estimate=pl.CostEstimate(
             flops=micros * 10**9, bytes_accessed=micros * 3 * 10**6, transcendentals=0
@@ -513,15 +555,19 @@
     def kernel(*refs):
         meta, vec, stream, q, kv, kvo = refs[:6]
         bufs = refs[6 : 6 + nw]
-        mixed, out, prob, w, sums, spreads, acc, sems = refs[6 + nw :]
-        copies = weight_copies(meta, bufs, [w], sems, sz["n"])
+        mixed_out, out, prob_out, w, sums, spreads, acc, sems = refs[6 + nw :]
+        mixed, prob = mixed_out.ref, prob_out.ref
+        copies = weight_copies(meta, bufs, [w], sems, sz["n"], first_column=512)
         start_all(copies)
         head_sums(sums)
         head_spreads(spreads)
-        for h, ref in enumerate((kv, kvo)):
+        for h in range(2):
+            if h == 1:
+                kvo = kvo.get()
+            ref = (kv, kvo)[h]
 
             @pl.loop(0, 4)
-            def _(g):
+            def _(g, ref=ref, h=h):
                 prob[4 * h + g] = pair_sums(q, ref, 0, g, sums) * SCALING
 
         @pl.loop(0, 13)
@@ -534,6 +580,7 @@
             for g in range(8):
                 prob[g, at, :] = e[g] * inv
 
+        prob_out.send()
         acc[...] = jnp.zeros_like(acc)
         for h, ref in enumerate((kv, kvo)):
 
@@ -551,12 +598,13 @@
 
         for j in range(6):
             mixed[j] = acc[:, 128 * j : 128 * j + 128].astype(B16)
+        mixed_out.send()
         wait_all(copies)
-        project_out(mixed, w, stream, vec[2:3, :], out)
-
-    ins = [(meta, "s"), (vec, "v"), (stream, "v"), (q, "v"), (kv, "v"), (kvo, "v")]
+        project_out(mixed, w, stream.get(), vec[2:3, :], out)
+
+    ins = [(meta, "s"), (vec, "v"), (stream, "l"), (q, "v"), (kv, "v"), (kvo, "l")]
     ins += [(w, "a") for w in weights]
-    outs = [((6, rows, 128), B16, "v"), ((rows, d), F32, "v"), ((8, 208, 128), F32, "v")]
+    outs = [((6, rows, 128), B16, "e"), ((rows, d), F32, "v"), ((8, 208, 128), F32, "e")]
     scratch = [
         pltpu.VMEM((4, d, d), B16),
         pltpu.VMEM((4 * d, 128), B16),
@@ -604,34 +652,41 @@
     def kernel(*refs):
         meta, vec, stream, q, kv = refs[:5]
         bufs = refs[5 : 5 + nw]
-        mixed, logs, out, w, sems = refs[5 + nw :]
-        copies = weight_copies(meta, bufs, [w], sems, sz["n"])
+        mixed_out, logs, out, w, sems = refs[5 + nw :]
+        mixed = mixed_out.ref
+        copies = weight_copies(meta, bufs, [w], sems, sz["n"], first_column=512)
         start_all(copies)
+
+        def mix(j, f):
+            at = row_slices(f)
+            qj, kj, vj = q[j, at, :], kv[j, at, :], kv[6 + j, at, :]
+            mask = space_mask(places)
+            o = None
+            for h, keep in enumerate((keep_low, keep_high)):
+                s = jnp.where(mask, dot_nt(kj, keep(qj)) * SCALING, NEGATIVE)
+                top = jnp.max(s, axis=0, keepdims=True)
+                e = jnp.exp(s - top)
+                size = jnp.sum(e, axis=0, keepdims=True)
+                logs[j * 4 + f, h : h + 1, :] = top + jnp.log(size)
+                part = dot_tn((e * (1.0 / size)).astype(B16), keep(vj))
+                o = part if o is None else o + part
+            return o.astype(B16)
 
         @pl.loop(0, 6)
         def _(j):
-            @pl.loop(0, 4)
-            def _(f):
-                at = row_slices(f)
-                qj, kj, vj = q[j, at, :], kv[j, at, :], kv[6 + j, at, :]
-                mask = space_mask(places)
-                o = None
-                for h, keep in enumerate((keep_low, keep_high)):
-                    s = jnp.where(mask, dot_nt(kj, keep(qj)) * SCALING, NEGATIVE)
-                    top = jnp.max(s, axis=0, keepdims=True)
-                    e = jnp.exp(s - top)
-                    size = jnp.sum(e, axis=0, keepdims=True)
-                    logs[j * 4 + f, h : h + 1, :] = top + jnp.log(size)
-                    part = dot_tn((e * (1.0 / size)).astype(B16), keep(vj))
-                    o = part if o is None else o + part
-                mixed[j, at, :] = o.astype(B16)
-
+            @pl.loop(0, 2)
+            def _(g):
+                pair = [mix(j, 2 * g + i) for i in range(2)]
+                for i in range(2):
+                    mixed[j, row_slices(2 * g + i), :] = pair[i]
+
+        mixed_out.send()
         wait_all(copies)
-        project_out(mixed, w, stream, vec[5:6, :], out)
-
-    ins = [(meta, "s"), (vec, "v"), (stream, "v"), (q, "v"), (kv, "v")]
+        project_out(mixed, w, stream.get(), vec[5:6, :], out)
+
+    ins = [(meta, "s"), (vec, "v"), (stream, "l"), (q, "v"), (kv, "v")]
     ins += [(w, "a") for w in weights]
-    outs = [((6, rows, 128), B16, "v"), ((24, 8, 208), F32, "v"), ((rows, d), F32, "v")]
+    outs = [((6, rows, 128), B16, "e"), ((24, 8, 208), F32, "v"), ((rows, d), F32, "v")]
     scratch = [pltpu.VMEM((4, d, d), B16), copy_sems(sz, 1)]
     return run(kernel, "space_mix", ins, outs, scratch, 17)
 
@@ -663,7 +718,7 @@
         res, refs = refs[:nb], refs[nb:]
         d2, vgrad = refs[0], refs[1]
         g_bufs, refs = refs[2 : 2 + ng], refs[2 + ng :]
-        w1, w2, dw1, dw2, dz, dzr, normed, act, dpre, y, dn, sems = refs
+        w1, w2, dw1, dw2, dz, dzr, normed, act, dpre, y, dn, sems, back_sems = refs
         copies = weight_copies(meta, bufs, [w1, w2], sems, sz["n"])
         start_all(copies)
         take_blocks(blks, dz, places)
@@ -680,10 +735,20 @@
             y[at, :] = stream[at, :] + vec[8:9, :]
             dn[at, :] = jnp.zeros_like(up)
 
-        wait_all(copies)
+        back = weight_copies(meta, g_bufs, [dw1, dw2], back_sems, sz["n"], back=True)
+        group = len(copies) // 4
+        if not fast:
+            wait_all(copies)
 
         @pl.loop(0, 4)
-        def _(t):
+        def _(k):
+            t = k
+            if fast:
+                t = 2 * (meta[0] ^ (k // 2)) + (meta[2] ^ (k % 2))
+                rows_here = w1.shape[1] // (2 * sz["n"])
+                piece = (bufs[0].at[0, 0:rows_here, :], w1.at[0, 0:rows_here, :])
+                for i in range(group):
+                    pltpu.make_async_copy(*piece, sems.at[k * group + i]).wait()
             thirds = [slice(256 * i, 256 * i + 256) for i in range(3)]
             for cols in thirds:
                 pre = dot(normed[...], w1[t, :, cols]) + vec[pl.ds(9 + t, 1), cols]
@@ -698,9 +763,12 @@
             for cols in thirds:
                 dw1[t, :, cols] = dot_tn(normed[...], dpre[:, cols]).astype(B16)
                 dw2[t, :, cols] = dot_tn(dzr[...], act[:, cols]).astype(B16)
-
-        back = weight_copies(meta, g_bufs, [dw1, dw2], sems, sz["n"], back=True)
-        start_all(back)
+            if fast:
+                for i in range(4):
+                    pl.when(k == i)(lambda i=i: start_all(back[i * group : i * group + group]))
+
+        if not fast:
+            start_all(back)
         give_blocks(y, res, places)
 
         @pl.loop(0, 4)
@@ -720,7 +788,7 @@
     scratch = [pltpu.VMEM((4, d, d), B16)] * 4
     scratch += [pltpu.VMEM((rows, d), F32), pltpu.VMEM((rows, d), B16), pltpu.VMEM((rows, d), B16)]
     scratch += [pltpu.VMEM((rows, d), B16)] * 2 + [pltpu.VMEM((rows, d), F32)] * 2
-    scratch += [copy_sems(sz, 2)]
+    scratch += [copy_sems(sz, 2)] * 2
     r = run(kernel, "feed_forward", ins, outs, scratch, 47)
     return r[:nb], r[nb], r[nb + 1], r[nb + 2 :]
 
@@ -744,28 +812,29 @@
     dy[2 * u + 1, at, 512:640] = keep_low(v)
 
 
-def head_gradients(dw, normed, up, dy, mixed):
-    @pl.loop(0, 2)
-    def _(u):
-        for odd in range(2):
-            t = 2 * u + odd
-            dw[t, :, 0:512] = dot_tn(normed[...], dy[t, :, 0:512]).astype(B16)
-            m2 = jnp.concatenate([mixed[t], third_head(mixed[4 + u], odd)], axis=1)
-            out = dot_tn(up[...], m2)
-            dw[t, :, 512:640] = out[:, 0:128].astype(B16)
-            third = dot_tn(normed[...], dy[t, :, 512:640])
-            dw[t, :, 640:768] = (out[:, 128:256] + third).astype(B16)
-
-
-def norm_slopes(dy, w_ref, out):
+def third_head_of(v, odd):
+    return jnp.where(low_lanes(v.shape) == (odd == 0), v, jnp.zeros_like(v))
+
+
+def output_gradients(dw, up, mixed):
+    @pl.loop(0, 4)
+    def _(t):
+        third = third_head_of(mixed[4 + t // 2], t % 2)
+        out = dot_tn(up[...], jnp.concatenate([mixed[t], third], axis=1))
+        dw[t, :, 512:768] = out.astype(B16)
+
+
+def head_gradients(t, dw, normed, dy):
+    dw[t, :, 0:512] = dot_tn(normed[...], dy[t, :, 0:512]).astype(B16)
+    third = dot_tn(normed[...], dy[t, :, 512:640])
+    dw[t, :, 640:768] = (dw[t, :, 640:768].astype(F32) + third).astype(B16)
+
+
+def norm_slopes(t, dy, w_ref, out):
     for n in range(3):
         cols = slice(256 * n, 256 * n + 256)
-        acc = None
-        for t in range(4):
-            part = dot_nt(dy[t, :, 0:512], w_ref[t, cols, 0:512])
-            part = part + dot_nt(dy[t, :, 512:640], w_ref[t, cols, 640:768])
-            acc = part if acc is None else acc + part
-        out[:, cols] = acc
+        part = dot_nt(dy[t, :, 0:512], w_ref[t, cols, 0:512])
+        out[:, cols] += part + dot_nt(dy[t, :, 512:640], w_ref[t, cols, 640:768])
 
 
 def space_backward_scores(sz, meta, d2, q, kv, logs, weights):
@@ -775,8 +844,9 @@
     def kernel(*refs):
         meta, d2, q, kv, logs = refs[:5]
         bufs, refs = refs[5 : 5 + nw], refs[5 + nw :]
-        up, dy, w, dm, third, sems = refs
-        copies = weight_copies(meta, bufs, [w], sems, sz["n"])
+        up_out, dy, w, dm, third, sems = refs
+        up = up_out.ref
+        copies = weight_copies(meta, bufs, [w], sems, sz["n"], first_column=512)
         start_all(copies)
 
         @pl.loop(0, 4)
@@ -784,7 +854,9 @@
             up[row_slices(r), :] = d2[row_slices(r), :].astype(B16)
 
         wait_all(copies)
+        up_out.send()
         mixed_slopes(up, w, dm)
+        q, kv, logs = q.get(), kv.get(), logs.get()
 
         def slopes(j, at, f):
             qj, kj, vj, mj = q[j, at, :], kv[j, at, :], kv[6 + j, at, :], dm[j, at, :]
@@ -803,23 +875,26 @@
 
         @pl.loop(0, 4)
         def _(j):
-            @pl.loop(0, 4)
-            def _(f):
-                at = row_slices(f)
-                dq, dk, dv = slopes(j, at, f)
-                dy[j, at, 0:128] = dq
-                dy[j, at, 128:256] = dk
-                dy[j, at, 256:384] = dv
+            @pl.loop(0, 2)
+            def _(g):
+                ats = [row_slices(2 * g + i) for i in range(2)]
+                pair = [slopes(j, ats[i], 2 * g + i) for i in range(2)]
+                for at, (dq, dk, dv) in zip(ats, pair):
+                    dy[j, at, 0:128] = dq
+                    dy[j, at, 128:256] = dk
+                    dy[j, at, 256:384] = dv
 
         @pl.loop(0, 2)
         def _(u):
-            @pl.loop(0, 4)
-            def _(f):
-                at = row_slices(f)
-                place_third(*slopes(4 + u, at, f), dy, u, at)
-
-    ins = [(meta, "s")] + [(v, "v") for v in (d2, q, kv, logs)] + [(w, "a") for w in weights]
-    outs = [((rows, d), B16, "v"), ((4, rows, 640), B16, "v")]
+            @pl.loop(0, 2)
+            def _(g):
+                ats = [row_slices(2 * g + i) for i in range(2)]
+                pair = [slopes(4 + u, ats[i], 2 * g + i) for i in range(2)]
+                for at, v in zip(ats, pair):
+                    place_third(*v, dy, u, at)
+
+    ins = [(meta, "s")] + [(d2, "v")] + [(v, "l") for v in (q, kv, logs)] + [(w, "a") for w in weights]
+    outs = [((rows, d), B16, "e"), ((4, rows, 640), B16, "v")]
     scratch = [pltpu.VMEM((4, d, d), B16), pltpu.VMEM((6, rows, 128), B16)]
     scratch += [pltpu.VMEM((rows, 128), B16), copy_sems(sz, 1)]
     return run(kernel, "space_backward_scores", ins, outs, scratch, 30)
@@ -833,7 +908,7 @@
     def kernel(*refs):
         meta, up, normed, mixed = refs[:4]
         given, refs = refs[4 : 4 + len(slopes)], refs[4 + len(slopes) :]
-        dy = refs[0] if join else given[0]
+        dy = refs[0].ref if join else given[0]
         g_bufs, (dw, sems) = refs[1 if join else 0 : -2], refs[-2:]
         if join:
             dq, dkv, got = given
@@ -851,13 +926,29 @@
                 for u in range(2):
                     place_third(dq[4 + u, at, :], both(4 + u, at), both(10 + u, at), dy, u, at)
 
-        head_gradients(dw, normed, up, dy, mixed)
+            refs[0].send()
         back = weight_copies(meta, g_bufs, [dw], sems, sz["n"], back=True, shifts=join)
-        start_all(back)
+        group = len(back) // 4
+        output_gradients(dw, up.get(), mixed.get())
+        normed = normed.get()
+        if not join:
+            dy = dy.get()
+
+        @pl.loop(0, 4)
+        def _(k):
+            t = 2 * (meta[0] ^ (k // 2)) + (meta[2] ^ (k % 2)) if fast else k
+            head_gradients(t, dw, normed, dy)
+            if fast:
+                for i in range(4):
+                    pl.when(k == i)(lambda i=i: start_all(back[i * group : i * group + group]))
+
+        if not fast:
+            start_all(back)
         wait_all(back)
 
-    ins = [(meta, "s")] + [(v, "v") for v in (up, normed, mixed, *slopes)]
-    outs = ([((4, rows, 640), B16, "v")] if join else []) + g_outs
+    ins = [(meta, "s")] + [(v, "l") for v in (up, normed, mixed)]
+    ins += [(v, "v" if join else "l") for v in slopes]
+    outs = ([((4, rows, 640), B16, "e")] if join else []) + g_outs
     scratch = [pltpu.VMEM((4, d, d), B16), copy_sems(sz, 1)]
     return run(kernel, name, ins, outs, scratch, 14)
 
@@ -877,8 +968,24 @@
         copies = weight_copies(meta, bufs, [w], sems, sz["n"])
         start_all(copies)
         vgrad[...] = jnp.zeros_like(vgrad)
-        wait_all(copies)
-        norm_slopes(dy, w, dn)
+        dn[...] = jnp.zeros_like(dn)
+        fast = nw > 1
+        group = len(copies) // 4
+        if not fast:
+            wait_all(copies)
+
+        @pl.loop(0, 4)
+        def _(k):
+            t = k
+            if fast:
+                t = 2 * (meta[0] ^ (k // 2)) + (meta[2] ^ (k % 2))
+                rows_here = w.shape[1] // (2 * sz["n"])
+                piece = (bufs[0].at[0, 0:rows_here, :], w.at[0, 0:rows_here, :])
+                for i in range(group):
+                    pltpu.make_async_copy(*piece, sems.at[k * group + i]).wait()
+            norm_slopes(t, dy, w, dn)
+
+        up, stream = up.get(), stream.get()
 
         @pl.loop(0, 4)
         def _(r):
@@ -894,7 +1001,8 @@
         if blocks:
             give_blocks(dx, outs, places)
 
-    ins = [(meta, "s")] + [(v, "v") for v in (vec, up, stream, dy)] + [(w, "a") for w in weights]
+    ins = [(meta, "s"), (vec, "v"), (up, "l"), (stream, "l"), (dy, "v")]
+    ins += [(w, "a") for w in weights]
     outs = [((rows, d), F32, "v")]
     scratch = []
     if blocks:
@@ -912,8 +1020,9 @@
     def kernel(*refs):
         meta, d1, q, kv, kvo, prob = refs[:6]
         bufs, refs = refs[6 : 6 + nw], refs[6 + nw :]
-        up, dq, dkv, dkvo, w, dm, sums, spreads, ds, acc, sems = refs
-        copies = weight_copies(meta, bufs, [w], sems, sz["n"])
+        up_out, dq, dkv_out, dkvo, w, dm, sums, spreads, ds, acc, sems = refs
+        up, dkv = up_out.ref, dkv_out.ref
+        copies = weight_copies(meta, bufs, [w], sems, sz["n"], first_column=512)
         start_all(copies)
         head_sums(sums)
         head_spreads(spreads)
@@ -923,7 +1032,9 @@
             up[row_slices(r), :] = d1[row_slices(r), :].astype(B16)
 
         wait_all(copies)
+        up_out.send()
         mixed_slopes(up, w, dm)
+        q, kv, kvo, prob = q.get(), kv.get(), kvo.get(), prob.get()
         for h, ref in enumerate((kv, kvo)):
 
             @pl.loop(0, 4)
@@ -962,14 +1073,17 @@
                         out[2 * jj + i, at, :] = dk[:, 128 * i : 128 * i + 128]
                         out[6 + 2 * jj + i, at, :] = dv[:, 128 * i : 128 * i + 128]
 
+            if h == 0:
+                dkv_out.send()
+
         for j in range(6):
             dq[j] = acc[:, 128 * j : 128 * j + 128].astype(B16)
 
-    ins = [(meta, "s")] + [(v, "v") for v in (d1, q, kv, kvo, prob)] + [(w, "a") for w in weights]
+    ins = [(meta, "s")] + [(d1, "v")] + [(v, "l") for v in (q, kv, kvo, prob)] + [(w, "a") for w in weights]
     outs = [
-        ((rows, d), B16, "v"),
+        ((rows, d), B16, "e"),
         ((6, rows, 128), B16, "v"),
-        ((12, rows, 128), B16, "v"),
+        ((12, rows, 128), B16, "e"),
         ((12, rows, 128), B16, "v"),
     ]
     scratch = [

time: 419 us -> 400 us (0.955)
  Pallas kernels: 237 us -> 215 us
  waiting for transfers between devices: 53.3 us -> 57.6 us
    pallas_call x12, Pallas kernels: 210 us -> 188 us  [run(): pl.pallas_call(body, name=name, in_specs=[space[s] for _, s in ins], out_...]
  transfers between devices with their start and end apart: 65 -> 65, of which waited for: 17 -> 22; matrix products, arithmetic and copies ran while one was open for 6% -> 6% of each run, Pallas kernels for 47% -> 44%
where the time goes in v2:
time: 400 us; the launch traced here: 395 us
  Pallas kernels  215 us (54%)
  starting transfers between devices  79.1 us (20%)
  waiting for transfers between devices  57.6 us (14%)
  local copies, waits for them, and re-layouts  34.9 us (9%)
  other arithmetic  6.43 us (2%)
    pallas_call x12, Pallas kernels, run(): pl.pallas_call(body, name=name, in_specs=[space[s] for _, s in ins], out_...  188 us
    pallas_call x9, Pallas kernels, block_sums(): pl.pallas_call(kernel, name=name, grid=(1,), in_specs=[spec(blocks, index...  26.8 us
    all_to_all x5, starting transfers between devices, over_z(): return lax.all_to_all(v, 'shard', split_axis=0, concat_axis=0, tiled=True)  25.3 us
    ppermute x16, waiting for transfers between devices, over_x(): return lax.ppermute(v, 'x', FLIP)  18.4 us
    ppermute x16, starting transfers between devices, over_x(): return lax.ppermute(v, 'x', FLIP)  16.2 us
    ppermute x16, starting transfers between devices, over_y(): return lax.ppermute(v, 'ctx', FLIP)  15.6 us
    all_to_all x5, waiting for transfers between devices, over_z(): return lax.all_to_all(v, 'shard', split_axis=0, concat_axis=0, tiled=True)  14.4 us
    ppermute x16, waiting for transfers between devices, over_y(): return lax.ppermute(v, 'ctx', FLIP)  13.1 us
  transfers between devices with their start and end apart: 65, of which 22 were waited for; matrix products, arithmetic and copies ran while one was open for 6% of the time, Pallas kernels for 44%

profile of v2, /device:TPU:0, one launch (start us, length us, event | category | flops | bytes accessed | tf_op | source)
XLA Modules:
  0.0 394.8 jit_solution(4068989060773584356)
XLA Ops:
  4.5 6.3 %all-to-all-start = ((bf16[4,1,104,768]{3,2,1,0:T(8,128)(2,1)}), bf16[4,1,104,768]{3,2,1,0:T(8,128)(2,1)S(1)}, u32[]{:S(2)}, u32[]{:S(2)}) async-start(bf16[4,1,104,768]{3,2,1,0:T(8,128)(2,1)} %broadcast_in_dim.68), calls=%async_computation | async-start | bytes 1277952 | tf_op jit(solution)/shard_map/all_to_all | solution.py:41
  11.7 1.6 collective-permute-start.3
  13.3 1.6 collective-permute-start.4
  17.8 2.5 collective-permute-start.2
  21.3 6.5 %all-to-all-done = bf16[4,1,104,768]{3,2,1,0:T(8,128)(2,1)S(1)} async-done(((bf16[4,1,104,768]{3,2,1,0:T(8,128)(2,1)}), bf16[4,1,104,768]{3,2,1,0:T(8,128)(2,1)S(1)}, u32[]{:S(2)}, u32[]{:S(2)}) %all-to-all-start) | async-done | bytes 639008 | tf_op jit(solution)/shard_map/all_to_all | solution.py:41
  27.8 4.1 %all-to-all-start.1 = ((bf16[4,1,96,768]{3,2,1,0:T(8,128)(2,1)}), bf16[4,1,96,768]{3,2,1,0:T(8,128)(2,1)}, u32[]{:S(2)}, u32[]{:S(2)}) async-start(bf16[4,1,96,768]{3,2,1,0:T(8,128)(2,1)} %broadcast_in_dim.69), calls=%async_computation.1 | async-start | bytes 1179648 | tf_op jit(solution)/shard_map/all_to_all | solution.py:41
  32.0 3.9 collective-permute-done.1.refs_5_
  38.0 12.6 %collective-permute-done.5.refs_2_.refs_7_.refs_6_ = bf16[4,104,768]{2,1,0:T(8,128)(2,1)S(1)} collective-permute-done((bf16[4,104,768]{2,1,0:T(8,128)(2,1)S(1)}, bf16[4,104,768]{2,1,0:T(8,128)(2,1)S(1)}, u32[]{:S(2)}, u32[]{:S(2)}) %collective-permute-start.5) | collective-permute-done | bytes 639008 | tf_op jit(solution)/shard_map/ppermute | solution.py:25
  54.7 5.4 %all-to-all-start.2 = ((bf16[4,2,96,768]{3,2,1,0:T(8,128)(2,1)}), bf16[4,2,96,768]{3,2,1,0:T(8,128)(2,1)}, u32[]{:S(2)}, u32[]{:S(2)}) async-start(bf16[4,2,96,768]{3,2,1,0:T(8,128)(2,1)} %broadcast_in_dim.70), calls=%async_computation.2 | async-start | bytes 2359296 | tf_op jit(solution)/shard_map/all_to_all | solution.py:41
  61.4 2.2 collective-permute-start.14
  66.3 3.0 norm_vectors.1.refs_1_
  69.3 3.7 collective-permute-done.14.refs_5_
  73.1 10.3 %time_qkv.1 = (f32[832,768]{1,0:T(8,128)}, bf16[832,768]{1,0:T(8,128)(2,1)}, bf16[6,832,128]{2,1,0:T(8,128)(2,1)}, bf16[12,832,128]{2,1,0:T(8,128)(2,1)}) custom-call(s32[4]{0:T(128)} %pad_add_fusion.refs_0_, f32[16,768]{1,0:T(8,128)} %norm_vectors.1.refs_1_, bf16[2,98,768]{2,1,0:T(8,128)(2,1)} %bitcast.108, ...), custom_call_target="tpu_custom_call" | custom-call | flops 12000000000 | bytes 36000000 | tf_op jit(solution)/shard_map/time_qkv/pallas_call | solution.py:414
  84.8 4.0 %all-to-all-done.2 = bf16[4,2,96,768]{3,2,1,0:T(8,128)(2,1)} async-done(((bf16[4,2,96,768]{3,2,1,0:T(8,128)(2,1)}), bf16[4,2,96,768]{3,2,1,0:T(8,128)(2,1)}, u32[]{:S(2)}, u32[]{:S(2)}) %all-to-all-start.2) | async-done | bytes 1179680 | tf_op jit(solution)/shard_map/all_to_all | solution.py:41
  93.7 5.6 %collective-permute-done.18.refs_6_.refs_8_ = bf16[2,96,768]{2,1,0:T(8,128)(2,1)S(1)} collective-permute-done((bf16[2,96,768]{2,1,0:T(8,128)(2,1)S(1)}, bf16[2,96,768]{2,1,0:T(8,128)(2,1)S(1)}, u32[]{:S(2)}, u32[]{:S(2)}) %collective-permute-start.18) | collective-permute-done | bytes 294944 | tf_op jit(solution)/shard_map/ppermute | solution.py:29
  99.3 2.2 collective-permute-done.19.refs_7_.refs_9_
  105.5 15.4 %time_mix.1 = (bf16[6,832,128]{2,1,0:T(8,128)(2,1)}, f32[832,768]{1,0:T(8,128)}, f32[8,208,128]{2,1,0:T(8,128)}) custom-call(s32[4]{0:T(128)} %pad_add_fusion.refs_0_, f32[16,768]{1,0:T(8,128)} %norm_vectors.1.refs_1_, f32[832,768]{1,0:T(8,128)} %get-tuple-element.153.refs_2_.refs_3_, bf16[6,832,128]{2,1,0:T(8,128)(2,1)} %get-tuple-element.154.refs_3_.refs_2_, ...), custom_call_target="tpu_custom_call" | custom-call | flops 16999999488 | bytes 51000000 | tf_op jit(solution)/shard_map/time_mix/pallas_call | solution.py:414
  121.0 10.8 %space_qkv.1 = (bf16[832,768]{1,0:T(8,128)(2,1)}, bf16[6,832,128]{2,1,0:T(8,128)(2,1)}, bf16[12,832,128]{2,1,0:T(8,128)(2,1)}) custom-call(s32[4]{0:T(128)} %pad_add_fusion.refs_0_, f32[16,768]{1,0:T(8,128)} %norm_vectors.1.refs_1_, f32[832,768]{1,0:T(8,128)} %get-tuple-element.162.refs_2_.refs_3_, bf16[4,96,768]{2,1,0:T(8,128)(2,1)} %bitcast.18.refs_3_.refs_5_, ...), custom_call_target="tpu_custom_call" | custom-call | flops 12000000000 | bytes 36000000 | tf_op jit(solution)/shard_map/space_qkv/pallas_call | solution.py:414
  132.6 1.9 slice.229
  134.6 1.9 slice.230
  139.1 15.3 %space_mix.1 = (bf16[6,832,128]{2,1,0:T(8,128)(2,1)}, f32[24,8,208]{2,1,0:T(8,128)}, f32[832,768]{1,0:T(8,128)}) custom-call(s32[4]{0:T(128)} %pad_add_fusion.refs_0_, f32[16,768]{1,0:T(8,128)} %norm_vectors.1.refs_1_, f32[832,768]{1,0:T(8,128)} %get-tuple-element.162.refs_2_.refs_3_, bf16[6,832,128]{2,1,0:T(8,128)(2,1)} %get-tuple-element.165.refs_3_.refs_2_, ...), custom_call_target="tpu_custom_call" | custom-call | flops 16999999488 | bytes 51000000 | tf_op jit(solution)/shard_map/space_mix/pallas_call | solution.py:414
  155.0 1.7 copy.144
  157.7 37.6 %feed_forward.1 = (bf16[2,98,768]{2,1,0:T(8,128)(2,1)}, bf16[2,98,768]{2,1,0:T(8,128)(2,1)}, bf16[2,98,768]{2,1,0:T(8,128)(2,1)}, bf16[2,98,768]{2,1,0:T(8,128)(...) custom-call(s32[4]{0:T(128)} %pad_add_fusion.refs_0_, ...), custom_call_target="tpu_custom_call" | custom-call | flops 46999998464 | bytes 141000000 | tf_op jit(solution)/shard_map/feed_forward/pallas_call | solution.py:414
  199.0 23.7 %space_backward_scores.1 = (bf16[832,768]{1,0:T(8,128)(2,1)}, bf16[4,832,640]{2,1,0:T(8,128)(2,1)}) custom-call(s32[4]{0:T(128)} %pad_add_fusion.refs_0_, f32[832,768]{1,0:T(8,128)} %get-tuple-element.195.refs_1_.refs_2_, bf16[6,832,128]{2,1,0:T(8,128)(2,1)} %get-tuple-element.165.refs_3_.refs_2_, bf16[12,832,128]{2,1,0:T(8,128)(2,1)} %get-tuple-element.169.refs_4_.refs_3_, ...), custom_call_target="tpu_custom_call" | custom-call | flops 30000001024 | bytes 90000000 | tf_op jit(solution)/shard_map/space_backward_scores/pallas_call | solution.py:414
  222.7 2.7 mlp_rest.1
  227.4 12.2 %space_weights.1 = (bf16[16,96,768]{2,1,0:T(8,128)(2,1)}, bf16[16,96,768]{2,1,0:T(8,128)(2,1)}) custom-call(s32[4]{0:T(128)} %pad_add_fusion.refs_0_, bf16[832,768]{1,0:T(8,128)(2,1)} %get-tuple-element.175.refs_1_, bf16[832,768]{1,0:T(8,128)(2,1)} %get-tuple-element.176.refs_2_, bf16[6,832,128]{2,1,0:T(8,128)(2,1)} %get-tuple-element.177.refs_3_, ...), custom_call_target="tpu_custom_call" | custom-call | flops 14000000000 | bytes 42000000 | tf_op jit(solution)/shard_map/space_weights/pallas_call | solution.py:414
  241.5 4.5 %mlp_xy.1 = (bf16[8,96,768]{2,1,0:T(8,128)(2,1)}, bf16[8,96,768]{2,1,0:T(8,128)(2,1)}) custom-call(bf16[32,96,768]{2,1,0:T(8,128)(2,1)} %get-tuple-element.183.refs_0_.refs_2_.refs_3_.refs_4_.refs_8_.refs_12_.refs_16_.refs_20_.refs_24_.refs_28_, ...), custom_call_target="tpu_custom_call" | custom-call | flops 100000000 | bytes 100000 | tf_op jit(solution)/shard_map/mlp_xy/pallas_call | solution.py:104
  247.5 12.1 %space_input.1 = (f32[832,768]{1,0:T(8,128)}, f32[8,768]{1,0:T(8,128)}) custom-call(s32[4]{0:T(128)} %pad_add_fusion.refs_0_, f32[16,768]{1,0:T(8,128)} %norm_vectors.1.refs_1_, f32[832,768]{1,0:T(8,128)} %get-tuple-element.195.refs_1_.refs_2_, f32[832,768]{1,0:T(8,128)} %get-tuple-element.162.refs_2_.refs_3_, ...), custom_call_target="tpu_custom_call" | custom-call | flops 14000000000 | bytes 42000000 | tf_op jit(solution)/shard_map/space_input/pallas_call | solution.py:414
  259.7 2.1 space_rest.1
  264.3 20.7 %time_backward_scores.1 = (bf16[832,768]{1,0:T(8,128)(2,1)}, bf16[6,832,128]{2,1,0:T(8,128)(2,1)}, bf16[12,832,128]{2,1,0:T(8,128)(2,1)}, bf16[12,832,128]{2,1,0:T(8,128)(2,1)}) custom-call(s32[4]{0:T(128)} %pad_add_fusion.refs_0_, f32[832,768]{1,0:T(8,128)} %get-tuple-element.228.refs_1_.refs_2_, bf16[6,832,128]{2,1,0:T(8,128)(2,1)} %get-tuple-element.154.refs_3_.refs_2_, ...), custom_call_target="tpu_custom_call" | custom-call | flops 23000000512 | bytes 69000000 | tf_op jit(solution)/shard_map/time_backward_scores/pallas_call | solution.py:414
  285.1 2.8 mlp_z.1
  287.9 4.4 %all-to-all-start.3 = ((bf16[4,1,96,768]{3,2,1,0:T(8,128)(2,1)}), bf16[4,1,96,768]{3,2,1,0:T(8,128)(2,1)}, u32[]{:S(2)}, u32[]{:S(2)}) async-start(bf16[4,1,96,768]{3,2,1,0:T(8,128)(2,1)} %bitcast.94), calls=%async_computation.3 | async-start | bytes 1179648 | tf_op jit(solution)/shard_map/all_to_all | solution.py:41
  292.3 3.0 space_xy.1
  296.8 14.8 %time_weights.1 = (bf16[4,832,640]{2,1,0:T(8,128)(2,1)}, bf16[16,96,768]{2,1,0:T(8,128)(2,1)}, bf16[16,96,768]{2,1,0:T(8,128)(2,1)}) custom-call(s32[4]{0:T(128)} %pad_add_fusion.refs_0_, bf16[832,768]{1,0:T(8,128)(2,1)} %get-tuple-element.203.refs_1_, bf16[832,768]{1,0:T(8,128)(2,1)} %get-tuple-element.204.refs_2_, ...), custom_call_target="tpu_custom_call" | custom-call | flops 14000000000 | bytes 42000000 | tf_op jit(solution)/shard_map/time_weights/pallas_call | solution.py:414
  311.8 4.9 %collective-permute-done.48.refs_1_.refs_3_.refs_4_.refs_5_.refs_9_.refs_13_ = bf16[16,96,768]{2,1,0:T(8,128)(2,1)} collective-permute-done((bf16[16,96,768]{2,1,0:T(8,128)(2,1)}, bf16[16,96,768]{2,1,0:T(8,128)(2,1)}, u32[]{:S(2)}, u32[]{:S(2)}) %collective-permute-start.48) | collective-permute-done | bytes 2359328 | tf_op jit(solution)/shard_map/ppermute | solution.py:37
  316.6 2.1 time_rest.1
  326.8 4.0 %joint_z.1 = bf16[8,96,768]{2,1,0:T(8,128)(2,1)} custom-call(bf16[16,96,768]{2,1,0:T(8,128)(2,1)} %get-tuple-element.189.refs_0_.refs_2_.refs_3_.refs_4_.refs_8_.refs_12_, bf16[16,96,768]{2,1,0:T(8,128)(2,1)} %collective-permute-done.40.refs_1_.refs_3_.refs_4_.refs_5_.refs_9_.refs_13_, ...), custom_call_target="tpu_custom_call" | custom-call | flops 100000000 | bytes 100000 | tf_op jit(solution)/shard_map/joint_z/pallas_call | solution.py:104
  330.8 5.1 %all-to-all-start.4 = ((bf16[4,2,96,768]{3,2,1,0:T(8,128)(2,1)}), bf16[4,2,96,768]{3,2,1,0:T(8,128)(2,1)}, u32[]{:S(2)}, u32[]{:S(2)}) async-start(bf16[4,2,96,768]{3,2,1,0:T(8,128)(2,1)} %bitcast.93), calls=%async_computation.4 | async-start | bytes 2359296 | tf_op jit(solution)/shard_map/all_to_all | solution.py:41
  335.9 3.0 time_xy.1
  340.4 11.8 %time_input.1 = (f32[2,98,768]{2,1,0:T(8,128)}, bf16[2,98,768]{2,1,0:T(8,128)(2,1)}, bf16[2,98,768]{2,1,0:T(8,128)(2,1)}, bf16[2,98,768]{2,1,0:T(8,128)(2,1)}, f32[8,768]{1,0:T(8,128)}) custom-call(s32[4]{0:T(128)} %pad_add_fusion.refs_0_, f32[16,768]{1,0:T(8,128)} %norm_vectors.1.refs_1_, f32[832,768]{1,0:T(8,128)} %get-tuple-element.228.refs_1_.refs_2_, ...), custom_call_target="tpu_custom_call" | custom-call | flops 14000000000 | bytes 42000000 | tf_op jit(solution)/shard_map/time_input/pallas_call | solution.py:414
  354.1 2.6 time_z.1
  356.8 1.8 collective-permute-start.56
  358.6 2.4 collective-permute-start.57
  367.8 3.8 all-to-all-done.4
  372.7 2.6 all-to-all-start.5
  375.3 4.1 %collective-permute-start.58 = (bf16[1,96,768]{2,1,0:T(8,128)(2,1)S(1)}, bf16[1,96,768]{2,1,0:T(8,128)(2,1)S(1)}, u32[]{:S(2)}, u32[]{:S(2)}) collective-permute-start(bf16[1,96,768]{2,1,0:T(8,128)(2,1)S(1)} %copy-done.34), channel_id=1, source_target_pairs={{0,24},{8,0},{16,8},{24,16},{1,25},{9,1},{17,9},{25,17},{2,26},{10... | collective-permute-start | bytes 442376 | tf_op jit(solution)/shard_map/ppermute | solution.py:165
  380.7 2.0 all-to-all-done.5
  388.5 1.9 convert_reduce_fusion.1
  (285 shorter events, 77.4 us)
Async XLA Ops:
  4.5 23.3 %all-to-all-start = ((bf16[4,1,104,768]{3,2,1,0:T(8,128)(2,1)}), bf16[4,1,104,768]{3,2,1,0:T(8,128)(2,1)S(1)}, u32[]{:S(2)}, u32[]{:S(2)}) async-start(bf16[4,1,104,768]{3,2,1,0:T(8,128)(2,1)} %broadcast_in_dim.68), calls=%async_computation | async-start | bytes 1277952 | tf_op jit(solution)/shard_map/all_to_all | solution.py:41
  11.7 20.2 %collective-permute-start.3 = (bf16[2,98,768]{2,1,0:T(8,128)(2,1)S(1)}, bf16[2,98,768]{2,1,0:T(8,128)(2,1)}, u32[]{:S(2)}, u32[]{:S(2)}) collective-permute-start(bf16[2,98,768]{2,1,0:T(8,128)(2,1)S(1)} %bitcast.105), channel_id=1, source_target_pairs={{0,2},{2,0},{1,3},{3,1},{4,6},{6,4},{5,7},{7,5},{8,10},{10,8},{9,1... | collective-permute-start | bytes 903176 | tf_op jit(solution)/shard_map/ppermute | solution.py:25
  13.3 18.6 %collective-permute-start.4 = (bf16[2,98,768]{2,1,0:T(8,128)(2,1)S(1)}, bf16[2,98,768]{2,1,0:T(8,128)(2,1)}, u32[]{:S(2)}, u32[]{:S(2)}) collective-permute-start(bf16[2,98,768]{2,1,0:T(8,128)(2,1)S(1)} %bitcast.106), channel_id=1, source_target_pairs={{0,4},{4,0},{1,5},{5,1},{2,6},{6,2},{3,7},{7,3},{8,12},{12,8},{9,1... | collective-permute-start | bytes 903176 | tf_op jit(solution)/shard_map/ppermute | solution.py:29
  16.5 15.5 %collective-permute-start = (bf16[2,98,768]{2,1,0:T(8,128)(2,1)S(1)}, bf16[2,98,768]{2,1,0:T(8,128)(2,1)}, u32[]{:S(2)}, u32[]{:S(2)}) collective-permute-start(bf16[2,98,768]{2,1,0:T(8,128)(2,1)S(1)} %bitcast.107), channel_id=1, source_target_pairs={{0,2},{2,0},{1,3},{3,1},{4,6},{6,4},{5,7},{7,5},{8,10},{10,8},{9,1... | collective-permute-start | bytes 903176 | tf_op jit(solution)/shard_map/ppermute | solution.py:25
  17.1 18.8 %collective-permute-start.1 = (bf16[2,98,768]{2,1,0:T(8,128)(2,1)S(1)}, bf16[2,98,768]{2,1,0:T(8,128)(2,1)}, u32[]{:S(2)}, u32[]{:S(2)}) collective-permute-start(bf16[2,98,768]{2,1,0:T(8,128)(2,1)S(1)} %bitcast.110), channel_id=1, source_target_pairs={{0,4},{4,0},{1,5},{5,1},{2,6},{6,2},{3,7},{7,3},{8,12},{12,8},{9,1... | collective-permute-start | bytes 903176 | tf_op jit(solution)/shard_map/ppermute | solution.py:29
  17.8 18.2 %collective-permute-start.2 = (bf16[2,98,768]{2,1,0:T(8,128)(2,1)S(1)}, bf16[2,98,768]{2,1,0:T(8,128)(2,1)}, u32[]{:S(2)}, u32[]{:S(2)}) collective-permute-start(bf16[2,98,768]{2,1,0:T(8,128)(2,1)S(1)} %bitcast.111), channel_id=1, source_target_pairs={{0,6},{2,4},{4,2},{6,0},{1,7},{3,5},{5,3},{7,1},{8,14},{10,12},{12... | collective-permute-start | bytes 903176 | tf_op jit(solution)/shard_map/ppermute | solution.py:33
  27.8 26.9 %all-to-all-start.1 = ((bf16[4,1,96,768]{3,2,1,0:T(8,128)(2,1)}), bf16[4,1,96,768]{3,2,1,0:T(8,128)(2,1)}, u32[]{:S(2)}, u32[]{:S(2)}) async-start(bf16[4,1,96,768]{3,2,1,0:T(8,128)(2,1)} %broadcast_in_dim.69), calls=%async_computation.1 | async-start | bytes 1179648 | tf_op jit(solution)/shard_map/all_to_all | solution.py:41
  35.9 14.6 %collective-permute-start.5 = (bf16[4,104,768]{2,1,0:T(8,128)(2,1)S(1)}, bf16[4,104,768]{2,1,0:T(8,128)(2,1)S(1)}, u32[]{:S(2)}, u32[]{:S(2)}) collective-permute-start(bf16[4,104,768]{2,1,0:T(8,128)(2,1)S(1)} %bitcast.95), channel_id=1, source_target_pairs={{0,2},{2,0},{1,3},{3,1},{4,6},{6,4},{5,7},{7,5},{8,10},{10,8},{9,1... | collective-permute-start | bytes 1916936 | tf_op jit(solution)/shard_map/ppermute | solution.py:25
  37.1 14.7 %collective-permute-start.6 = (bf16[4,104,768]{2,1,0:T(8,128)(2,1)S(1)}, bf16[4,104,768]{2,1,0:T(8,128)(2,1)S(1)}, u32[]{:S(2)}, u32[]{:S(2)}) collective-permute-start(bf16[4,104,768]{2,1,0:T(8,128)(2,1)S(1)} %bitcast.96), channel_id=1, source_target_pairs={{0,4},{4,0},{1,5},{5,1},{2,6},{6,2},{3,7},{7,3},{8,12},{12,8},{9,1... | collective-permute-start | bytes 1916936 | tf_op jit(solution)/shard_map/ppermute | solution.py:29
  38.0 23.4 %collective-permute-start.9 = (bf16[4,104,768]{2,1,0:T(8,128)(2,1)S(1)}, bf16[4,104,768]{2,1,0:T(8,128)(2,1)}, u32[]{:S(2)}, u32[]{:S(2)}) collective-permute-start(bf16[4,104,768]{2,1,0:T(8,128)(2,1)S(1)} %bitcast.97), channel_id=1, source_target_pairs={{0,1},{1,0},{2,3},{3,2},{4,5},{5,4},{6,7},{7,6},{8,9},{9,8},{10,11... | collective-permute-start | bytes 1916936 | tf_op jit(solution)/shard_map/ppermute | solution.py:37
  53.0 13.3 %collective-permute-start.11 = (bf16[4,104,768]{2,1,0:T(8,128)(2,1)S(1)}, bf16[4,104,768]{2,1,0:T(8,128)(2,1)}, u32[]{:S(2)}, u32[]{:S(2)}) collective-permute-start(bf16[4,104,768]{2,1,0:T(8,128)(2,1)S(1)} %collective-permute-done.6.refs_3_.refs_8_.refs_7_), channel_id=1, source_target_pairs={{0,1},{1,0},{2,3},{3,2},{4,5},{5,4},{6,7},{7,6},{8,9},{9,8},{10,11... | collective-permute-start | bytes 1916936 | tf_op jit(solution)/shard_map/ppermute | solution.py:37
  54.7 34.2 %all-to-all-start.2 = ((bf16[4,2,96,768]{3,2,1,0:T(8,128)(2,1)}), bf16[4,2,96,768]{3,2,1,0:T(8,128)(2,1)}, u32[]{:S(2)}, u32[]{:S(2)}) async-start(bf16[4,2,96,768]{3,2,1,0:T(8,128)(2,1)} %broadcast_in_dim.70), calls=%async_computation.2 | async-start | bytes 2359296 | tf_op jit(solution)/shard_map/all_to_all | solution.py:41
  64.9 19.7 %collective-permute-start.15 = (bf16[4,96,768]{2,1,0:T(8,128)(2,1)}, bf16[4,96,768]{2,1,0:T(8,128)(2,1)}, u32[]{:S(2)}, u32[]{:S(2)}) collective-permute-start(bf16[4,96,768]{2,1,0:T(8,128)(2,1)} %bitcast.18.refs_3_.refs_5_), channel_id=1, source_target_pairs={{0,2},{2,0},{1,3},{3,1},{4,6},{6,4},{5,7},{7,5},{8,10},{10,8},{9,1... | collective-permute-start | bytes 1769480 | tf_op jit(solution)/shard_map/ppermute | solution.py:25
  65.5 19.3 %collective-permute-start.16 = (bf16[4,96,768]{2,1,0:T(8,128)(2,1)}, bf16[4,96,768]{2,1,0:T(8,128)(2,1)}, u32[]{:S(2)}, u32[]{:S(2)}) collective-permute-start(bf16[4,96,768]{2,1,0:T(8,128)(2,1)} %bitcast.18.refs_3_.refs_5_), channel_id=1, source_target_pairs={{0,4},{4,0},{1,5},{5,1},{2,6},{6,2},{3,7},{7,3},{8,12},{12,8},{9,1... | collective-permute-start | bytes 1769480 | tf_op jit(solution)/shard_map/ppermute | solution.py:29
  101.5 19.5 %collective-permute-start.21 = (bf16[4,96,768]{2,1,0:T(8,128)(2,1)}, bf16[4,96,768]{2,1,0:T(8,128)(2,1)}, u32[]{:S(2)}, u32[]{:S(2)}) collective-permute-start(bf16[4,96,768]{2,1,0:T(8,128)(2,1)} %collective-permute-done.15.refs_4_.refs_6_), channel_id=1, source_target_pairs={{0,1},{1,0},{2,3},{3,2},{4,5},{5,4},{6,7},{7,6},{8,9},{9,8},{10,11... | collective-permute-start | bytes 1769480 | tf_op jit(solution)/shard_map/ppermute | solution.py:37
  102.0 19.0 %collective-permute-start.22 = (bf16[4,96,768]{2,1,0:T(8,128)(2,1)}, bf16[4,96,768]{2,1,0:T(8,128)(2,1)}, u32[]{:S(2)}, u32[]{:S(2)}) collective-permute-start(bf16[4,96,768]{2,1,0:T(8,128)(2,1)} %collective-permute-done.16.refs_5_.refs_7_), channel_id=1, source_target_pairs={{0,1},{1,0},{2,3},{3,2},{4,5},{5,4},{6,7},{7,6},{8,9},{9,8},{10,11... | collective-permute-start | bytes 1769480 | tf_op jit(solution)/shard_map/ppermute | solution.py:37
  102.0 18.9 %collective-permute-start.24 = (bf16[2,96,768]{2,1,0:T(8,128)(2,1)}, bf16[2,96,768]{2,1,0:T(8,128)(2,1)}, u32[]{:S(2)}, u32[]{:S(2)}) collective-permute-start(bf16[2,96,768]{2,1,0:T(8,128)(2,1)} %collective-permute-done.19.refs_7_.refs_9_), channel_id=1, source_target_pairs={{0,1},{1,0},{2,3},{3,2},{4,5},{5,4},{6,7},{7,6},{8,9},{9,8},{10,11... | collective-permute-start | bytes 884744 | tf_op jit(solution)/shard_map/ppermute | solution.py:37
  102.5 29.3 %collective-permute-start.25 = (bf16[8,96,768]{2,1,0:T(8,128)(2,1)}, bf16[8,96,768]{2,1,0:T(8,128)(2,1)}, u32[]{:S(2)}, u32[]{:S(2)}) collective-permute-start(bf16[8,96,768]{2,1,0:T(8,128)(2,1)} %bitcast.24.refs_7_), channel_id=1, source_target_pairs={{0,2},{2,0},{1,3},{3,1},{4,6},{6,4},{5,7},{7,5},{8,10},{10,8},{9,1... | collective-permute-start | bytes 3538952 | tf_op jit(solution)/shard_map/ppermute | solution.py:25
  104.7 28.0 %collective-permute-start.26 = (bf16[8,96,768]{2,1,0:T(8,128)(2,1)}, bf16[8,96,768]{2,1,0:T(8,128)(2,1)}, u32[]{:S(2)}, u32[]{:S(2)}) collective-permute-start(bf16[8,96,768]{2,1,0:T(8,128)(2,1)} %bitcast.24.refs_7_), channel_id=1, source_target_pairs={{0,4},{4,0},{1,5},{5,1},{2,6},{6,2},{3,7},{7,3},{8,12},{12,8},{9,1... | collective-permute-start | bytes 3538952 | tf_op jit(solution)/shard_map/ppermute | solution.py:29
  120.9 35.9 %collective-permute-start.29 = (bf16[8,96,768]{2,1,0:T(8,128)(2,1)}, bf16[8,96,768]{2,1,0:T(8,128)(2,1)}, u32[]{:S(2)}, u32[]{:S(2)}) collective-permute-start(bf16[8,96,768]{2,1,0:T(8,128)(2,1)} %bitcast.24.refs_7_), channel_id=1, source_target_pairs={{0,1},{1,0},{2,3},{3,2},{4,5},{5,4},{6,7},{7,6},{8,9},{9,8},{10,11... | collective-permute-start | bytes 3538952 | tf_op jit(solution)/shard_map/ppermute | solution.py:37
  136.5 17.9 %collective-permute-start.27 = (bf16[4,96,768]{2,1,0:T(8,128)(2,1)}, bf16[4,96,768]{2,1,0:T(8,128)(2,1)}, u32[]{:S(2)}, u32[]{:S(2)}) collective-permute-start(bf16[4,96,768]{2,1,0:T(8,128)(2,1)} %slice.229), channel_id=1, source_target_pairs={{0,4},{4,0},{1,5},{5,1},{2,6},{6,2},{3,7},{7,3},{8,12},{12,8},{9,1... | collective-permute-start | bytes 1769480 | tf_op jit(solution)/shard_map/ppermute | solution.py:29
  137.3 17.1 %collective-permute-start.28 = (bf16[4,96,768]{2,1,0:T(8,128)(2,1)}, bf16[4,96,768]{2,1,0:T(8,128)(2,1)}, u32[]{:S(2)}, u32[]{:S(2)}) collective-permute-start(bf16[4,96,768]{2,1,0:T(8,128)(2,1)} %slice.230), channel_id=1, source_target_pairs={{0,2},{2,0},{1,3},{3,1},{4,6},{6,4},{5,7},{7,5},{8,10},{10,8},{9,1... | collective-permute-start | bytes 1769480 | tf_op jit(solution)/shard_map/ppermute | solution.py:25
  138.6 18.2 %collective-permute-start.30 = (bf16[8,96,768]{2,1,0:T(8,128)(2,1)}, bf16[8,96,768]{2,1,0:T(8,128)(2,1)}, u32[]{:S(2)}, u32[]{:S(2)}) collective-permute-start(bf16[8,96,768]{2,1,0:T(8,128)(2,1)} %collective-permute-done.25.refs_8_), channel_id=1, source_target_pairs={{0,1},{1,0},{2,3},{3,2},{4,5},{5,4},{6,7},{7,6},{8,9},{9,8},{10,11... | collective-permute-start | bytes 3538952 | tf_op jit(solution)/shard_map/ppermute | solution.py:37
  138.6 18.2 %collective-permute-start.31 = (bf16[8,96,768]{2,1,0:T(8,128)(2,1)}, bf16[8,96,768]{2,1,0:T(8,128)(2,1)}, u32[]{:S(2)}, u32[]{:S(2)}) collective-permute-start(bf16[8,96,768]{2,1,0:T(8,128)(2,1)} %collective-permute-done.26.refs_9_), channel_id=1, source_target_pairs={{0,1},{1,0},{2,3},{3,2},{4,5},{5,4},{6,7},{7,6},{8,9},{9,8},{10,11... | collective-permute-start | bytes 3538952 | tf_op jit(solution)/shard_map/ppermute | solution.py:37
  195.3 27.4 %collective-permute-start.37 = (bf16[32,96,768]{2,1,0:T(8,128)(2,1)}, bf16[32,96,768]{2,1,0:T(8,128)(2,1)}, u32[]{:S(2)}, u32[]{:S(2)}) collective-permute-start(bf16[32,96,768]{2,1,0:T(8,128)(2,1)} %get-tuple-element.184), channel_id=1, source_target_pairs={{0,1},{1,0},{2,3},{3,2},{4,5},{5,4},{6,7},{7,6},{8,9},{9,8},{10,11... | collective-permute-start | bytes 14155784 | tf_op jit(solution)/shard_map/ppermute | solution.py:37
  195.5 31.9 %collective-permute-start.34 = (bf16[2,98,768]{2,1,0:T(8,128)(2,1)}, bf16[2,98,768]{2,1,0:T(8,128)(2,1)}, u32[]{:S(2)}, u32[]{:S(2)}) collective-permute-start(bf16[2,98,768]{2,1,0:T(8,128)(2,1)} %get-tuple-element.180), channel_id=1, source_target_pairs={{0,2},{2,0},{1,3},{3,1},{4,6},{6,4},{5,7},{7,5},{8,10},{10,8},{9,1... | collective-permute-start | bytes 903176 | tf_op jit(solution)/shard_map/ppermute | solution.py:25
  196.3 31.1 %collective-permute-start.35 = (bf16[2,98,768]{2,1,0:T(8,128)(2,1)}, bf16[2,98,768]{2,1,0:T(8,128)(2,1)}, u32[]{:S(2)}, u32[]{:S(2)}) collective-permute-start(bf16[2,98,768]{2,1,0:T(8,128)(2,1)} %get-tuple-element.181), channel_id=1, source_target_pairs={{0,4},{4,0},{1,5},{5,1},{2,6},{6,2},{3,7},{7,3},{8,12},{12,8},{9,1... | collective-permute-start | bytes 903176 | tf_op jit(solution)/shard_map/ppermute | solution.py:29
  197.5 29.9 %collective-permute-start.36 = (bf16[2,98,768]{2,1,0:T(8,128)(2,1)}, bf16[2,98,768]{2,1,0:T(8,128)(2,1)}, u32[]{:S(2)}, u32[]{:S(2)}) collective-permute-start(bf16[2,98,768]{2,1,0:T(8,128)(2,1)} %get-tuple-element.182), channel_id=1, source_target_pairs={{0,6},{2,4},{4,2},{6,0},{1,7},{3,5},{5,3},{7,1},{8,14},{10,12},{12... | collective-permute-start | bytes 903176 | tf_op jit(solution)/shard_map/ppermute | solution.py:33
  225.5 15.1 %collective-permute-start.38 = (bf16[4,96,768]{2,1,0:T(8,128)(2,1)}, bf16[4,96,768]{2,1,0:T(8,128)(2,1)}, u32[]{:S(2)}, u32[]{:S(2)}) collective-permute-start(bf16[4,96,768]{2,1,0:T(8,128)(2,1)} %get-tuple-element.186), channel_id=1, source_target_pairs={{0,4},{4,0},{1,5},{5,1},{2,6},{6,2},{3,7},{7,3},{8,12},{12,8},{9,1... | collective-permute-start | bytes 1769480 | tf_op jit(solution)/shard_map/ppermute | solution.py:29
  226.7 14.8 %collective-permute-start.39 = (bf16[4,96,768]{2,1,0:T(8,128)(2,1)}, bf16[4,96,768]{2,1,0:T(8,128)(2,1)}, u32[]{:S(2)}, u32[]{:S(2)}) collective-permute-start(bf16[4,96,768]{2,1,0:T(8,128)(2,1)} %get-tuple-element.187), channel_id=1, source_target_pairs={{0,2},{2,0},{1,3},{3,1},{4,6},{6,4},{5,7},{7,5},{8,10},{10,8},{9,1... | collective-permute-start | bytes 1769480 | tf_op jit(solution)/shard_map/ppermute | solution.py:25
  241.5 18.2 %collective-permute-start.40 = (bf16[16,96,768]{2,1,0:T(8,128)(2,1)}, bf16[16,96,768]{2,1,0:T(8,128)(2,1)}, u32[]{:S(2)}, u32[]{:S(2)}) collective-permute-start(bf16[16,96,768]{2,1,0:T(8,128)(2,1)} %get-tuple-element.197), channel_id=1, source_target_pairs={{0,1},{1,0},{2,3},{3,2},{4,5},{5,4},{6,7},{7,6},{8,9},{9,8},{10,11... | collective-permute-start | bytes 7077896 | tf_op jit(solution)/shard_map/ppermute | solution.py:37
  245.9 39.0 %collective-permute-start.41 = (bf16[8,96,768]{2,1,0:T(8,128)(2,1)}, bf16[8,96,768]{2,1,0:T(8,128)(2,1)}, u32[]{:S(2)}, u32[]{:S(2)}) collective-permute-start(bf16[8,96,768]{2,1,0:T(8,128)(2,1)} %get-tuple-element.193), channel_id=1, source_target_pairs={{0,2},{2,0},{1,3},{3,1},{4,6},{6,4},{5,7},{7,5},{8,10},{10,8},{9,1... | collective-permute-start | bytes 3538952 | tf_op jit(solution)/shard_map/ppermute | solution.py:25
  246.7 38.3 %collective-permute-start.42 = (bf16[8,96,768]{2,1,0:T(8,128)(2,1)}, bf16[8,96,768]{2,1,0:T(8,128)(2,1)}, u32[]{:S(2)}, u32[]{:S(2)}) collective-permute-start(bf16[8,96,768]{2,1,0:T(8,128)(2,1)} %get-tuple-element.194), channel_id=1, source_target_pairs={{0,4},{4,0},{1,5},{5,1},{2,6},{6,2},{3,7},{7,3},{8,12},{12,8},{9,1... | collective-permute-start | bytes 3538952 | tf_op jit(solution)/shard_map/ppermute | solution.py:29
  261.8 23.2 %collective-permute-start.43 = (bf16[2,96,768]{2,1,0:T(8,128)(2,1)}, bf16[2,96,768]{2,1,0:T(8,128)(2,1)}, u32[]{:S(2)}, u32[]{:S(2)}) collective-permute-start(bf16[2,96,768]{2,1,0:T(8,128)(2,1)} %get-tuple-element.199), channel_id=1, source_target_pairs={{0,4},{4,0},{1,5},{5,1},{2,6},{6,2},{3,7},{7,3},{8,12},{12,8},{9,1... | collective-permute-start | bytes 884744 | tf_op jit(solution)/shard_map/ppermute | solution.py:29
  263.0 22.0 %collective-permute-start.44 = (bf16[2,96,768]{2,1,0:T(8,128)(2,1)}, bf16[2,96,768]{2,1,0:T(8,128)(2,1)}, u32[]{:S(2)}, u32[]{:S(2)}) collective-permute-start(bf16[2,96,768]{2,1,0:T(8,128)(2,1)} %get-tuple-element.200), channel_id=1, source_target_pairs={{0,2},{2,0},{1,3},{3,1},{4,6},{6,4},{5,7},{7,5},{8,10},{10,8},{9,1... | collective-permute-start | bytes 884744 | tf_op jit(solution)/shard_map/ppermute | solution.py:25
  287.9 23.8 %all-to-all-start.3 = ((bf16[4,1,96,768]{3,2,1,0:T(8,128)(2,1)}), bf16[4,1,96,768]{3,2,1,0:T(8,128)(2,1)}, u32[]{:S(2)}, u32[]{:S(2)}) async-start(bf16[4,1,96,768]{3,2,1,0:T(8,128)(2,1)} %bitcast.94), calls=%async_computation.3 | async-start | bytes 1179648 | tf_op jit(solution)/shard_map/all_to_all | solution.py:41
  295.3 16.4 %collective-permute-start.46 = (bf16[4,96,768]{2,1,0:T(8,128)(2,1)}, bf16[4,96,768]{2,1,0:T(8,128)(2,1)}, u32[]{:S(2)}, u32[]{:S(2)}) collective-permute-start(bf16[4,96,768]{2,1,0:T(8,128)(2,1)} %get-tuple-element.212), channel_id=1, source_target_pairs={{0,2},{2,0},{1,3},{3,1},{4,6},{6,4},{5,7},{7,5},{8,10},{10,8},{9,1... | collective-permute-start | bytes 1769480 | tf_op jit(solution)/shard_map/ppermute | solution.py:25
  296.0 15.8 %collective-permute-start.47 = (bf16[4,96,768]{2,1,0:T(8,128)(2,1)}, bf16[4,96,768]{2,1,0:T(8,128)(2,1)}, u32[]{:S(2)}, u32[]{:S(2)}) collective-permute-start(bf16[4,96,768]{2,1,0:T(8,128)(2,1)} %get-tuple-element.213), channel_id=1, source_target_pairs={{0,4},{4,0},{1,5},{5,1},{2,6},{6,2},{3,7},{7,3},{8,12},{12,8},{9,1... | collective-permute-start | bytes 1769480 | tf_op jit(solution)/shard_map/ppermute | solution.py:29
  318.8 17.1 %collective-permute-start.49 = (bf16[2,96,768]{2,1,0:T(8,128)(2,1)}, bf16[2,96,768]{2,1,0:T(8,128)(2,1)}, u32[]{:S(2)}, u32[]{:S(2)}) collective-permute-start(bf16[2,96,768]{2,1,0:T(8,128)(2,1)} %get-tuple-element.220), channel_id=1, source_target_pairs={{0,4},{4,0},{1,5},{5,1},{2,6},{6,2},{3,7},{7,3},{8,12},{12,8},{9,1... | collective-permute-start | bytes 884744 | tf_op jit(solution)/shard_map/ppermute | solution.py:29
  320.0 15.9 %collective-permute-start.50 = (bf16[2,96,768]{2,1,0:T(8,128)(2,1)}, bf16[2,96,768]{2,1,0:T(8,128)(2,1)}, u32[]{:S(2)}, u32[]{:S(2)}) collective-permute-start(bf16[2,96,768]{2,1,0:T(8,128)(2,1)} %get-tuple-element.221), channel_id=1, source_target_pairs={{0,2},{2,0},{1,3},{3,1},{4,6},{6,4},{5,7},{7,5},{8,10},{10,8},{9,1... | collective-permute-start | bytes 884744 | tf_op jit(solution)/shard_map/ppermute | solution.py:25
  330.8 40.8 %all-to-all-start.4 = ((bf16[4,2,96,768]{3,2,1,0:T(8,128)(2,1)}), bf16[4,2,96,768]{3,2,1,0:T(8,128)(2,1)}, u32[]{:S(2)}, u32[]{:S(2)}) async-start(bf16[4,2,96,768]{3,2,1,0:T(8,128)(2,1)} %bitcast.93), calls=%async_computation.4 | async-start | bytes 2359296 | tf_op jit(solution)/shard_map/all_to_all | solution.py:41
  338.8 14.8 %collective-permute-start.51 = (bf16[4,96,768]{2,1,0:T(8,128)(2,1)}, bf16[4,96,768]{2,1,0:T(8,128)(2,1)}, u32[]{:S(2)}, u32[]{:S(2)}) collective-permute-start(bf16[4,96,768]{2,1,0:T(8,128)(2,1)} %get-tuple-element.226), channel_id=1, source_target_pairs={{0,2},{2,0},{1,3},{3,1},{4,6},{6,4},{5,7},{7,5},{8,10},{10,8},{9,1... | collective-permute-start | bytes 1769480 | tf_op jit(solution)/shard_map/ppermute | solution.py:25
  339.6 14.6 %collective-permute-start.52 = (bf16[4,96,768]{2,1,0:T(8,128)(2,1)}, bf16[4,96,768]{2,1,0:T(8,128)(2,1)}, u32[]{:S(2)}, u32[]{:S(2)}) collective-permute-start(bf16[4,96,768]{2,1,0:T(8,128)(2,1)} %get-tuple-element.227), channel_id=1, source_target_pairs={{0,4},{4,0},{1,5},{5,1},{2,6},{6,2},{3,7},{7,3},{8,12},{12,8},{9,1... | collective-permute-start | bytes 1769480 | tf_op jit(solution)/shard_map/ppermute | solution.py:29
  356.8 18.6 %collective-permute-start.56 = (bf16[1,96,768]{2,1,0:T(8,128)(2,1)}, bf16[1,96,768]{2,1,0:T(8,128)(2,1)S(1)}, u32[]{:S(2)}, u32[]{:S(2)}) collective-permute-start(bf16[1,96,768]{2,1,0:T(8,128)(2,1)} %get-tuple-element.237), channel_id=1, source_target_pairs={{0,8},{8,16},{16,24},{24,0},{1,9},{9,17},{17,25},{25,1},{2,10},{10... | collective-permute-start | bytes 442376 | tf_op jit(solution)/shard_map/ppermute | solution.py:165
  358.6 24.2 %collective-permute-start.57 = (bf16[1,96,768]{2,1,0:T(8,128)(2,1)}, bf16[1,96,768]{2,1,0:T(8,128)(2,1)S(1)}, u32[]{:S(2)}, u32[]{:S(2)}) collective-permute-start(bf16[1,96,768]{2,1,0:T(8,128)(2,1)} %get-tuple-element.238), channel_id=1, source_target_pairs={{0,16},{8,24},{16,0},{24,8},{1,17},{9,25},{17,1},{25,9},{2,18},{10... | collective-permute-start | bytes 442376 | tf_op jit(solution)/shard_map/ppermute | solution.py:165
  360.9 22.0 %collective-permute-start.53 = (bf16[2,98,768]{2,1,0:T(8,128)(2,1)}, bf16[2,98,768]{2,1,0:T(8,128)(2,1)S(1)}, u32[]{:S(2)}, u32[]{:S(2)}) collective-permute-start(bf16[2,98,768]{2,1,0:T(8,128)(2,1)} %get-tuple-element.249), channel_id=1, source_target_pairs={{0,2},{2,0},{1,3},{3,1},{4,6},{6,4},{5,7},{7,5},{8,10},{10,8},{9,1... | collective-permute-start | bytes 903176 | tf_op jit(solution)/shard_map/ppermute | solution.py:25
  362.2 20.7 %collective-permute-start.54 = (bf16[2,98,768]{2,1,0:T(8,128)(2,1)}, bf16[2,98,768]{2,1,0:T(8,128)(2,1)S(1)}, u32[]{:S(2)}, u32[]{:S(2)}) collective-permute-start(bf16[2,98,768]{2,1,0:T(8,128)(2,1)} %get-tuple-element.250), channel_id=1, source_target_pairs={{0,4},{4,0},{1,5},{5,1},{2,6},{6,2},{3,7},{7,3},{8,12},{12,8},{9,1... | collective-permute-start | bytes 903176 | tf_op jit(solution)/shard_map/ppermute | solution.py:29
  363.0 19.9 %collective-permute-start.55 = (bf16[2,98,768]{2,1,0:T(8,128)(2,1)}, bf16[2,98,768]{2,1,0:T(8,128)(2,1)S(1)}, u32[]{:S(2)}, u32[]{:S(2)}) collective-permute-start(bf16[2,98,768]{2,1,0:T(8,128)(2,1)} %get-tuple-element.251), channel_id=1, source_target_pairs={{0,6},{2,4},{4,2},{6,0},{1,7},{3,5},{5,3},{7,1},{8,14},{10,12},{12... | collective-permute-start | bytes 903176 | tf_op jit(solution)/shard_map/ppermute | solution.py:33
  (52 other events, 323.8 us)

commit v3 on v2

--- a/solution.py
+++ b/solution.py
@@ -674,11 +674,9 @@
 
         @pl.loop(0, 6)
         def _(j):
-            @pl.loop(0, 2)
-            def _(g):
-                pair = [mix(j, 2 * g + i) for i in range(2)]
-                for i in range(2):
-                    mixed[j, row_slices(2 * g + i), :] = pair[i]
+            frames = [mix(j, f) for f in range(4)]
+            for f in range(4):
+                mixed[j, row_slices(f), :] = frames[f]
 
         mixed_out.send()
         wait_all(copies)
@@ -875,23 +873,19 @@
 
         @pl.loop(0, 4)
         def _(j):
-            @pl.loop(0, 2)
-            def _(g):
-                ats = [row_slices(2 * g + i) for i in range(2)]
-                pair = [slopes(j, ats[i], 2 * g + i) for i in range(2)]
-                for at, (dq, dk, dv) in zip(ats, pair):
-                    dy[j, at, 0:128] = dq
-                    dy[j, at, 128:256] = dk
-                    dy[j, at, 256:384] = dv
+            ats = [row_slices(f) for f in range(4)]
+            frames = [slopes(j, ats[f], f) for f in range(4)]
+            for at, (dq, dk, dv) in zip(ats, frames):
+                dy[j, at, 0:128] = dq
+                dy[j, at, 128:256] = dk
+                dy[j, at, 256:384] = dv
 
         @pl.loop(0, 2)
         def _(u):
-            @pl.loop(0, 2)
-            def _(g):
-                ats = [row_slices(2 * g + i) for i in range(2)]
-                pair = [slopes(4 + u, ats[i], 2 * g + i) for i in range(2)]
-                for at, v in zip(ats, pair):
-                    place_third(*v, dy, u, at)
+            ats = [row_slices(f) for f in range(4)]
+            frames = [slopes(4 + u, ats[f], f) for f in range(4)]
+            for at, v in zip(ats, frames):
+                place_third(*v, dy, u, at)
 
     ins = [(meta, "s")] + [(d2, "v")] + [(v, "l") for v in (q, kv, logs)] + [(w, "a") for w in weights]
     outs = [((rows, d), B16, "e"), ((4, rows, 640), B16, "v")]

time: 400 us -> 396 us (0.990)
  Pallas kernels: 215 us -> 211 us
  transfers between devices with their start and end apart: 65 -> 65, of which waited for: 22 -> 21; matrix products, arithmetic and copies ran while one was open for 6% -> 7% of each run, Pallas kernels for 44% -> 44%
where the time goes in v3:
time: 396 us; the launch traced here: 391 us
  Pallas kernels  211 us (53%)
  starting transfers between devices  78.9 us (20%)
  waiting for transfers between devices  57.6 us (15%)
  local copies, waits for them, and re-layouts  34.9 us (9%)
  other arithmetic  6.43 us (2%)
    pallas_call x12, Pallas kernels, run(): pl.pallas_call(body, name=name, in_specs=[space[s] for _, s in ins], out_...  184 us
    pallas_call x9, Pallas kernels, block_sums(): pl.pallas_call(kernel, name=name, grid=(1,), in_specs=[spec(blocks, index...  26.8 us
    all_to_all x5, starting transfers between devices, over_z(): return lax.all_to_all(v, 'shard', split_axis=0, concat_axis=0, tiled=True)  25 us
    ppermute x16, waiting for transfers between devices, over_x(): return lax.ppermute(v, 'x', FLIP)  18.1 us
    ppermute x16, starting transfers between devices, over_x(): return lax.ppermute(v, 'x', FLIP)  16.6 us
    ppermute x16, starting transfers between devices, over_y(): return lax.ppermute(v, 'ctx', FLIP)  15.6 us
    all_to_all x5, waiting for transfers between devices, over_z(): return lax.all_to_all(v, 'shard', split_axis=0, concat_axis=0, tiled=True)  14.2 us
    ppermute x16, waiting for transfers between devices, over_y(): return lax.ppermute(v, 'ctx', FLIP)  13.4 us
  transfers between devices with their start and end apart: 65, of which 21 were waited for; matrix products, arithmetic and copies ran while one was open for 7% of the time, Pallas kernels for 44%

profile of v3, /device:TPU:0, one launch (start us, length us, event | category | flops | bytes accessed | tf_op | source)
XLA Modules:
  0.0 390.7 jit_solution(13912833469820126184)
XLA Ops:
  4.5 6.3 %all-to-all-start = ((bf16[4,1,104,768]{3,2,1,0:T(8,128)(2,1)}), bf16[4,1,104,768]{3,2,1,0:T(8,128)(2,1)S(1)}, u32[]{:S(2)}, u32[]{:S(2)}) async-start(bf16[4,1,104,768]{3,2,1,0:T(8,128)(2,1)} %broadcast_in_dim.68), calls=%async_computation | async-start | bytes 1277952 | tf_op jit(solution)/shard_map/all_to_all | solution.py:41
  13.3 1.6 collective-permute-start.4
  17.8 2.5 collective-permute-start.2
  21.3 6.5 %all-to-all-done = bf16[4,1,104,768]{3,2,1,0:T(8,128)(2,1)S(1)} async-done(((bf16[4,1,104,768]{3,2,1,0:T(8,128)(2,1)}), bf16[4,1,104,768]{3,2,1,0:T(8,128)(2,1)S(1)}, u32[]{:S(2)}, u32[]{:S(2)}) %all-to-all-start) | async-done | bytes 639008 | tf_op jit(solution)/shard_map/all_to_all | solution.py:41
  27.8 4.1 %all-to-all-start.1 = ((bf16[4,1,96,768]{3,2,1,0:T(8,128)(2,1)}), bf16[4,1,96,768]{3,2,1,0:T(8,128)(2,1)}, u32[]{:S(2)}, u32[]{:S(2)}) async-start(bf16[4,1,96,768]{3,2,1,0:T(8,128)(2,1)} %broadcast_in_dim.69), calls=%async_computation.1 | async-start | bytes 1179648 | tf_op jit(solution)/shard_map/all_to_all | solution.py:41
  32.0 3.9 %collective-permute-done.1.refs_5_ = bf16[2,98,768]{2,1,0:T(8,128)(2,1)} collective-permute-done((bf16[2,98,768]{2,1,0:T(8,128)(2,1)S(1)}, bf16[2,98,768]{2,1,0:T(8,128)(2,1)}, u32[]{:S(2)}, u32[]{:S(2)}) %collective-permute-start.1) | collective-permute-done | bytes 301088 | tf_op jit(solution)/shard_map/ppermute | solution.py:29
  38.0 12.6 %collective-permute-done.5.refs_2_.refs_7_.refs_6_ = bf16[4,104,768]{2,1,0:T(8,128)(2,1)S(1)} collective-permute-done((bf16[4,104,768]{2,1,0:T(8,128)(2,1)S(1)}, bf16[4,104,768]{2,1,0:T(8,128)(2,1)S(1)}, u32[]{:S(2)}, u32[]{:S(2)}) %collective-permute-start.5) | collective-permute-done | bytes 639008 | tf_op jit(solution)/shard_map/ppermute | solution.py:25
  54.7 5.4 %all-to-all-start.2 = ((bf16[4,2,96,768]{3,2,1,0:T(8,128)(2,1)}), bf16[4,2,96,768]{3,2,1,0:T(8,128)(2,1)}, u32[]{:S(2)}, u32[]{:S(2)}) async-start(bf16[4,2,96,768]{3,2,1,0:T(8,128)(2,1)} %broadcast_in_dim.70), calls=%async_computation.2 | async-start | bytes 2359296 | tf_op jit(solution)/shard_map/all_to_all | solution.py:41
  61.4 2.2 collective-permute-start.14
  66.3 3.0 norm_vectors.1.refs_1_
  69.3 3.7 collective-permute-done.14.refs_5_
  73.1 10.3 %time_qkv.1 = (f32[832,768]{1,0:T(8,128)}, bf16[832,768]{1,0:T(8,128)(2,1)}, bf16[6,832,128]{2,1,0:T(8,128)(2,1)}, bf16[12,832,128]{2,1,0:T(8,128)(2,1)}) custom-call(s32[4]{0:T(128)} %pad_add_fusion.refs_0_, f32[16,768]{1,0:T(8,128)} %norm_vectors.1.refs_1_, bf16[2,98,768]{2,1,0:T(8,128)(2,1)} %bitcast.108, ...), custom_call_target="tpu_custom_call" | custom-call | flops 12000000000 | bytes 36000000 | tf_op jit(solution)/shard_map/time_qkv/pallas_call | solution.py:414
  84.8 4.0 %all-to-all-done.2 = bf16[4,2,96,768]{3,2,1,0:T(8,128)(2,1)} async-done(((bf16[4,2,96,768]{3,2,1,0:T(8,128)(2,1)}), bf16[4,2,96,768]{3,2,1,0:T(8,128)(2,1)}, u32[]{:S(2)}, u32[]{:S(2)}) %all-to-all-start.2) | async-done | bytes 1179680 | tf_op jit(solution)/shard_map/all_to_all | solution.py:41
  93.7 5.6 %collective-permute-done.18.refs_6_.refs_8_ = bf16[2,96,768]{2,1,0:T(8,128)(2,1)S(1)} collective-permute-done((bf16[2,96,768]{2,1,0:T(8,128)(2,1)S(1)}, bf16[2,96,768]{2,1,0:T(8,128)(2,1)S(1)}, u32[]{:S(2)}, u32[]{:S(2)}) %collective-permute-start.18) | collective-permute-done | bytes 294944 | tf_op jit(solution)/shard_map/ppermute | solution.py:29
  99.3 2.2 collective-permute-done.19.refs_7_.refs_9_
  105.5 15.4 %time_mix.1 = (bf16[6,832,128]{2,1,0:T(8,128)(2,1)}, f32[832,768]{1,0:T(8,128)}, f32[8,208,128]{2,1,0:T(8,128)}) custom-call(s32[4]{0:T(128)} %pad_add_fusion.refs_0_, f32[16,768]{1,0:T(8,128)} %norm_vectors.1.refs_1_, f32[832,768]{1,0:T(8,128)} %get-tuple-element.153.refs_2_.refs_3_, bf16[6,832,128]{2,1,0:T(8,128)(2,1)} %get-tuple-element.154.refs_3_.refs_2_, ...), custom_call_target="tpu_custom_call" | custom-call | flops 16999999488 | bytes 51000000 | tf_op jit(solution)/shard_map/time_mix/pallas_call | solution.py:414
  121.0 10.8 %space_qkv.1 = (bf16[832,768]{1,0:T(8,128)(2,1)}, bf16[6,832,128]{2,1,0:T(8,128)(2,1)}, bf16[12,832,128]{2,1,0:T(8,128)(2,1)}) custom-call(s32[4]{0:T(128)} %pad_add_fusion.refs_0_, f32[16,768]{1,0:T(8,128)} %norm_vectors.1.refs_1_, f32[832,768]{1,0:T(8,128)} %get-tuple-element.162.refs_2_.refs_3_, bf16[4,96,768]{2,1,0:T(8,128)(2,1)} %bitcast.18.refs_3_.refs_5_, ...), custom_call_target="tpu_custom_call" | custom-call | flops 12000000000 | bytes 36000000 | tf_op jit(solution)/shard_map/space_qkv/pallas_call | solution.py:414
  132.6 1.9 slice.229
  134.6 1.9 slice.230
  139.1 12.9 %space_mix.1 = (bf16[6,832,128]{2,1,0:T(8,128)(2,1)}, f32[24,8,208]{2,1,0:T(8,128)}, f32[832,768]{1,0:T(8,128)}) custom-call(s32[4]{0:T(128)} %pad_add_fusion.refs_0_, f32[16,768]{1,0:T(8,128)} %norm_vectors.1.refs_1_, f32[832,768]{1,0:T(8,128)} %get-tuple-element.162.refs_2_.refs_3_, bf16[6,832,128]{2,1,0:T(8,128)(2,1)} %get-tuple-element.165.refs_3_.refs_2_, ...), custom_call_target="tpu_custom_call" | custom-call | flops 16999999488 | bytes 51000000 | tf_op jit(solution)/shard_map/space_mix/pallas_call | solution.py:414
  153.1 1.7 copy.144
  155.8 37.6 %feed_forward.1 = (bf16[2,98,768]{2,1,0:T(8,128)(2,1)}, bf16[2,98,768]{2,1,0:T(8,128)(2,1)}, bf16[2,98,768]{2,1,0:T(8,128)(2,1)}, bf16[2,98,768]{2,1,0:T(8,128)(...) custom-call(s32[4]{0:T(128)} %pad_add_fusion.refs_0_, ...), custom_call_target="tpu_custom_call" | custom-call | flops 46999998464 | bytes 141000000 | tf_op jit(solution)/shard_map/feed_forward/pallas_call | solution.py:414
  195.4 1.7 collective-permute-start.36
  197.2 21.7 %space_backward_scores.1 = (bf16[832,768]{1,0:T(8,128)(2,1)}, bf16[4,832,640]{2,1,0:T(8,128)(2,1)}) custom-call(s32[4]{0:T(128)} %pad_add_fusion.refs_0_, f32[832,768]{1,0:T(8,128)} %get-tuple-element.195.refs_1_.refs_2_, bf16[6,832,128]{2,1,0:T(8,128)(2,1)} %get-tuple-element.165.refs_3_.refs_2_, bf16[12,832,128]{2,1,0:T(8,128)(2,1)} %get-tuple-element.169.refs_4_.refs_3_, ...), custom_call_target="tpu_custom_call" | custom-call | flops 30000001024 | bytes 90000000 | tf_op jit(solution)/shard_map/space_backward_scores/pallas_call | solution.py:414
  218.9 2.7 mlp_rest.1
  223.4 12.2 %space_weights.1 = (bf16[16,96,768]{2,1,0:T(8,128)(2,1)}, bf16[16,96,768]{2,1,0:T(8,128)(2,1)}) custom-call(s32[4]{0:T(128)} %pad_add_fusion.refs_0_, bf16[832,768]{1,0:T(8,128)(2,1)} %get-tuple-element.175.refs_1_, bf16[832,768]{1,0:T(8,128)(2,1)} %get-tuple-element.176.refs_2_, bf16[6,832,128]{2,1,0:T(8,128)(2,1)} %get-tuple-element.177.refs_3_, ...), custom_call_target="tpu_custom_call" | custom-call | flops 14000000000 | bytes 42000000 | tf_op jit(solution)/shard_map/space_weights/pallas_call | solution.py:414
  237.2 4.5 %mlp_xy.1 = (bf16[8,96,768]{2,1,0:T(8,128)(2,1)}, bf16[8,96,768]{2,1,0:T(8,128)(2,1)}) custom-call(bf16[32,96,768]{2,1,0:T(8,128)(2,1)} %get-tuple-element.183.refs_0_.refs_2_.refs_3_.refs_4_.refs_8_.refs_12_.refs_16_.refs_20_.refs_24_.refs_28_, ...), custom_call_target="tpu_custom_call" | custom-call | flops 100000000 | bytes 100000 | tf_op jit(solution)/shard_map/mlp_xy/pallas_call | solution.py:104
  243.8 12.1 %space_input.1 = (f32[832,768]{1,0:T(8,128)}, f32[8,768]{1,0:T(8,128)}) custom-call(s32[4]{0:T(128)} %pad_add_fusion.refs_0_, f32[16,768]{1,0:T(8,128)} %norm_vectors.1.refs_1_, f32[832,768]{1,0:T(8,128)} %get-tuple-element.195.refs_1_.refs_2_, f32[832,768]{1,0:T(8,128)} %get-tuple-element.162.refs_2_.refs_3_, ...), custom_call_target="tpu_custom_call" | custom-call | flops 14000000000 | bytes 42000000 | tf_op jit(solution)/shard_map/space_input/pallas_call | solution.py:414
  256.0 2.1 space_rest.1
  260.0 21.1 %time_backward_scores.1 = (bf16[832,768]{1,0:T(8,128)(2,1)}, bf16[6,832,128]{2,1,0:T(8,128)(2,1)}, bf16[12,832,128]{2,1,0:T(8,128)(2,1)}, bf16[12,832,128]{2,1,0:T(8,128)(2,1)}) custom-call(s32[4]{0:T(128)} %pad_add_fusion.refs_0_, f32[832,768]{1,0:T(8,128)} %get-tuple-element.228.refs_1_.refs_2_, bf16[6,832,128]{2,1,0:T(8,128)(2,1)} %get-tuple-element.154.refs_3_.refs_2_, ...), custom_call_target="tpu_custom_call" | custom-call | flops 23000000512 | bytes 69000000 | tf_op jit(solution)/shard_map/time_backward_scores/pallas_call | solution.py:414
  281.3 2.8 mlp_z.1
  284.1 4.1 %all-to-all-start.3 = ((bf16[4,1,96,768]{3,2,1,0:T(8,128)(2,1)}), bf16[4,1,96,768]{3,2,1,0:T(8,128)(2,1)}, u32[]{:S(2)}, u32[]{:S(2)}) async-start(bf16[4,1,96,768]{3,2,1,0:T(8,128)(2,1)} %bitcast.94), calls=%async_computation.3 | async-start | bytes 1179648 | tf_op jit(solution)/shard_map/all_to_all | solution.py:41
  288.3 3.0 space_xy.1
  293.3 14.8 %time_weights.1 = (bf16[4,832,640]{2,1,0:T(8,128)(2,1)}, bf16[16,96,768]{2,1,0:T(8,128)(2,1)}, bf16[16,96,768]{2,1,0:T(8,128)(2,1)}) custom-call(s32[4]{0:T(128)} %pad_add_fusion.refs_0_, bf16[832,768]{1,0:T(8,128)(2,1)} %get-tuple-element.203.refs_1_, bf16[832,768]{1,0:T(8,128)(2,1)} %get-tuple-element.204.refs_2_, ...), custom_call_target="tpu_custom_call" | custom-call | flops 14000000000 | bytes 42000000 | tf_op jit(solution)/shard_map/time_weights/pallas_call | solution.py:414
  308.3 4.9 %collective-permute-done.48.refs_1_.refs_3_.refs_4_.refs_5_.refs_9_.refs_13_ = bf16[16,96,768]{2,1,0:T(8,128)(2,1)} collective-permute-done((bf16[16,96,768]{2,1,0:T(8,128)(2,1)}, bf16[16,96,768]{2,1,0:T(8,128)(2,1)}, u32[]{:S(2)}, u32[]{:S(2)}) %collective-permute-start.48) | collective-permute-done | bytes 2359328 | tf_op jit(solution)/shard_map/ppermute | solution.py:37
  313.1 2.1 time_rest.1
  322.7 4.0 %joint_z.1 = bf16[8,96,768]{2,1,0:T(8,128)(2,1)} custom-call(bf16[16,96,768]{2,1,0:T(8,128)(2,1)} %get-tuple-element.189.refs_0_.refs_2_.refs_3_.refs_4_.refs_8_.refs_12_, bf16[16,96,768]{2,1,0:T(8,128)(2,1)} %collective-permute-done.40.refs_1_.refs_3_.refs_4_.refs_5_.refs_9_.refs_13_, ...), custom_call_target="tpu_custom_call" | custom-call | flops 100000000 | bytes 100000 | tf_op jit(solution)/shard_map/joint_z/pallas_call | solution.py:104
  326.7 5.1 %all-to-all-start.4 = ((bf16[4,2,96,768]{3,2,1,0:T(8,128)(2,1)}), bf16[4,2,96,768]{3,2,1,0:T(8,128)(2,1)}, u32[]{:S(2)}, u32[]{:S(2)}) async-start(bf16[4,2,96,768]{3,2,1,0:T(8,128)(2,1)} %bitcast.93), calls=%async_computation.4 | async-start | bytes 2359296 | tf_op jit(solution)/shard_map/all_to_all | solution.py:41
  331.8 3.0 time_xy.1
  336.8 11.8 %time_input.1 = (f32[2,98,768]{2,1,0:T(8,128)}, bf16[2,98,768]{2,1,0:T(8,128)(2,1)}, bf16[2,98,768]{2,1,0:T(8,128)(2,1)}, bf16[2,98,768]{2,1,0:T(8,128)(2,1)}, f32[8,768]{1,0:T(8,128)}) custom-call(s32[4]{0:T(128)} %pad_add_fusion.refs_0_, f32[16,768]{1,0:T(8,128)} %norm_vectors.1.refs_1_, f32[832,768]{1,0:T(8,128)} %get-tuple-element.228.refs_1_.refs_2_, ...), custom_call_target="tpu_custom_call" | custom-call | flops 14000000000 | bytes 42000000 | tf_op jit(solution)/shard_map/time_input/pallas_call | solution.py:414
  350.2 2.6 time_z.1
  352.9 1.8 collective-permute-start.56
  354.6 2.4 collective-permute-start.57
  363.9 3.6 all-to-all-done.4
  368.7 2.6 all-to-all-start.5
  371.2 3.8 collective-permute-start.58
  376.3 2.4 all-to-all-done.5
  384.4 1.9 convert_reduce_fusion.1
  (285 shorter events, 77.4 us)
Async XLA Ops:
  4.5 23.3 %all-to-all-start = ((bf16[4,1,104,768]{3,2,1,0:T(8,128)(2,1)}), bf16[4,1,104,768]{3,2,1,0:T(8,128)(2,1)S(1)}, u32[]{:S(2)}, u32[]{:S(2)}) async-start(bf16[4,1,104,768]{3,2,1,0:T(8,128)(2,1)} %broadcast_in_dim.68), calls=%async_computation | async-start | bytes 1277952 | tf_op jit(solution)/shard_map/all_to_all | solution.py:41
  11.7 20.2 %collective-permute-start.3 = (bf16[2,98,768]{2,1,0:T(8,128)(2,1)S(1)}, bf16[2,98,768]{2,1,0:T(8,128)(2,1)}, u32[]{:S(2)}, u32[]{:S(2)}) collective-permute-start(bf16[2,98,768]{2,1,0:T(8,128)(2,1)S(1)} %bitcast.105), channel_id=1, source_target_pairs={{0,2},{2,0},{1,3},{3,1},{4,6},{6,4},{5,7},{7,5},{8,10},{10,8},{9,1... | collective-permute-start | bytes 903176 | tf_op jit(solution)/shard_map/ppermute | solution.py:25
  13.3 18.6 %collective-permute-start.4 = (bf16[2,98,768]{2,1,0:T(8,128)(2,1)S(1)}, bf16[2,98,768]{2,1,0:T(8,128)(2,1)}, u32[]{:S(2)}, u32[]{:S(2)}) collective-permute-start(bf16[2,98,768]{2,1,0:T(8,128)(2,1)S(1)} %bitcast.106), channel_id=1, source_target_pairs={{0,4},{4,0},{1,5},{5,1},{2,6},{6,2},{3,7},{7,3},{8,12},{12,8},{9,1... | collective-permute-start | bytes 903176 | tf_op jit(solution)/shard_map/ppermute | solution.py:29
  16.5 15.5 %collective-permute-start = (bf16[2,98,768]{2,1,0:T(8,128)(2,1)S(1)}, bf16[2,98,768]{2,1,0:T(8,128)(2,1)}, u32[]{:S(2)}, u32[]{:S(2)}) collective-permute-start(bf16[2,98,768]{2,1,0:T(8,128)(2,1)S(1)} %bitcast.107), channel_id=1, source_target_pairs={{0,2},{2,0},{1,3},{3,1},{4,6},{6,4},{5,7},{7,5},{8,10},{10,8},{9,1... | collective-permute-start | bytes 903176 | tf_op jit(solution)/shard_map/ppermute | solution.py:25
  17.1 18.8 %collective-permute-start.1 = (bf16[2,98,768]{2,1,0:T(8,128)(2,1)S(1)}, bf16[2,98,768]{2,1,0:T(8,128)(2,1)}, u32[]{:S(2)}, u32[]{:S(2)}) collective-permute-start(bf16[2,98,768]{2,1,0:T(8,128)(2,1)S(1)} %bitcast.110), channel_id=1, source_target_pairs={{0,4},{4,0},{1,5},{5,1},{2,6},{6,2},{3,7},{7,3},{8,12},{12,8},{9,1... | collective-permute-start | bytes 903176 | tf_op jit(solution)/shard_map/ppermute | solution.py:29
  17.8 18.2 %collective-permute-start.2 = (bf16[2,98,768]{2,1,0:T(8,128)(2,1)S(1)}, bf16[2,98,768]{2,1,0:T(8,128)(2,1)}, u32[]{:S(2)}, u32[]{:S(2)}) collective-permute-start(bf16[2,98,768]{2,1,0:T(8,128)(2,1)S(1)} %bitcast.111), channel_id=1, source_target_pairs={{0,6},{2,4},{4,2},{6,0},{1,7},{3,5},{5,3},{7,1},{8,14},{10,12},{12... | collective-permute-start | bytes 903176 | tf_op jit(solution)/shard_map/ppermute | solution.py:33
  27.8 26.9 %all-to-all-start.1 = ((bf16[4,1,96,768]{3,2,1,0:T(8,128)(2,1)}), bf16[4,1,96,768]{3,2,1,0:T(8,128)(2,1)}, u32[]{:S(2)}, u32[]{:S(2)}) async-start(bf16[4,1,96,768]{3,2,1,0:T(8,128)(2,1)} %broadcast_in_dim.69), calls=%async_computation.1 | async-start | bytes 1179648 | tf_op jit(solution)/shard_map/all_to_all | solution.py:41
  35.9 14.6 %collective-permute-start.5 = (bf16[4,104,768]{2,1,0:T(8,128)(2,1)S(1)}, bf16[4,104,768]{2,1,0:T(8,128)(2,1)S(1)}, u32[]{:S(2)}, u32[]{:S(2)}) collective-permute-start(bf16[4,104,768]{2,1,0:T(8,128)(2,1)S(1)} %bitcast.95), channel_id=1, source_target_pairs={{0,2},{2,0},{1,3},{3,1},{4,6},{6,4},{5,7},{7,5},{8,10},{10,8},{9,1... | collective-permute-start | bytes 1916936 | tf_op jit(solution)/shard_map/ppermute | solution.py:25
  37.1 14.7 %collective-permute-start.6 = (bf16[4,104,768]{2,1,0:T(8,128)(2,1)S(1)}, bf16[4,104,768]{2,1,0:T(8,128)(2,1)S(1)}, u32[]{:S(2)}, u32[]{:S(2)}) collective-permute-start(bf16[4,104,768]{2,1,0:T(8,128)(2,1)S(1)} %bitcast.96), channel_id=1, source_target_pairs={{0,4},{4,0},{1,5},{5,1},{2,6},{6,2},{3,7},{7,3},{8,12},{12,8},{9,1... | collective-permute-start | bytes 1916936 | tf_op jit(solution)/shard_map/ppermute | solution.py:29
  38.0 23.4 %collective-permute-start.9 = (bf16[4,104,768]{2,1,0:T(8,128)(2,1)S(1)}, bf16[4,104,768]{2,1,0:T(8,128)(2,1)}, u32[]{:S(2)}, u32[]{:S(2)}) collective-permute-start(bf16[4,104,768]{2,1,0:T(8,128)(2,1)S(1)} %bitcast.97), channel_id=1, source_target_pairs={{0,1},{1,0},{2,3},{3,2},{4,5},{5,4},{6,7},{7,6},{8,9},{9,8},{10,11... | collective-permute-start | bytes 1916936 | tf_op jit(solution)/shard_map/ppermute | solution.py:37
  53.0 13.3 %collective-permute-start.11 = (bf16[4,104,768]{2,1,0:T(8,128)(2,1)S(1)}, bf16[4,104,768]{2,1,0:T(8,128)(2,1)}, u32[]{:S(2)}, u32[]{:S(2)}) collective-permute-start(bf16[4,104,768]{2,1,0:T(8,128)(2,1)S(1)} %collective-permute-done.6.refs_3_.refs_8_.refs_7_), channel_id=1, source_target_pairs={{0,1},{1,0},{2,3},{3,2},{4,5},{5,4},{6,7},{7,6},{8,9},{9,8},{10,11... | collective-permute-start | bytes 1916936 | tf_op jit(solution)/shard_map/ppermute | solution.py:37
  54.7 34.2 %all-to-all-start.2 = ((bf16[4,2,96,768]{3,2,1,0:T(8,128)(2,1)}), bf16[4,2,96,768]{3,2,1,0:T(8,128)(2,1)}, u32[]{:S(2)}, u32[]{:S(2)}) async-start(bf16[4,2,96,768]{3,2,1,0:T(8,128)(2,1)} %broadcast_in_dim.70), calls=%async_computation.2 | async-start | bytes 2359296 | tf_op jit(solution)/shard_map/all_to_all | solution.py:41
  64.9 19.7 %collective-permute-start.15 = (bf16[4,96,768]{2,1,0:T(8,128)(2,1)}, bf16[4,96,768]{2,1,0:T(8,128)(2,1)}, u32[]{:S(2)}, u32[]{:S(2)}) collective-permute-start(bf16[4,96,768]{2,1,0:T(8,128)(2,1)} %bitcast.18.refs_3_.refs_5_), channel_id=1, source_target_pairs={{0,2},{2,0},{1,3},{3,1},{4,6},{6,4},{5,7},{7,5},{8,10},{10,8},{9,1... | collective-permute-start | bytes 1769480 | tf_op jit(solution)/shard_map/ppermute | solution.py:25
  65.5 19.3 %collective-permute-start.16 = (bf16[4,96,768]{2,1,0:T(8,128)(2,1)}, bf16[4,96,768]{2,1,0:T(8,128)(2,1)}, u32[]{:S(2)}, u32[]{:S(2)}) collective-permute-start(bf16[4,96,768]{2,1,0:T(8,128)(2,1)} %bitcast.18.refs_3_.refs_5_), channel_id=1, source_target_pairs={{0,4},{4,0},{1,5},{5,1},{2,6},{6,2},{3,7},{7,3},{8,12},{12,8},{9,1... | collective-permute-start | bytes 1769480 | tf_op jit(solution)/shard_map/ppermute | solution.py:29
  101.5 19.5 %collective-permute-start.21 = (bf16[4,96,768]{2,1,0:T(8,128)(2,1)}, bf16[4,96,768]{2,1,0:T(8,128)(2,1)}, u32[]{:S(2)}, u32[]{:S(2)}) collective-permute-start(bf16[4,96,768]{2,1,0:T(8,128)(2,1)} %collective-permute-done.15.refs_4_.refs_6_), channel_id=1, source_target_pairs={{0,1},{1,0},{2,3},{3,2},{4,5},{5,4},{6,7},{7,6},{8,9},{9,8},{10,11... | collective-permute-start | bytes 1769480 | tf_op jit(solution)/shard_map/ppermute | solution.py:37
  102.0 19.0 %collective-permute-start.22 = (bf16[4,96,768]{2,1,0:T(8,128)(2,1)}, bf16[4,96,768]{2,1,0:T(8,128)(2,1)}, u32[]{:S(2)}, u32[]{:S(2)}) collective-permute-start(bf16[4,96,768]{2,1,0:T(8,128)(2,1)} %collective-permute-done.16.refs_5_.refs_7_), channel_id=1, source_target_pairs={{0,1},{1,0},{2,3},{3,2},{4,5},{5,4},{6,7},{7,6},{8,9},{9,8},{10,11... | collective-permute-start | bytes 1769480 | tf_op jit(solution)/shard_map/ppermute | solution.py:37
  102.0 18.9 %collective-permute-start.24 = (bf16[2,96,768]{2,1,0:T(8,128)(2,1)}, bf16[2,96,768]{2,1,0:T(8,128)(2,1)}, u32[]{:S(2)}, u32[]{:S(2)}) collective-permute-start(bf16[2,96,768]{2,1,0:T(8,128)(2,1)} %collective-permute-done.19.refs_7_.refs_9_), channel_id=1, source_target_pairs={{0,1},{1,0},{2,3},{3,2},{4,5},{5,4},{6,7},{7,6},{8,9},{9,8},{10,11... | collective-permute-start | bytes 884744 | tf_op jit(solution)/shard_map/ppermute | solution.py:37
  102.5 29.3 %collective-permute-start.25 = (bf16[8,96,768]{2,1,0:T(8,128)(2,1)}, bf16[8,96,768]{2,1,0:T(8,128)(2,1)}, u32[]{:S(2)}, u32[]{:S(2)}) collective-permute-start(bf16[8,96,768]{2,1,0:T(8,128)(2,1)} %bitcast.24.refs_7_), channel_id=1, source_target_pairs={{0,2},{2,0},{1,3},{3,1},{4,6},{6,4},{5,7},{7,5},{8,10},{10,8},{9,1... | collective-permute-start | bytes 3538952 | tf_op jit(solution)/shard_map/ppermute | solution.py:25
  104.7 28.0 %collective-permute-start.26 = (bf16[8,96,768]{2,1,0:T(8,128)(2,1)}, bf16[8,96,768]{2,1,0:T(8,128)(2,1)}, u32[]{:S(2)}, u32[]{:S(2)}) collective-permute-start(bf16[8,96,768]{2,1,0:T(8,128)(2,1)} %bitcast.24.refs_7_), channel_id=1, source_target_pairs={{0,4},{4,0},{1,5},{5,1},{2,6},{6,2},{3,7},{7,3},{8,12},{12,8},{9,1... | collective-permute-start | bytes 3538952 | tf_op jit(solution)/shard_map/ppermute | solution.py:29
  120.9 34.0 %collective-permute-start.29 = (bf16[8,96,768]{2,1,0:T(8,128)(2,1)}, bf16[8,96,768]{2,1,0:T(8,128)(2,1)}, u32[]{:S(2)}, u32[]{:S(2)}) collective-permute-start(bf16[8,96,768]{2,1,0:T(8,128)(2,1)} %bitcast.24.refs_7_), channel_id=1, source_target_pairs={{0,1},{1,0},{2,3},{3,2},{4,5},{5,4},{6,7},{7,6},{8,9},{9,8},{10,11... | collective-permute-start | bytes 3538952 | tf_op jit(solution)/shard_map/ppermute | solution.py:37
  136.5 15.5 %collective-permute-start.27 = (bf16[4,96,768]{2,1,0:T(8,128)(2,1)}, bf16[4,96,768]{2,1,0:T(8,128)(2,1)}, u32[]{:S(2)}, u32[]{:S(2)}) collective-permute-start(bf16[4,96,768]{2,1,0:T(8,128)(2,1)} %slice.229), channel_id=1, source_target_pairs={{0,4},{4,0},{1,5},{5,1},{2,6},{6,2},{3,7},{7,3},{8,12},{12,8},{9,1... | collective-permute-start | bytes 1769480 | tf_op jit(solution)/shard_map/ppermute | solution.py:29
  137.3 15.3 %collective-permute-start.28 = (bf16[4,96,768]{2,1,0:T(8,128)(2,1)}, bf16[4,96,768]{2,1,0:T(8,128)(2,1)}, u32[]{:S(2)}, u32[]{:S(2)}) collective-permute-start(bf16[4,96,768]{2,1,0:T(8,128)(2,1)} %slice.230), channel_id=1, source_target_pairs={{0,2},{2,0},{1,3},{3,1},{4,6},{6,4},{5,7},{7,5},{8,10},{10,8},{9,1... | collective-permute-start | bytes 1769480 | tf_op jit(solution)/shard_map/ppermute | solution.py:25
  138.6 16.3 %collective-permute-start.30 = (bf16[8,96,768]{2,1,0:T(8,128)(2,1)}, bf16[8,96,768]{2,1,0:T(8,128)(2,1)}, u32[]{:S(2)}, u32[]{:S(2)}) collective-permute-start(bf16[8,96,768]{2,1,0:T(8,128)(2,1)} %collective-permute-done.25.refs_8_), channel_id=1, source_target_pairs={{0,1},{1,0},{2,3},{3,2},{4,5},{5,4},{6,7},{7,6},{8,9},{9,8},{10,11... | collective-permute-start | bytes 3538952 | tf_op jit(solution)/shard_map/ppermute | solution.py:37
  138.6 16.3 %collective-permute-start.31 = (bf16[8,96,768]{2,1,0:T(8,128)(2,1)}, bf16[8,96,768]{2,1,0:T(8,128)(2,1)}, u32[]{:S(2)}, u32[]{:S(2)}) collective-permute-start(bf16[8,96,768]{2,1,0:T(8,128)(2,1)} %collective-permute-done.26.refs_9_), channel_id=1, source_target_pairs={{0,1},{1,0},{2,3},{3,2},{4,5},{5,4},{6,7},{7,6},{8,9},{9,8},{10,11... | collective-permute-start | bytes 3538952 | tf_op jit(solution)/shard_map/ppermute | solution.py:37
  193.4 25.4 %collective-permute-start.37 = (bf16[32,96,768]{2,1,0:T(8,128)(2,1)}, bf16[32,96,768]{2,1,0:T(8,128)(2,1)}, u32[]{:S(2)}, u32[]{:S(2)}) collective-permute-start(bf16[32,96,768]{2,1,0:T(8,128)(2,1)} %get-tuple-element.184), channel_id=1, source_target_pairs={{0,1},{1,0},{2,3},{3,2},{4,5},{5,4},{6,7},{7,6},{8,9},{9,8},{10,11... | collective-permute-start | bytes 14155784 | tf_op jit(solution)/shard_map/ppermute | solution.py:37
  193.7 29.7 %collective-permute-start.34 = (bf16[2,98,768]{2,1,0:T(8,128)(2,1)}, bf16[2,98,768]{2,1,0:T(8,128)(2,1)}, u32[]{:S(2)}, u32[]{:S(2)}) collective-permute-start(bf16[2,98,768]{2,1,0:T(8,128)(2,1)} %get-tuple-element.180), channel_id=1, source_target_pairs={{0,2},{2,0},{1,3},{3,1},{4,6},{6,4},{5,7},{7,5},{8,10},{10,8},{9,1... | collective-permute-start | bytes 903176 | tf_op jit(solution)/shard_map/ppermute | solution.py:25
  194.6 28.8 %collective-permute-start.35 = (bf16[2,98,768]{2,1,0:T(8,128)(2,1)}, bf16[2,98,768]{2,1,0:T(8,128)(2,1)}, u32[]{:S(2)}, u32[]{:S(2)}) collective-permute-start(bf16[2,98,768]{2,1,0:T(8,128)(2,1)} %get-tuple-element.181), channel_id=1, source_target_pairs={{0,4},{4,0},{1,5},{5,1},{2,6},{6,2},{3,7},{7,3},{8,12},{12,8},{9,1... | collective-permute-start | bytes 903176 | tf_op jit(solution)/shard_map/ppermute | solution.py:29
  195.4 28.0 %collective-permute-start.36 = (bf16[2,98,768]{2,1,0:T(8,128)(2,1)}, bf16[2,98,768]{2,1,0:T(8,128)(2,1)}, u32[]{:S(2)}, u32[]{:S(2)}) collective-permute-start(bf16[2,98,768]{2,1,0:T(8,128)(2,1)} %get-tuple-element.182), channel_id=1, source_target_pairs={{0,6},{2,4},{4,2},{6,0},{1,7},{3,5},{5,3},{7,1},{8,14},{10,12},{12... | collective-permute-start | bytes 903176 | tf_op jit(solution)/shard_map/ppermute | solution.py:33
  221.6 15.1 %collective-permute-start.38 = (bf16[4,96,768]{2,1,0:T(8,128)(2,1)}, bf16[4,96,768]{2,1,0:T(8,128)(2,1)}, u32[]{:S(2)}, u32[]{:S(2)}) collective-permute-start(bf16[4,96,768]{2,1,0:T(8,128)(2,1)} %get-tuple-element.186), channel_id=1, source_target_pairs={{0,4},{4,0},{1,5},{5,1},{2,6},{6,2},{3,7},{7,3},{8,12},{12,8},{9,1... | collective-permute-start | bytes 1769480 | tf_op jit(solution)/shard_map/ppermute | solution.py:29
  222.4 14.8 %collective-permute-start.39 = (bf16[4,96,768]{2,1,0:T(8,128)(2,1)}, bf16[4,96,768]{2,1,0:T(8,128)(2,1)}, u32[]{:S(2)}, u32[]{:S(2)}) collective-permute-start(bf16[4,96,768]{2,1,0:T(8,128)(2,1)} %get-tuple-element.187), channel_id=1, source_target_pairs={{0,2},{2,0},{1,3},{3,1},{4,6},{6,4},{5,7},{7,5},{8,10},{10,8},{9,1... | collective-permute-start | bytes 1769480 | tf_op jit(solution)/shard_map/ppermute | solution.py:25
  237.2 18.8 %collective-permute-start.40 = (bf16[16,96,768]{2,1,0:T(8,128)(2,1)}, bf16[16,96,768]{2,1,0:T(8,128)(2,1)}, u32[]{:S(2)}, u32[]{:S(2)}) collective-permute-start(bf16[16,96,768]{2,1,0:T(8,128)(2,1)} %get-tuple-element.197), channel_id=1, source_target_pairs={{0,1},{1,0},{2,3},{3,2},{4,5},{5,4},{6,7},{7,6},{8,9},{9,8},{10,11... | collective-permute-start | bytes 7077896 | tf_op jit(solution)/shard_map/ppermute | solution.py:37
  241.7 39.5 %collective-permute-start.41 = (bf16[8,96,768]{2,1,0:T(8,128)(2,1)}, bf16[8,96,768]{2,1,0:T(8,128)(2,1)}, u32[]{:S(2)}, u32[]{:S(2)}) collective-permute-start(bf16[8,96,768]{2,1,0:T(8,128)(2,1)} %get-tuple-element.193), channel_id=1, source_target_pairs={{0,2},{2,0},{1,3},{3,1},{4,6},{6,4},{5,7},{7,5},{8,10},{10,8},{9,1... | collective-permute-start | bytes 3538952 | tf_op jit(solution)/shard_map/ppermute | solution.py:25
  242.6 38.5 %collective-permute-start.42 = (bf16[8,96,768]{2,1,0:T(8,128)(2,1)}, bf16[8,96,768]{2,1,0:T(8,128)(2,1)}, u32[]{:S(2)}, u32[]{:S(2)}) collective-permute-start(bf16[8,96,768]{2,1,0:T(8,128)(2,1)} %get-tuple-element.194), channel_id=1, source_target_pairs={{0,4},{4,0},{1,5},{5,1},{2,6},{6,2},{3,7},{7,3},{8,12},{12,8},{9,1... | collective-permute-start | bytes 3538952 | tf_op jit(solution)/shard_map/ppermute | solution.py:29
  258.1 23.1 %collective-permute-start.43 = (bf16[2,96,768]{2,1,0:T(8,128)(2,1)}, bf16[2,96,768]{2,1,0:T(8,128)(2,1)}, u32[]{:S(2)}, u32[]{:S(2)}) collective-permute-start(bf16[2,96,768]{2,1,0:T(8,128)(2,1)} %get-tuple-element.199), channel_id=1, source_target_pairs={{0,4},{4,0},{1,5},{5,1},{2,6},{6,2},{3,7},{7,3},{8,12},{12,8},{9,1... | collective-permute-start | bytes 884744 | tf_op jit(solution)/shard_map/ppermute | solution.py:29
  258.9 22.3 %collective-permute-start.44 = (bf16[2,96,768]{2,1,0:T(8,128)(2,1)}, bf16[2,96,768]{2,1,0:T(8,128)(2,1)}, u32[]{:S(2)}, u32[]{:S(2)}) collective-permute-start(bf16[2,96,768]{2,1,0:T(8,128)(2,1)} %get-tuple-element.200), channel_id=1, source_target_pairs={{0,2},{2,0},{1,3},{3,1},{4,6},{6,4},{5,7},{7,5},{8,10},{10,8},{9,1... | collective-permute-start | bytes 884744 | tf_op jit(solution)/shard_map/ppermute | solution.py:25
  284.1 24.1 %all-to-all-start.3 = ((bf16[4,1,96,768]{3,2,1,0:T(8,128)(2,1)}), bf16[4,1,96,768]{3,2,1,0:T(8,128)(2,1)}, u32[]{:S(2)}, u32[]{:S(2)}) async-start(bf16[4,1,96,768]{3,2,1,0:T(8,128)(2,1)} %bitcast.94), calls=%async_computation.3 | async-start | bytes 1179648 | tf_op jit(solution)/shard_map/all_to_all | solution.py:41
  291.2 17.0 %collective-permute-start.46 = (bf16[4,96,768]{2,1,0:T(8,128)(2,1)}, bf16[4,96,768]{2,1,0:T(8,128)(2,1)}, u32[]{:S(2)}, u32[]{:S(2)}) collective-permute-start(bf16[4,96,768]{2,1,0:T(8,128)(2,1)} %get-tuple-element.212), channel_id=1, source_target_pairs={{0,2},{2,0},{1,3},{3,1},{4,6},{6,4},{5,7},{7,5},{8,10},{10,8},{9,1... | collective-permute-start | bytes 1769480 | tf_op jit(solution)/shard_map/ppermute | solution.py:25
  292.1 16.1 %collective-permute-start.47 = (bf16[4,96,768]{2,1,0:T(8,128)(2,1)}, bf16[4,96,768]{2,1,0:T(8,128)(2,1)}, u32[]{:S(2)}, u32[]{:S(2)}) collective-permute-start(bf16[4,96,768]{2,1,0:T(8,128)(2,1)} %get-tuple-element.213), channel_id=1, source_target_pairs={{0,4},{4,0},{1,5},{5,1},{2,6},{6,2},{3,7},{7,3},{8,12},{12,8},{9,1... | collective-permute-start | bytes 1769480 | tf_op jit(solution)/shard_map/ppermute | solution.py:29
  315.3 16.5 %collective-permute-start.49 = (bf16[2,96,768]{2,1,0:T(8,128)(2,1)}, bf16[2,96,768]{2,1,0:T(8,128)(2,1)}, u32[]{:S(2)}, u32[]{:S(2)}) collective-permute-start(bf16[2,96,768]{2,1,0:T(8,128)(2,1)} %get-tuple-element.220), channel_id=1, source_target_pairs={{0,4},{4,0},{1,5},{5,1},{2,6},{6,2},{3,7},{7,3},{8,12},{12,8},{9,1... | collective-permute-start | bytes 884744 | tf_op jit(solution)/shard_map/ppermute | solution.py:29
  316.1 15.7 %collective-permute-start.50 = (bf16[2,96,768]{2,1,0:T(8,128)(2,1)}, bf16[2,96,768]{2,1,0:T(8,128)(2,1)}, u32[]{:S(2)}, u32[]{:S(2)}) collective-permute-start(bf16[2,96,768]{2,1,0:T(8,128)(2,1)} %get-tuple-element.221), channel_id=1, source_target_pairs={{0,2},{2,0},{1,3},{3,1},{4,6},{6,4},{5,7},{7,5},{8,10},{10,8},{9,1... | collective-permute-start | bytes 884744 | tf_op jit(solution)/shard_map/ppermute | solution.py:25
  326.7 40.8 %all-to-all-start.4 = ((bf16[4,2,96,768]{3,2,1,0:T(8,128)(2,1)}), bf16[4,2,96,768]{3,2,1,0:T(8,128)(2,1)}, u32[]{:S(2)}, u32[]{:S(2)}) async-start(bf16[4,2,96,768]{3,2,1,0:T(8,128)(2,1)} %bitcast.93), calls=%async_computation.4 | async-start | bytes 2359296 | tf_op jit(solution)/shard_map/all_to_all | solution.py:41
  334.7 14.8 %collective-permute-start.51 = (bf16[4,96,768]{2,1,0:T(8,128)(2,1)}, bf16[4,96,768]{2,1,0:T(8,128)(2,1)}, u32[]{:S(2)}, u32[]{:S(2)}) collective-permute-start(bf16[4,96,768]{2,1,0:T(8,128)(2,1)} %get-tuple-element.226), channel_id=1, source_target_pairs={{0,2},{2,0},{1,3},{3,1},{4,6},{6,4},{5,7},{7,5},{8,10},{10,8},{9,1... | collective-permute-start | bytes 1769480 | tf_op jit(solution)/shard_map/ppermute | solution.py:25
  335.6 14.6 %collective-permute-start.52 = (bf16[4,96,768]{2,1,0:T(8,128)(2,1)}, bf16[4,96,768]{2,1,0:T(8,128)(2,1)}, u32[]{:S(2)}, u32[]{:S(2)}) collective-permute-start(bf16[4,96,768]{2,1,0:T(8,128)(2,1)} %get-tuple-element.227), channel_id=1, source_target_pairs={{0,4},{4,0},{1,5},{5,1},{2,6},{6,2},{3,7},{7,3},{8,12},{12,8},{9,1... | collective-permute-start | bytes 1769480 | tf_op jit(solution)/shard_map/ppermute | solution.py:29
  352.9 18.4 %collective-permute-start.56 = (bf16[1,96,768]{2,1,0:T(8,128)(2,1)}, bf16[1,96,768]{2,1,0:T(8,128)(2,1)S(1)}, u32[]{:S(2)}, u32[]{:S(2)}) collective-permute-start(bf16[1,96,768]{2,1,0:T(8,128)(2,1)} %get-tuple-element.237), channel_id=1, source_target_pairs={{0,8},{8,16},{16,24},{24,0},{1,9},{9,17},{17,25},{25,1},{2,10},{10... | collective-permute-start | bytes 442376 | tf_op jit(solution)/shard_map/ppermute | solution.py:165
  354.6 24.1 %collective-permute-start.57 = (bf16[1,96,768]{2,1,0:T(8,128)(2,1)}, bf16[1,96,768]{2,1,0:T(8,128)(2,1)S(1)}, u32[]{:S(2)}, u32[]{:S(2)}) collective-permute-start(bf16[1,96,768]{2,1,0:T(8,128)(2,1)} %get-tuple-element.238), channel_id=1, source_target_pairs={{0,16},{8,24},{16,0},{24,8},{1,17},{9,25},{17,1},{25,9},{2,18},{10... | collective-permute-start | bytes 442376 | tf_op jit(solution)/shard_map/ppermute | solution.py:165
  357.0 21.8 %collective-permute-start.53 = (bf16[2,98,768]{2,1,0:T(8,128)(2,1)}, bf16[2,98,768]{2,1,0:T(8,128)(2,1)S(1)}, u32[]{:S(2)}, u32[]{:S(2)}) collective-permute-start(bf16[2,98,768]{2,1,0:T(8,128)(2,1)} %get-tuple-element.249), channel_id=1, source_target_pairs={{0,2},{2,0},{1,3},{3,1},{4,6},{6,4},{5,7},{7,5},{8,10},{10,8},{9,1... | collective-permute-start | bytes 903176 | tf_op jit(solution)/shard_map/ppermute | solution.py:25
  358.1 20.6 %collective-permute-start.54 = (bf16[2,98,768]{2,1,0:T(8,128)(2,1)}, bf16[2,98,768]{2,1,0:T(8,128)(2,1)S(1)}, u32[]{:S(2)}, u32[]{:S(2)}) collective-permute-start(bf16[2,98,768]{2,1,0:T(8,128)(2,1)} %get-tuple-element.250), channel_id=1, source_target_pairs={{0,4},{4,0},{1,5},{5,1},{2,6},{6,2},{3,7},{7,3},{8,12},{12,8},{9,1... | collective-permute-start | bytes 903176 | tf_op jit(solution)/shard_map/ppermute | solution.py:29
  359.3 19.4 %collective-permute-start.55 = (bf16[2,98,768]{2,1,0:T(8,128)(2,1)}, bf16[2,98,768]{2,1,0:T(8,128)(2,1)S(1)}, u32[]{:S(2)}, u32[]{:S(2)}) collective-permute-start(bf16[2,98,768]{2,1,0:T(8,128)(2,1)} %get-tuple-element.251), channel_id=1, source_target_pairs={{0,6},{2,4},{4,2},{6,0},{1,7},{3,5},{5,3},{7,1},{8,14},{10,12},{12... | collective-permute-start | bytes 903176 | tf_op jit(solution)/shard_map/ppermute | solution.py:33
  (52 other events, 323.3 us)

commit v4 on v3

--- a/solution.py
+++ b/solution.py
@@ -1112,6 +1112,34 @@
     return jnp.stack([q, k, v], axis=1), o.T
 
 
+def join_clips(meta, blocks, dtype):
+    shape = blocks[0].shape
+
+    def kernel(meta, *refs):
+        for k in range(4):
+
+            @pl.when(pl.program_id(0) == k)
+            def _(k=k):
+                refs[4][0] = refs[k][...].astype(dtype)
+
+    def place(k, m):
+        return (2 * (m[0] ^ (k & 1)) + (m[1] ^ (k >> 1)), 0, 0, 0)
+
+    return pl.pallas_call(
+        kernel,
+        name="join_clips",
+        grid_spec=pltpu.PrefetchScalarGridSpec(
+            num_scalar_prefetch=1,
+            grid=(4,),
+            in_specs=[pl.BlockSpec(shape, lambda k, m: (0, 0, 0))] * 4,
+            out_specs=pl.BlockSpec((1,) + shape, place),
+        ),
+        out_shape=jax.ShapeDtypeStruct((4,) + shape, dtype),
+        compiler_params=pltpu.CompilerParams(vmem_limit_bytes=VMEM_LIMIT),
+        cost_estimate=pl.CostEstimate(flops=10**8, bytes_accessed=10**5, transcendentals=0),
+    )(meta, *blocks)
+
+
 def local(mesh_shape, video, cotangent, *params):
     qkv_time, proj_time, qkv_space, proj_space, fc_in, fc_out = params[:6]
     vectors = params[6:]
@@ -1147,13 +1175,6 @@
 
     def frames_back(blocks):
         return [blocks[0], over_x(blocks[1]), over_y(blocks[2]), over_xy(blocks[3])]
-
-    def join_clips(blocks, dtype):
-        out = jnp.zeros((4,) + blocks[0].shape, dtype)
-        for k, b in enumerate(blocks):
-            at = 2 * (x ^ (k % 2)) + (y ^ (k // 2))
-            out = lax.dynamic_update_slice_in_dim(out, b.astype(dtype)[None], at, 0)
-        return out
 
     g_t = gather([first_rows], n)
     g_s = gather([pack_heads(qkv_space, proj_space, c == 1)], n)
@@ -1250,7 +1271,7 @@
         axis=1,
     )
     got_parts = lax.all_to_all(parts, every, split_axis=0, concat_axis=0, tiled=True)
-    result = join_clips(result_back, B16)
+    result = join_clips(meta, result_back, B16)
     if fast:
         vec_got, video_back, r_t.z, joint, first = lax.optimization_barrier(
             (got_parts, tuple(video_back), tuple(r_t.z), got, first_z[0])
@@ -1263,7 +1284,7 @@
         grad_in, grad_out = r_m.results()
         (grad_s,) = r_s.results()
     (grad_t,) = r_t.results()
-    grad_video = join_clips(video_back, F32)
+    grad_video = join_clips(meta, video_back, F32)
     sums = jnp.sum(vec_got, axis=0)
     starts = [per * i for i in range(9)] + [per * 12]
     cuts = [sums[starts[i] : starts[i] + (4 * per if i == 8 else per)] for i in range(10)]

time: 396 us -> 411 us (1.038)
  Pallas kernels: 211 us -> 219 us
    ppermute x16, waiting for transfers between devices: 13.4 us -> 26.1 us  [over_y(): return lax.ppermute(v, 'ctx', FLIP)]
    unnamed x97 -> x89, local copies, waits for them, and re-layouts: 3.75 us -> 12.7 us
    pallas_call x0 -> x2, Pallas kernels: none -> 7.62 us  [join_clips(): pl.pallas_call(kernel, name='join_clips', grid_spec=pltpu.PrefetchScalarG...]
    dynamic_update_slice x8 -> x0, local copies, waits for them, and re-layouts: 5.44 us -> none  [join_clips(): out = lax.dynamic_update_slice_in_dim(out, b.astype(dtype)[None], at, 0)]
    ppermute x16, waiting for transfers between devices: 18.1 us -> 13.6 us  [over_x(): return lax.ppermute(v, 'x', FLIP)]
  transfers between devices with their start and end apart: 65 -> 65, of which waited for: 21 -> 22; matrix products, arithmetic and copies ran while one was open for 7% -> 6% of each run, Pallas kernels for 44% -> 42%
where the time goes in v4:
time: 411 us; the launch traced here: 405 us
  Pallas kernels  219 us (53%)
  starting transfers between devices  77.1 us (19%)
  waiting for transfers between devices  60.1 us (15%)
  local copies, waits for them, and re-layouts  38.4 us (9%)
  other arithmetic  9.36 us (2%)
    pallas_call x12, Pallas kernels, run(): pl.pallas_call(body, name=name, in_specs=[space[s] for _, s in ins], out_...  184 us
    pallas_call x9, Pallas kernels, block_sums(): pl.pallas_call(kernel, name=name, grid=(1,), in_specs=[spec(blocks, index...  26.8 us
    ppermute x16, waiting for transfers between devices, over_y(): return lax.ppermute(v, 'ctx', FLIP)  26.1 us
    all_to_all x5, starting transfers between devices, over_z(): return lax.all_to_all(v, 'shard', split_axis=0, concat_axis=0, tiled=True)  25.2 us
    ppermute x16, starting transfers between devices, over_y(): return lax.ppermute(v, 'ctx', FLIP)  18.1 us
    ppermute x16, starting transfers between devices, over_x(): return lax.ppermute(v, 'x', FLIP)  14.7 us
    ppermute x16, waiting for transfers between devices, over_x(): return lax.ppermute(v, 'x', FLIP)  13.6 us
    unnamed x89, local copies, waits for them, and re-layouts  12.7 us
  transfers between devices with their start and end apart: 65, of which 22 were waited for; matrix products, arithmetic and copies ran while one was open for 6% of the time, Pallas kernels for 42%

profile of v4, /device:TPU:0, one launch (start us, length us, event | category | flops | bytes accessed | tf_op | source)
XLA Modules:
  0.0 405.4 jit_solution(11196261766289490364)
XLA Ops:
  5.9 6.3 %all-to-all-start = ((bf16[4,1,104,768]{3,2,1,0:T(8,128)(2,1)}), bf16[4,1,104,768]{3,2,1,0:T(8,128)(2,1)S(1)}, u32[]{:S(2)}, u32[]{:S(2)}) async-start(bf16[4,1,104,768]{3,2,1,0:T(8,128)(2,1)} %broadcast_in_dim.28), calls=%async_computation | async-start | bytes 1277952 | tf_op jit(solution)/shard_map/all_to_all | solution.py:41
  15.4 1.6 collective-permute-start.1
  22.6 6.5 %all-to-all-done = bf16[4,1,104,768]{3,2,1,0:T(8,128)(2,1)S(1)} async-done(((bf16[4,1,104,768]{3,2,1,0:T(8,128)(2,1)}), bf16[4,1,104,768]{3,2,1,0:T(8,128)(2,1)S(1)}, u32[]{:S(2)}, u32[]{:S(2)}) %all-to-all-start) | async-done | bytes 639008 | tf_op jit(solution)/shard_map/all_to_all | solution.py:41
  29.2 4.2 %all-to-all-start.1 = ((bf16[4,1,96,768]{3,2,1,0:T(8,128)(2,1)}), bf16[4,1,96,768]{3,2,1,0:T(8,128)(2,1)}, u32[]{:S(2)}, u32[]{:S(2)}) async-start(bf16[4,1,96,768]{3,2,1,0:T(8,128)(2,1)} %broadcast_in_dim.29), calls=%async_computation.1 | async-start | bytes 1179648 | tf_op jit(solution)/shard_map/all_to_all | solution.py:41
  33.4 3.3 collective-permute-done.3.refs_3_
  40.0 12.6 %collective-permute-done.6.refs_3_.refs_8_.refs_7_ = bf16[4,104,768]{2,1,0:T(8,128)(2,1)S(1)} collective-permute-done((bf16[4,104,768]{2,1,0:T(8,128)(2,1)S(1)}, bf16[4,104,768]{2,1,0:T(8,128)(2,1)S(1)}, u32[]{:S(2)}, u32[]{:S(2)}) %collective-permute-start.6) | collective-permute-done | bytes 639008 | tf_op jit(solution)/shard_map/ppermute | solution.py:29
  57.6 5.4 %all-to-all-start.2 = ((bf16[4,2,96,768]{3,2,1,0:T(8,128)(2,1)}), bf16[4,2,96,768]{3,2,1,0:T(8,128)(2,1)}, u32[]{:S(2)}, u32[]{:S(2)}) async-start(bf16[4,2,96,768]{3,2,1,0:T(8,128)(2,1)} %broadcast_in_dim.30), calls=%async_computation.2 | async-start | bytes 2359296 | tf_op jit(solution)/shard_map/all_to_all | solution.py:41
  64.3 2.5 collective-permute-start.14
  69.3 3.0 norm_vectors.1.refs_1_
  72.4 3.6 collective-permute-done.14.refs_5_
  76.0 10.3 %time_qkv.1 = (f32[832,768]{1,0:T(8,128)}, bf16[832,768]{1,0:T(8,128)(2,1)}, bf16[6,832,128]{2,1,0:T(8,128)(2,1)}, bf16[12,832,128]{2,1,0:T(8,128)(2,1)}) custom-call(s32[4]{0:T(128)} %pad_add_fusion.refs_0_.meta, f32[16,768]{1,0:T(8,128)} %norm_vectors.1.refs_1_, bf16[2,98,768]{2,1,0:T(8,128)(2,1)} %bitcast.93, ...), custom_call_target="tpu_custom_call" | custom-call | flops 12000000000 | bytes 36000000 | tf_op jit(solution)/shard_map/time_qkv/pallas_call | solution.py:414
  87.8 3.9 all-to-all-done.2
  96.9 6.4 %collective-permute-done.19.refs_7_.refs_9_ = bf16[2,96,768]{2,1,0:T(8,128)(2,1)} collective-permute-done((bf16[2,96,768]{2,1,0:T(8,128)(2,1)S(1)}, bf16[2,96,768]{2,1,0:T(8,128)(2,1)}, u32[]{:S(2)}, u32[]{:S(2)}) %collective-permute-start.19) | collective-permute-done | bytes 294944 | tf_op jit(solution)/shard_map/ppermute | solution.py:25
  109.0 15.4 %time_mix.1 = (bf16[6,832,128]{2,1,0:T(8,128)(2,1)}, f32[832,768]{1,0:T(8,128)}, f32[8,208,128]{2,1,0:T(8,128)}) custom-call(s32[4]{0:T(128)} %pad_add_fusion.refs_0_.meta, f32[16,768]{1,0:T(8,128)} %norm_vectors.1.refs_1_, f32[832,768]{1,0:T(8,128)} %get-tuple-element.153.refs_2_.refs_3_, bf16[6,832,128]{2,1,0:T(8,128)(2,1)} %get-tuple-element.154.refs_3_.refs_2_, ...), custom_call_target="tpu_custom_call" | custom-call | flops 16999999488 | bytes 51000000 | tf_op jit(solution)/shard_map/time_mix/pallas_call | solution.py:414
  124.6 10.9 %space_qkv.1 = (bf16[832,768]{1,0:T(8,128)(2,1)}, bf16[6,832,128]{2,1,0:T(8,128)(2,1)}, bf16[12,832,128]{2,1,0:T(8,128)(2,1)}) custom-call(s32[4]{0:T(128)} %pad_add_fusion.refs_0_.meta, f32[16,768]{1,0:T(8,128)} %norm_vectors.1.refs_1_, f32[832,768]{1,0:T(8,128)} %get-tuple-element.162.refs_2_.refs_3_, bf16[4,96,768]{2,1,0:T(8,128)(2,1)} %bitcast.18.refs_3_.refs_5_, ...), custom_call_target="tpu_custom_call" | custom-call | flops 12000000000 | bytes 36000000 | tf_op jit(solution)/shard_map/space_qkv/pallas_call | solution.py:414
  136.5 1.9 slice.229
  138.4 1.9 slice.230
  142.6 12.9 %space_mix.1 = (bf16[6,832,128]{2,1,0:T(8,128)(2,1)}, f32[24,8,208]{2,1,0:T(8,128)}, f32[832,768]{1,0:T(8,128)}) custom-call(s32[4]{0:T(128)} %pad_add_fusion.refs_0_.meta, f32[16,768]{1,0:T(8,128)} %norm_vectors.1.refs_1_, f32[832,768]{1,0:T(8,128)} %get-tuple-element.162.refs_2_.refs_3_, bf16[6,832,128]{2,1,0:T(8,128)(2,1)} %get-tuple-element.165.refs_3_.refs_2_, ...), custom_call_target="tpu_custom_call" | custom-call | flops 16999999488 | bytes 51000000 | tf_op jit(solution)/shard_map/space_mix/pallas_call | solution.py:414
  157.1 1.7 copy.118
  159.7 37.6 %feed_forward.1 = (bf16[2,98,768]{2,1,0:T(8,128)(2,1)}, bf16[2,98,768]{2,1,0:T(8,128)(2,1)}, bf16[2,98,768]{2,1,0:T(8,128)(2,1)}, bf16[2,98,768]{2,1,0:T(8,128)(...) custom-call(s32[4]{0:T(128)} %pad_add_fusion.refs_0_.meta, ...), custom_call_target="tpu_custom_call" | custom-call | flops 46999998464 | bytes 141000000 | tf_op jit(solution)/shard_map/feed_forward/pallas_call | solution.py:414
  199.2 1.9 collective-permute-start.36
  201.1 21.7 %space_backward_scores.1 = (bf16[832,768]{1,0:T(8,128)(2,1)}, bf16[4,832,640]{2,1,0:T(8,128)(2,1)}) custom-call(s32[4]{0:T(128)} %pad_add_fusion.refs_0_.meta, f32[832,768]{1,0:T(8,128)} %get-tuple-element.195.refs_1_.refs_2_, bf16[6,832,128]{2,1,0:T(8,128)(2,1)} %get-tuple-element.165.refs_3_.refs_2_, ...), custom_call_target="tpu_custom_call" | custom-call | flops 30000001024 | bytes 90000000 | tf_op jit(solution)/shard_map/space_backward_scores/pallas_call | solution.py:414
  222.8 2.7 mlp_rest.1
  227.1 12.2 %space_weights.1 = (bf16[16,96,768]{2,1,0:T(8,128)(2,1)}, bf16[16,96,768]{2,1,0:T(8,128)(2,1)}) custom-call(s32[4]{0:T(128)} %pad_add_fusion.refs_0_.meta, bf16[832,768]{1,0:T(8,128)(2,1)} %get-tuple-element.175.refs_1_, bf16[832,768]{1,0:T(8,128)(2,1)} %get-tuple-element.176.refs_2_, bf16[6,832,128]{2,1,0:T(8,128)(2,1)} %get-tuple-element.177.refs_3_, ...), custom_call_target="tpu_custom_call" | custom-call | flops 14000000000 | bytes 42000000 | tf_op jit(solution)/shard_map/space_weights/pallas_call | solution.py:414
  241.3 4.4 %mlp_xy.1 = (bf16[8,96,768]{2,1,0:T(8,128)(2,1)}, bf16[8,96,768]{2,1,0:T(8,128)(2,1)}) custom-call(bf16[32,96,768]{2,1,0:T(8,128)(2,1)} %get-tuple-element.183.refs_0_.refs_2_.refs_3_.refs_4_.refs_8_.refs_12_.refs_16_.refs_20_.refs_24_.refs_28_, ...), custom_call_target="tpu_custom_call" | custom-call | flops 100000000 | bytes 100000 | tf_op jit(solution)/shard_map/mlp_xy/pallas_call | solution.py:104
  247.3 12.3 %space_input.1 = (f32[832,768]{1,0:T(8,128)}, f32[8,768]{1,0:T(8,128)}) custom-call(s32[4]{0:T(128)} %pad_add_fusion.refs_0_.meta, f32[16,768]{1,0:T(8,128)} %norm_vectors.1.refs_1_, f32[832,768]{1,0:T(8,128)} %get-tuple-element.195.refs_1_.refs_2_, f32[832,768]{1,0:T(8,128)} %get-tuple-element.162.refs_2_.refs_3_, ...), custom_call_target="tpu_custom_call" | custom-call | flops 14000000000 | bytes 42000000 | tf_op jit(solution)/shard_map/space_input/pallas_call | solution.py:414
  259.6 2.1 space_rest.1
  264.1 21.2 %time_backward_scores.1 = (bf16[832,768]{1,0:T(8,128)(2,1)}, bf16[6,832,128]{2,1,0:T(8,128)(2,1)}, bf16[12,832,128]{2,1,0:T(8,128)(2,1)}, bf16[12,832,128]{2,1,0:T(8,128)(2,1)}) custom-call(s32[4]{0:T(128)} %pad_add_fusion.refs_0_.meta, f32[832,768]{1,0:T(8,128)} %get-tuple-element.228.refs_1_.refs_2_, ...), custom_call_target="tpu_custom_call" | custom-call | flops 23000000512 | bytes 69000000 | tf_op jit(solution)/shard_map/time_backward_scores/pallas_call | solution.py:414
  285.4 2.8 mlp_z.1
  288.2 4.1 %all-to-all-start.3 = ((bf16[4,1,96,768]{3,2,1,0:T(8,128)(2,1)}), bf16[4,1,96,768]{3,2,1,0:T(8,128)(2,1)}, u32[]{:S(2)}, u32[]{:S(2)}) async-start(bf16[4,1,96,768]{3,2,1,0:T(8,128)(2,1)} %bitcast.80), calls=%async_computation.3 | async-start | bytes 1179648 | tf_op jit(solution)/shard_map/all_to_all | solution.py:41
  292.4 3.0 space_xy.1
  297.0 14.8 %time_weights.1 = (bf16[4,832,640]{2,1,0:T(8,128)(2,1)}, bf16[16,96,768]{2,1,0:T(8,128)(2,1)}, bf16[16,96,768]{2,1,0:T(8,128)(2,1)}) custom-call(s32[4]{0:T(128)} %pad_add_fusion.refs_0_.meta, bf16[832,768]{1,0:T(8,128)(2,1)} %get-tuple-element.203.refs_1_, bf16[832,768]{1,0:T(8,128)(2,1)} %get-tuple-element.204.refs_2_, ...), custom_call_target="tpu_custom_call" | custom-call | flops 14000000000 | bytes 42000000 | tf_op jit(solution)/shard_map/time_weights/pallas_call | solution.py:414
  312.0 4.9 %collective-permute-done.48.refs_1_.refs_3_.refs_4_.refs_5_.refs_9_.refs_13_ = bf16[16,96,768]{2,1,0:T(8,128)(2,1)} collective-permute-done((bf16[16,96,768]{2,1,0:T(8,128)(2,1)}, bf16[16,96,768]{2,1,0:T(8,128)(2,1)}, u32[]{:S(2)}, u32[]{:S(2)}) %collective-permute-start.48) | collective-permute-done | bytes 2359328 | tf_op jit(solution)/shard_map/ppermute | solution.py:37
  316.8 2.1 time_rest.1
  318.9 4.0 joint_z.1
  323.0 5.2 %all-to-all-start.4 = ((bf16[4,2,96,768]{3,2,1,0:T(8,128)(2,1)}), bf16[4,2,96,768]{3,2,1,0:T(8,128)(2,1)}, u32[]{:S(2)}, u32[]{:S(2)}) async-start(bf16[4,2,96,768]{3,2,1,0:T(8,128)(2,1)} %bitcast.79), calls=%async_computation.4 | async-start | bytes 2359296 | tf_op jit(solution)/shard_map/all_to_all | solution.py:41
  330.6 6.5 %collective-permute-done.49.refs_2_ = bf16[2,96,768]{2,1,0:T(8,128)(2,1)} collective-permute-done((bf16[2,96,768]{2,1,0:T(8,128)(2,1)S(1)}, bf16[2,96,768]{2,1,0:T(8,128)(2,1)}, u32[]{:S(2)}, u32[]{:S(2)}) %collective-permute-start.49) | collective-permute-done | bytes 294944 | tf_op jit(solution)/shard_map/ppermute | solution.py:29
  337.8 3.0 time_xy.1
  343.2 11.8 %time_input.1 = (f32[2,98,768]{2,1,0:T(8,128)}, bf16[2,98,768]{2,1,0:T(8,128)(2,1)}, bf16[2,98,768]{2,1,0:T(8,128)(2,1)}, bf16[2,98,768]{2,1,0:T(8,128)(2,1)}, f32[8,768]{1,0:T(8,128)}) custom-call(s32[4]{0:T(128)} %pad_add_fusion.refs_0_.meta, f32[16,768]{1,0:T(8,128)} %norm_vectors.1.refs_1_, f32[832,768]{1,0:T(8,128)} %get-tuple-element.228.refs_1_.refs_2_, ...), custom_call_target="tpu_custom_call" | custom-call | flops 14000000000 | bytes 42000000 | tf_op jit(solution)/shard_map/time_input/pallas_call | solution.py:414
  356.1 2.6 time_z.1
  363.3 2.4 collective-permute-start.57
  367.3 1.8 collective-permute-start.55
  372.5 3.4 all-to-all-start.5
  375.9 3.6 join_clips.2
  379.5 3.3 copy.98
  392.2 1.9 convert_reduce_fusion.1
  394.9 4.0 join_clips.3
  399.0 4.5 %copy.99 = f32[4,2,98,768]{3,1,2,0:T(2,128)} copy(f32[4,2,98,768]{3,2,1,0:T(8,128)} %join_clips.3) | data formatting | bytes 4816896
  (266 shorter events, 83.1 us)
Async XLA Ops:
  5.9 23.3 %all-to-all-start = ((bf16[4,1,104,768]{3,2,1,0:T(8,128)(2,1)}), bf16[4,1,104,768]{3,2,1,0:T(8,128)(2,1)S(1)}, u32[]{:S(2)}, u32[]{:S(2)}) async-start(bf16[4,1,104,768]{3,2,1,0:T(8,128)(2,1)} %broadcast_in_dim.28), calls=%async_computation | async-start | bytes 1277952 | tf_op jit(solution)/shard_map/all_to_all | solution.py:41
  13.8 19.5 %collective-permute-start = (bf16[2,98,768]{2,1,0:T(8,128)(2,1)S(1)}, bf16[2,98,768]{2,1,0:T(8,128)(2,1)S(1)}, u32[]{:S(2)}, u32[]{:S(2)}) collective-permute-start(bf16[2,98,768]{2,1,0:T(8,128)(2,1)S(1)} %bitcast.90), channel_id=1, source_target_pairs={{0,2},{2,0},{1,3},{3,1},{4,6},{6,4},{5,7},{7,5},{8,10},{10,8},{9,1... | collective-permute-start | bytes 903176 | tf_op jit(solution)/shard_map/ppermute | solution.py:25
  15.4 18.0 %collective-permute-start.1 = (bf16[2,98,768]{2,1,0:T(8,128)(2,1)S(1)}, bf16[2,98,768]{2,1,0:T(8,128)(2,1)}, u32[]{:S(2)}, u32[]{:S(2)}) collective-permute-start(bf16[2,98,768]{2,1,0:T(8,128)(2,1)S(1)} %bitcast.91), channel_id=1, source_target_pairs={{0,4},{4,0},{1,5},{5,1},{2,6},{6,2},{3,7},{7,3},{8,12},{12,8},{9,1... | collective-permute-start | bytes 903176 | tf_op jit(solution)/shard_map/ppermute | solution.py:29
  17.0 16.3 %collective-permute-start.2 = (bf16[2,98,768]{2,1,0:T(8,128)(2,1)S(1)}, bf16[2,98,768]{2,1,0:T(8,128)(2,1)}, u32[]{:S(2)}, u32[]{:S(2)}) collective-permute-start(bf16[2,98,768]{2,1,0:T(8,128)(2,1)S(1)} %bitcast.92), channel_id=1, source_target_pairs={{0,6},{2,4},{4,2},{6,0},{1,7},{3,5},{5,3},{7,1},{8,14},{10,12},{12... | collective-permute-start | bytes 903176 | tf_op jit(solution)/shard_map/ppermute | solution.py:33
  18.5 18.3 %collective-permute-start.3 = (bf16[2,98,768]{2,1,0:T(8,128)(2,1)S(1)}, bf16[2,98,768]{2,1,0:T(8,128)(2,1)}, u32[]{:S(2)}, u32[]{:S(2)}) collective-permute-start(bf16[2,98,768]{2,1,0:T(8,128)(2,1)S(1)} %bitcast.95), channel_id=1, source_target_pairs={{0,2},{2,0},{1,3},{3,1},{4,6},{6,4},{5,7},{7,5},{8,10},{10,8},{9,1... | collective-permute-start | bytes 903176 | tf_op jit(solution)/shard_map/ppermute | solution.py:25
  20.0 17.9 %collective-permute-start.4 = (bf16[2,98,768]{2,1,0:T(8,128)(2,1)S(1)}, bf16[2,98,768]{2,1,0:T(8,128)(2,1)}, u32[]{:S(2)}, u32[]{:S(2)}) collective-permute-start(bf16[2,98,768]{2,1,0:T(8,128)(2,1)S(1)} %bitcast.96), channel_id=1, source_target_pairs={{0,4},{4,0},{1,5},{5,1},{2,6},{6,2},{3,7},{7,3},{8,12},{12,8},{9,1... | collective-permute-start | bytes 903176 | tf_op jit(solution)/shard_map/ppermute | solution.py:29
  29.2 28.4 %all-to-all-start.1 = ((bf16[4,1,96,768]{3,2,1,0:T(8,128)(2,1)}), bf16[4,1,96,768]{3,2,1,0:T(8,128)(2,1)}, u32[]{:S(2)}, u32[]{:S(2)}) async-start(bf16[4,1,96,768]{3,2,1,0:T(8,128)(2,1)} %broadcast_in_dim.29), calls=%async_computation.1 | async-start | bytes 1179648 | tf_op jit(solution)/shard_map/all_to_all | solution.py:41
  38.0 14.6 %collective-permute-start.6 = (bf16[4,104,768]{2,1,0:T(8,128)(2,1)S(1)}, bf16[4,104,768]{2,1,0:T(8,128)(2,1)S(1)}, u32[]{:S(2)}, u32[]{:S(2)}) collective-permute-start(bf16[4,104,768]{2,1,0:T(8,128)(2,1)S(1)} %bitcast.81), channel_id=1, source_target_pairs={{0,4},{4,0},{1,5},{5,1},{2,6},{6,2},{3,7},{7,3},{8,12},{12,8},{9,1... | collective-permute-start | bytes 1916936 | tf_op jit(solution)/shard_map/ppermute | solution.py:29
  39.5 14.4 %collective-permute-start.5 = (bf16[4,104,768]{2,1,0:T(8,128)(2,1)S(1)}, bf16[4,104,768]{2,1,0:T(8,128)(2,1)S(1)}, u32[]{:S(2)}, u32[]{:S(2)}) collective-permute-start(bf16[4,104,768]{2,1,0:T(8,128)(2,1)S(1)} %bitcast.82), channel_id=1, source_target_pairs={{0,2},{2,0},{1,3},{3,1},{4,6},{6,4},{5,7},{7,5},{8,10},{10,8},{9,1... | collective-permute-start | bytes 1916936 | tf_op jit(solution)/shard_map/ppermute | solution.py:25
  40.0 24.3 %collective-permute-start.9 = (bf16[4,104,768]{2,1,0:T(8,128)(2,1)S(1)}, bf16[4,104,768]{2,1,0:T(8,128)(2,1)}, u32[]{:S(2)}, u32[]{:S(2)}) collective-permute-start(bf16[4,104,768]{2,1,0:T(8,128)(2,1)S(1)} %bitcast.83), channel_id=1, source_target_pairs={{0,1},{1,0},{2,3},{3,2},{4,5},{5,4},{6,7},{7,6},{8,9},{9,8},{10,11... | collective-permute-start | bytes 1916936 | tf_op jit(solution)/shard_map/ppermute | solution.py:37
  55.0 14.1 %collective-permute-start.10 = (bf16[4,104,768]{2,1,0:T(8,128)(2,1)S(1)}, bf16[4,104,768]{2,1,0:T(8,128)(2,1)}, u32[]{:S(2)}, u32[]{:S(2)}) collective-permute-start(bf16[4,104,768]{2,1,0:T(8,128)(2,1)S(1)} %collective-permute-done.5.refs_2_.refs_7_.refs_6_), channel_id=1, source_target_pairs={{0,1},{1,0},{2,3},{3,2},{4,5},{5,4},{6,7},{7,6},{8,9},{9,8},{10,11... | collective-permute-start | bytes 1916936 | tf_op jit(solution)/shard_map/ppermute | solution.py:37
  55.0 14.3 %collective-permute-start.11 = (bf16[4,104,768]{2,1,0:T(8,128)(2,1)S(1)}, bf16[4,104,768]{2,1,0:T(8,128)(2,1)}, u32[]{:S(2)}, u32[]{:S(2)}) collective-permute-start(bf16[4,104,768]{2,1,0:T(8,128)(2,1)S(1)} %collective-permute-done.6.refs_3_.refs_8_.refs_7_), channel_id=1, source_target_pairs={{0,1},{1,0},{2,3},{3,2},{4,5},{5,4},{6,7},{7,6},{8,9},{9,8},{10,11... | collective-permute-start | bytes 1916936 | tf_op jit(solution)/shard_map/ppermute | solution.py:37
  57.6 34.2 %all-to-all-start.2 = ((bf16[4,2,96,768]{3,2,1,0:T(8,128)(2,1)}), bf16[4,2,96,768]{3,2,1,0:T(8,128)(2,1)}, u32[]{:S(2)}, u32[]{:S(2)}) async-start(bf16[4,2,96,768]{3,2,1,0:T(8,128)(2,1)} %broadcast_in_dim.30), calls=%async_computation.2 | async-start | bytes 2359296 | tf_op jit(solution)/shard_map/all_to_all | solution.py:41
  68.2 19.5 %collective-permute-start.16 = (bf16[4,96,768]{2,1,0:T(8,128)(2,1)}, bf16[4,96,768]{2,1,0:T(8,128)(2,1)}, u32[]{:S(2)}, u32[]{:S(2)}) collective-permute-start(bf16[4,96,768]{2,1,0:T(8,128)(2,1)} %bitcast.18.refs_3_.refs_5_), channel_id=1, source_target_pairs={{0,4},{4,0},{1,5},{5,1},{2,6},{6,2},{3,7},{7,3},{8,12},{12,8},{9,1... | collective-permute-start | bytes 1769480 | tf_op jit(solution)/shard_map/ppermute | solution.py:29
  68.6 19.2 %collective-permute-start.15 = (bf16[4,96,768]{2,1,0:T(8,128)(2,1)}, bf16[4,96,768]{2,1,0:T(8,128)(2,1)}, u32[]{:S(2)}, u32[]{:S(2)}) collective-permute-start(bf16[4,96,768]{2,1,0:T(8,128)(2,1)} %bitcast.18.refs_3_.refs_5_), channel_id=1, source_target_pairs={{0,2},{2,0},{1,3},{3,1},{4,6},{6,4},{5,7},{7,5},{8,10},{10,8},{9,1... | collective-permute-start | bytes 1769480 | tf_op jit(solution)/shard_map/ppermute | solution.py:25
  91.8 13.9 %collective-permute-start.17 = (bf16[12,832,128]{2,1,0:T(8,128)(2,1)}, bf16[12,832,128]{2,1,0:T(8,128)(2,1)}, u32[]{:S(2)}, u32[]{:S(2)}) collective-permute-start(bf16[12,832,128]{2,1,0:T(8,128)(2,1)} %get-tuple-element.157.refs_4_.refs_3_), channel_id=1, source_target_pairs={{0,1},{1,0},{2,3},{3,2},{4,5},{5,4},{6,7},{7,6},{8,9},{9,8},{10,11... | collective-permute-start | bytes 7667720 | tf_op jit(solution)/shard_map/ppermute | solution.py:37
  105.1 19.4 %collective-permute-start.21 = (bf16[4,96,768]{2,1,0:T(8,128)(2,1)}, bf16[4,96,768]{2,1,0:T(8,128)(2,1)}, u32[]{:S(2)}, u32[]{:S(2)}) collective-permute-start(bf16[4,96,768]{2,1,0:T(8,128)(2,1)} %collective-permute-done.15.refs_4_.refs_6_), channel_id=1, source_target_pairs={{0,1},{1,0},{2,3},{3,2},{4,5},{5,4},{6,7},{7,6},{8,9},{9,8},{10,11... | collective-permute-start | bytes 1769480 | tf_op jit(solution)/shard_map/ppermute | solution.py:37
  105.7 18.9 %collective-permute-start.22 = (bf16[4,96,768]{2,1,0:T(8,128)(2,1)}, bf16[4,96,768]{2,1,0:T(8,128)(2,1)}, u32[]{:S(2)}, u32[]{:S(2)}) collective-permute-start(bf16[4,96,768]{2,1,0:T(8,128)(2,1)} %collective-permute-done.16.refs_5_.refs_7_), channel_id=1, source_target_pairs={{0,1},{1,0},{2,3},{3,2},{4,5},{5,4},{6,7},{7,6},{8,9},{9,8},{10,11... | collective-permute-start | bytes 1769480 | tf_op jit(solution)/shard_map/ppermute | solution.py:37
  105.7 18.8 %collective-permute-start.24 = (bf16[2,96,768]{2,1,0:T(8,128)(2,1)}, bf16[2,96,768]{2,1,0:T(8,128)(2,1)}, u32[]{:S(2)}, u32[]{:S(2)}) collective-permute-start(bf16[2,96,768]{2,1,0:T(8,128)(2,1)} %collective-permute-done.19.refs_7_.refs_9_), channel_id=1, source_target_pairs={{0,1},{1,0},{2,3},{3,2},{4,5},{5,4},{6,7},{7,6},{8,9},{9,8},{10,11... | collective-permute-start | bytes 884744 | tf_op jit(solution)/shard_map/ppermute | solution.py:37
  106.2 29.3 %collective-permute-start.26 = (bf16[8,96,768]{2,1,0:T(8,128)(2,1)}, bf16[8,96,768]{2,1,0:T(8,128)(2,1)}, u32[]{:S(2)}, u32[]{:S(2)}) collective-permute-start(bf16[8,96,768]{2,1,0:T(8,128)(2,1)} %bitcast.24.refs_7_), channel_id=1, source_target_pairs={{0,4},{4,0},{1,5},{5,1},{2,6},{6,2},{3,7},{7,3},{8,12},{12,8},{9,1... | collective-permute-start | bytes 3538952 | tf_op jit(solution)/shard_map/ppermute | solution.py:29
  108.5 28.0 %collective-permute-start.25 = (bf16[8,96,768]{2,1,0:T(8,128)(2,1)}, bf16[8,96,768]{2,1,0:T(8,128)(2,1)}, u32[]{:S(2)}, u32[]{:S(2)}) collective-permute-start(bf16[8,96,768]{2,1,0:T(8,128)(2,1)} %bitcast.24.refs_7_), channel_id=1, source_target_pairs={{0,2},{2,0},{1,3},{3,1},{4,6},{6,4},{5,7},{7,5},{8,10},{10,8},{9,1... | collective-permute-start | bytes 3538952 | tf_op jit(solution)/shard_map/ppermute | solution.py:25
  124.5 34.3 %collective-permute-start.29 = (bf16[8,96,768]{2,1,0:T(8,128)(2,1)}, bf16[8,96,768]{2,1,0:T(8,128)(2,1)}, u32[]{:S(2)}, u32[]{:S(2)}) collective-permute-start(bf16[8,96,768]{2,1,0:T(8,128)(2,1)} %bitcast.24.refs_7_), channel_id=1, source_target_pairs={{0,1},{1,0},{2,3},{3,2},{4,5},{5,4},{6,7},{7,6},{8,9},{9,8},{10,11... | collective-permute-start | bytes 3538952 | tf_op jit(solution)/shard_map/ppermute | solution.py:37
  140.3 15.3 %collective-permute-start.28 = (bf16[4,96,768]{2,1,0:T(8,128)(2,1)}, bf16[4,96,768]{2,1,0:T(8,128)(2,1)}, u32[]{:S(2)}, u32[]{:S(2)}) collective-permute-start(bf16[4,96,768]{2,1,0:T(8,128)(2,1)} %slice.230), channel_id=1, source_target_pairs={{0,2},{2,0},{1,3},{3,1},{4,6},{6,4},{5,7},{7,5},{8,10},{10,8},{9,1... | collective-permute-start | bytes 1769480 | tf_op jit(solution)/shard_map/ppermute | solution.py:25
  140.8 15.7 %collective-permute-start.27 = (bf16[4,96,768]{2,1,0:T(8,128)(2,1)}, bf16[4,96,768]{2,1,0:T(8,128)(2,1)}, u32[]{:S(2)}, u32[]{:S(2)}) collective-permute-start(bf16[4,96,768]{2,1,0:T(8,128)(2,1)} %slice.229), channel_id=1, source_target_pairs={{0,4},{4,0},{1,5},{5,1},{2,6},{6,2},{3,7},{7,3},{8,12},{12,8},{9,1... | collective-permute-start | bytes 1769480 | tf_op jit(solution)/shard_map/ppermute | solution.py:29
  142.1 16.7 %collective-permute-start.30 = (bf16[8,96,768]{2,1,0:T(8,128)(2,1)}, bf16[8,96,768]{2,1,0:T(8,128)(2,1)}, u32[]{:S(2)}, u32[]{:S(2)}) collective-permute-start(bf16[8,96,768]{2,1,0:T(8,128)(2,1)} %collective-permute-done.25.refs_8_), channel_id=1, source_target_pairs={{0,1},{1,0},{2,3},{3,2},{4,5},{5,4},{6,7},{7,6},{8,9},{9,8},{10,11... | collective-permute-start | bytes 3538952 | tf_op jit(solution)/shard_map/ppermute | solution.py:37
  142.1 16.7 %collective-permute-start.31 = (bf16[8,96,768]{2,1,0:T(8,128)(2,1)}, bf16[8,96,768]{2,1,0:T(8,128)(2,1)}, u32[]{:S(2)}, u32[]{:S(2)}) collective-permute-start(bf16[8,96,768]{2,1,0:T(8,128)(2,1)} %collective-permute-done.26.refs_9_), channel_id=1, source_target_pairs={{0,1},{1,0},{2,3},{3,2},{4,5},{5,4},{6,7},{7,6},{8,9},{9,8},{10,11... | collective-permute-start | bytes 3538952 | tf_op jit(solution)/shard_map/ppermute | solution.py:37
  197.4 25.4 %collective-permute-start.37 = (bf16[32,96,768]{2,1,0:T(8,128)(2,1)}, bf16[32,96,768]{2,1,0:T(8,128)(2,1)}, u32[]{:S(2)}, u32[]{:S(2)}) collective-permute-start(bf16[32,96,768]{2,1,0:T(8,128)(2,1)} %get-tuple-element.184), channel_id=1, source_target_pairs={{0,1},{1,0},{2,3},{3,2},{4,5},{5,4},{6,7},{7,6},{8,9},{9,8},{10,11... | collective-permute-start | bytes 14155784 | tf_op jit(solution)/shard_map/ppermute | solution.py:37
  197.6 29.6 %collective-permute-start.34 = (bf16[2,98,768]{2,1,0:T(8,128)(2,1)}, bf16[2,98,768]{2,1,0:T(8,128)(2,1)}, u32[]{:S(2)}, u32[]{:S(2)}) collective-permute-start(bf16[2,98,768]{2,1,0:T(8,128)(2,1)} %get-tuple-element.180), channel_id=1, source_target_pairs={{0,2},{2,0},{1,3},{3,1},{4,6},{6,4},{5,7},{7,5},{8,10},{10,8},{9,1... | collective-permute-start | bytes 903176 | tf_op jit(solution)/shard_map/ppermute | solution.py:25
  198.1 29.0 %collective-permute-start.35 = (bf16[2,98,768]{2,1,0:T(8,128)(2,1)}, bf16[2,98,768]{2,1,0:T(8,128)(2,1)}, u32[]{:S(2)}, u32[]{:S(2)}) collective-permute-start(bf16[2,98,768]{2,1,0:T(8,128)(2,1)} %get-tuple-element.181), channel_id=1, source_target_pairs={{0,4},{4,0},{1,5},{5,1},{2,6},{6,2},{3,7},{7,3},{8,12},{12,8},{9,1... | collective-permute-start | bytes 903176 | tf_op jit(solution)/shard_map/ppermute | solution.py:29
  199.2 27.9 %collective-permute-start.36 = (bf16[2,98,768]{2,1,0:T(8,128)(2,1)}, bf16[2,98,768]{2,1,0:T(8,128)(2,1)}, u32[]{:S(2)}, u32[]{:S(2)}) collective-permute-start(bf16[2,98,768]{2,1,0:T(8,128)(2,1)} %get-tuple-element.182), channel_id=1, source_target_pairs={{0,6},{2,4},{4,2},{6,0},{1,7},{3,5},{5,3},{7,1},{8,14},{10,12},{12... | collective-permute-start | bytes 903176 | tf_op jit(solution)/shard_map/ppermute | solution.py:33
  225.5 15.1 %collective-permute-start.38 = (bf16[4,96,768]{2,1,0:T(8,128)(2,1)}, bf16[4,96,768]{2,1,0:T(8,128)(2,1)}, u32[]{:S(2)}, u32[]{:S(2)}) collective-permute-start(bf16[4,96,768]{2,1,0:T(8,128)(2,1)} %get-tuple-element.186), channel_id=1, source_target_pairs={{0,4},{4,0},{1,5},{5,1},{2,6},{6,2},{3,7},{7,3},{8,12},{12,8},{9,1... | collective-permute-start | bytes 1769480 | tf_op jit(solution)/shard_map/ppermute | solution.py:29
  226.5 14.8 %collective-permute-start.39 = (bf16[4,96,768]{2,1,0:T(8,128)(2,1)}, bf16[4,96,768]{2,1,0:T(8,128)(2,1)}, u32[]{:S(2)}, u32[]{:S(2)}) collective-permute-start(bf16[4,96,768]{2,1,0:T(8,128)(2,1)} %get-tuple-element.187), channel_id=1, source_target_pairs={{0,2},{2,0},{1,3},{3,1},{4,6},{6,4},{5,7},{7,5},{8,10},{10,8},{9,1... | collective-permute-start | bytes 1769480 | tf_op jit(solution)/shard_map/ppermute | solution.py:25
  241.3 18.3 %collective-permute-start.40 = (bf16[16,96,768]{2,1,0:T(8,128)(2,1)}, bf16[16,96,768]{2,1,0:T(8,128)(2,1)}, u32[]{:S(2)}, u32[]{:S(2)}) collective-permute-start(bf16[16,96,768]{2,1,0:T(8,128)(2,1)} %get-tuple-element.197), channel_id=1, source_target_pairs={{0,1},{1,0},{2,3},{3,2},{4,5},{5,4},{6,7},{7,6},{8,9},{9,8},{10,11... | collective-permute-start | bytes 7077896 | tf_op jit(solution)/shard_map/ppermute | solution.py:37
  245.7 39.7 %collective-permute-start.41 = (bf16[8,96,768]{2,1,0:T(8,128)(2,1)}, bf16[8,96,768]{2,1,0:T(8,128)(2,1)}, u32[]{:S(2)}, u32[]{:S(2)}) collective-permute-start(bf16[8,96,768]{2,1,0:T(8,128)(2,1)} %get-tuple-element.193), channel_id=1, source_target_pairs={{0,2},{2,0},{1,3},{3,1},{4,6},{6,4},{5,7},{7,5},{8,10},{10,8},{9,1... | collective-permute-start | bytes 3538952 | tf_op jit(solution)/shard_map/ppermute | solution.py:25
  246.3 39.0 %collective-permute-start.42 = (bf16[8,96,768]{2,1,0:T(8,128)(2,1)}, bf16[8,96,768]{2,1,0:T(8,128)(2,1)}, u32[]{:S(2)}, u32[]{:S(2)}) collective-permute-start(bf16[8,96,768]{2,1,0:T(8,128)(2,1)} %get-tuple-element.194), channel_id=1, source_target_pairs={{0,4},{4,0},{1,5},{5,1},{2,6},{6,2},{3,7},{7,3},{8,12},{12,8},{9,1... | collective-permute-start | bytes 3538952 | tf_op jit(solution)/shard_map/ppermute | solution.py:29
  261.7 23.6 %collective-permute-start.43 = (bf16[2,96,768]{2,1,0:T(8,128)(2,1)}, bf16[2,96,768]{2,1,0:T(8,128)(2,1)}, u32[]{:S(2)}, u32[]{:S(2)}) collective-permute-start(bf16[2,96,768]{2,1,0:T(8,128)(2,1)} %get-tuple-element.199), channel_id=1, source_target_pairs={{0,4},{4,0},{1,5},{5,1},{2,6},{6,2},{3,7},{7,3},{8,12},{12,8},{9,1... | collective-permute-start | bytes 884744 | tf_op jit(solution)/shard_map/ppermute | solution.py:29
  262.8 22.6 %collective-permute-start.44 = (bf16[2,96,768]{2,1,0:T(8,128)(2,1)}, bf16[2,96,768]{2,1,0:T(8,128)(2,1)}, u32[]{:S(2)}, u32[]{:S(2)}) collective-permute-start(bf16[2,96,768]{2,1,0:T(8,128)(2,1)} %get-tuple-element.200), channel_id=1, source_target_pairs={{0,2},{2,0},{1,3},{3,1},{4,6},{6,4},{5,7},{7,5},{8,10},{10,8},{9,1... | collective-permute-start | bytes 884744 | tf_op jit(solution)/shard_map/ppermute | solution.py:25
  288.2 23.6 %all-to-all-start.3 = ((bf16[4,1,96,768]{3,2,1,0:T(8,128)(2,1)}), bf16[4,1,96,768]{3,2,1,0:T(8,128)(2,1)}, u32[]{:S(2)}, u32[]{:S(2)}) async-start(bf16[4,1,96,768]{3,2,1,0:T(8,128)(2,1)} %bitcast.80), calls=%async_computation.3 | async-start | bytes 1179648 | tf_op jit(solution)/shard_map/all_to_all | solution.py:41
  295.4 16.5 %collective-permute-start.46 = (bf16[4,96,768]{2,1,0:T(8,128)(2,1)}, bf16[4,96,768]{2,1,0:T(8,128)(2,1)}, u32[]{:S(2)}, u32[]{:S(2)}) collective-permute-start(bf16[4,96,768]{2,1,0:T(8,128)(2,1)} %get-tuple-element.212), channel_id=1, source_target_pairs={{0,2},{2,0},{1,3},{3,1},{4,6},{6,4},{5,7},{7,5},{8,10},{10,8},{9,1... | collective-permute-start | bytes 1769480 | tf_op jit(solution)/shard_map/ppermute | solution.py:25
  296.1 15.8 %collective-permute-start.47 = (bf16[4,96,768]{2,1,0:T(8,128)(2,1)}, bf16[4,96,768]{2,1,0:T(8,128)(2,1)}, u32[]{:S(2)}, u32[]{:S(2)}) collective-permute-start(bf16[4,96,768]{2,1,0:T(8,128)(2,1)} %get-tuple-element.213), channel_id=1, source_target_pairs={{0,4},{4,0},{1,5},{5,1},{2,6},{6,2},{3,7},{7,3},{8,12},{12,8},{9,1... | collective-permute-start | bytes 1769480 | tf_op jit(solution)/shard_map/ppermute | solution.py:29
  323.0 46.2 %all-to-all-start.4 = ((bf16[4,2,96,768]{3,2,1,0:T(8,128)(2,1)}), bf16[4,2,96,768]{3,2,1,0:T(8,128)(2,1)}, u32[]{:S(2)}, u32[]{:S(2)}) async-start(bf16[4,2,96,768]{3,2,1,0:T(8,128)(2,1)} %bitcast.79), calls=%async_computation.4 | async-start | bytes 2359296 | tf_op jit(solution)/shard_map/all_to_all | solution.py:41
  340.8 14.3 %collective-permute-start.51 = (bf16[4,96,768]{2,1,0:T(8,128)(2,1)}, bf16[4,96,768]{2,1,0:T(8,128)(2,1)}, u32[]{:S(2)}, u32[]{:S(2)}) collective-permute-start(bf16[4,96,768]{2,1,0:T(8,128)(2,1)} %get-tuple-element.226), channel_id=1, source_target_pairs={{0,2},{2,0},{1,3},{3,1},{4,6},{6,4},{5,7},{7,5},{8,10},{10,8},{9,1... | collective-permute-start | bytes 1769480 | tf_op jit(solution)/shard_map/ppermute | solution.py:25
  342.1 13.9 %collective-permute-start.52 = (bf16[4,96,768]{2,1,0:T(8,128)(2,1)}, bf16[4,96,768]{2,1,0:T(8,128)(2,1)}, u32[]{:S(2)}, u32[]{:S(2)}) collective-permute-start(bf16[4,96,768]{2,1,0:T(8,128)(2,1)} %get-tuple-element.227), channel_id=1, source_target_pairs={{0,4},{4,0},{1,5},{5,1},{2,6},{6,2},{3,7},{7,3},{8,12},{12,8},{9,1... | collective-permute-start | bytes 1769480 | tf_op jit(solution)/shard_map/ppermute | solution.py:29
  363.3 20.8 %collective-permute-start.57 = (bf16[1,96,768]{2,1,0:T(8,128)(2,1)}, bf16[1,96,768]{2,1,0:T(8,128)(2,1)}, u32[]{:S(2)}, u32[]{:S(2)}) collective-permute-start(bf16[1,96,768]{2,1,0:T(8,128)(2,1)} %get-tuple-element.238), channel_id=1, source_target_pairs={{0,16},{8,24},{16,0},{24,8},{1,17},{9,25},{17,1},{25,9},{2,18},{10... | collective-permute-start | bytes 442376 | tf_op jit(solution)/shard_map/ppermute | solution.py:165
  365.7 18.4 %collective-permute-start.53 = (bf16[2,98,768]{2,1,0:T(8,128)(2,1)}, bf16[2,98,768]{2,1,0:T(8,128)(2,1)}, u32[]{:S(2)}, u32[]{:S(2)}) collective-permute-start(bf16[2,98,768]{2,1,0:T(8,128)(2,1)} %get-tuple-element.249), channel_id=1, source_target_pairs={{0,2},{2,0},{1,3},{3,1},{4,6},{6,4},{5,7},{7,5},{8,10},{10,8},{9,1... | collective-permute-start | bytes 903176 | tf_op jit(solution)/shard_map/ppermute | solution.py:25
  366.3 17.7 %collective-permute-start.54 = (bf16[2,98,768]{2,1,0:T(8,128)(2,1)}, bf16[2,98,768]{2,1,0:T(8,128)(2,1)}, u32[]{:S(2)}, u32[]{:S(2)}) collective-permute-start(bf16[2,98,768]{2,1,0:T(8,128)(2,1)} %get-tuple-element.250), channel_id=1, source_target_pairs={{0,4},{4,0},{1,5},{5,1},{2,6},{6,2},{3,7},{7,3},{8,12},{12,8},{9,1... | collective-permute-start | bytes 903176 | tf_op jit(solution)/shard_map/ppermute | solution.py:29
  367.3 16.8 %collective-permute-start.55 = (bf16[2,98,768]{2,1,0:T(8,128)(2,1)}, bf16[2,98,768]{2,1,0:T(8,128)(2,1)}, u32[]{:S(2)}, u32[]{:S(2)}) collective-permute-start(bf16[2,98,768]{2,1,0:T(8,128)(2,1)} %get-tuple-element.251), channel_id=1, source_target_pairs={{0,6},{2,4},{4,2},{6,0},{1,7},{3,5},{5,3},{7,1},{8,14},{10,12},{12... | collective-permute-start | bytes 903176 | tf_op jit(solution)/shard_map/ppermute | solution.py:33
  370.2 13.8 %collective-permute-start.58 = (bf16[1,96,768]{2,1,0:T(8,128)(2,1)}, bf16[1,96,768]{2,1,0:T(8,128)(2,1)}, u32[]{:S(2)}, u32[]{:S(2)}) collective-permute-start(bf16[1,96,768]{2,1,0:T(8,128)(2,1)} %get-tuple-element.239), channel_id=1, source_target_pairs={{0,24},{8,0},{16,8},{24,16},{1,25},{9,1},{17,9},{25,17},{2,26},{10... | collective-permute-start | bytes 442376 | tf_op jit(solution)/shard_map/ppermute | solution.py:165
  (47 other events, 307.0 us)
